TPU v7x, 32 devices: a whole 2x2x4 slice. The times are simulated.
32 devices in a mesh: dp: 16 (over z, x, core), tensor: 2 (over y).
Axes of the slice: x: 2, y: 2, z: 4, core: 2. Of those that a mesh axis runs over, the one named last changes fastest.
Arguments:
- block_input: bfloat16 [32, 1024, 768], P('dp', 'tensor'), may hold values from -6 to 6
- skip_values: bfloat16 [32, 1024, 384], P('dp', None, 'tensor'), may hold values from -6 to 6
- segment_ids: int32 [32, 1024], P('dp'), may hold values from 0 to 7, never falling along the last dimension, each value on 1 to 256 neighbouring positions
- row_fill: int32 [32], P('dp'), may hold values from 512 to 1024, as said below
- query_weight: bfloat16 [768, 768], P(None, 'tensor'), may hold values from -0.21875 to 0.21875
- query_bias: float32 [768], P('tensor'), may hold values from -3 to 3
- key_weight: bfloat16 [768, 768], P(None, 'tensor'), may hold values from -0.21875 to 0.21875
- value_weight: bfloat16 [768, 384], P(None, 'tensor'), may hold values from -0.21875 to 0.21875
- value_bias: float32 [384], P('tensor'), may hold values from -3 to 3
- out_weight: bfloat16 [768, 768], P('tensor'), may hold values from -0.625 to 0.625
- out_bias: float32 [768], replicated, may hold values from -2 to 2
- up_weight: bfloat16 [768, 3072], P(None, 'tensor'), may hold values from -0.21875 to 0.21875
- up_bias: float32 [3072], P('tensor'), may hold values from -3 to 3
- down_weight: bfloat16 [3072, 768], P('tensor'), may hold values from -0.109375 to 0.109375
- down_bias: float32 [768], replicated, may hold values from -2 to 2
- first_gain: float32 [768], replicated, may hold values from 0.1 to 1.9
- first_shift: float32 [768], replicated, may hold values from -2 to 2
- second_gain: float32 [768], replicated, may hold values from 0.1 to 1.9
- second_shift: float32 [768], replicated, may hold values from -2 to 2
- cotangent: bfloat16 [32, 1024, 768], P('dp', 'tensor'), may hold values from -6 to 6
Outputs:
- block_output: float32 [32, 1024, 768], P('dp', 'tensor')
- input_grad: float32 [32, 1024, 768], P('dp', 'tensor')
- skip_grad: float32 [32, 1024, 384], P('dp', None, 'tensor')
- query_weight_grad: float32 [768, 768], P(None, 'tensor')
- query_bias_grad: float32 [768], P('tensor')
- key_weight_grad: float32 [768, 768], P(None, 'tensor')
- value_weight_grad: float32 [768, 384], P(None, 'tensor')
- value_bias_grad: float32 [384], P('tensor')
- out_weight_grad: float32 [768, 768], P('tensor')
- out_bias_grad: float32 [768], replicated
- up_weight_grad: float32 [768, 3072], P(None, 'tensor')
- up_bias_grad: float32 [3072], P('tensor')
- down_weight_grad: float32 [3072, 768], P('tensor')
- down_bias_grad: float32 [768], replicated
- first_gain_grad: float32 [768], replicated
- first_shift_grad: float32 [768], replicated
- second_gain_grad: float32 [768], replicated
- second_shift_grad: float32 [768], replicated
Inputs may be any that keep to these rules, and one draw needn't show every extreme that they name: `row_fill`: row 0 is filled to 1024 in every draw; positions at or after a row's fill are padding that no other position sees.
All inputs are finite; a program needn't handle non-finite values.
Results may differ from a plain program's by a relative error of at most 0.012.
The roundings to bfloat16 on the way count: a program that leaves them out, or rounds other values in their place, can miss the bound.
Values may be sent and summed in bfloat16 or wider, within the bound.
No kernel may reach another device: no remote copies, remote signals or barrier semaphores. Data moves between devices by JAX's collectives and lax.ppermute only.
A program may use at most 256 MiB of HBM per device.

v0:
```python
import jax
import jax.numpy as jnp
from jax import lax
from jax.sharding import PartitionSpec as P

DH = 64


def layer_norm(values, gain_row, shift_row):
    center = values - jnp.mean(values, axis=-1, keepdims=True)
    variance = jnp.mean(center * center, axis=-1, keepdims=True)
    return center * lax.rsqrt(variance + 1e-05) * gain_row + shift_row


def gelu_tanh(values):
    return jax.nn.gelu(values, approximate=True)


def row_mask(segment_row, fill_value, position, start, block_rows):
    query_pos = position[start : start + block_rows]
    same_doc = segment_row[start : start + block_rows][:, None] == segment_row[None, :]
    causal = position[None, :] <= query_pos[:, None]
    usable = (position[None, :] < fill_value) | (position[None, :] == query_pos[:, None])
    return same_doc & causal & usable


def attend_row(queries, keys_all, values_all, segment_row, fill_value, block_rows, scale):
    length = queries.shape[0]
    position = jnp.arange(length, dtype=jnp.int32)
    outputs = []
    totals = []
    for start in range(0, length, block_rows):
        query_block = queries[start : start + block_rows]
        allowed = row_mask(segment_row, fill_value, position, start, block_rows)
        scores = (
            jnp.einsum("ihd,jhd->hij", query_block, keys_all, preferred_element_type=jnp.float32)
            * scale
        )
        scores = jnp.where(allowed[None], scores, -1000000000.0)
        largest = jnp.max(scores, axis=-1, keepdims=True)
        expon = jnp.exp(scores - largest)
        total_sum = jnp.sum(expon, axis=-1, keepdims=True)
        probability = expon / total_sum
        block_out = jnp.einsum(
            "hij,jhd->ihd",
            probability.astype(jnp.bfloat16),
            values_all,
            preferred_element_type=jnp.float32,
        )
        outputs.append(block_out.astype(jnp.bfloat16))
        totals.append((largest + jnp.log(total_sum))[..., 0])
    return (jnp.concatenate(outputs, axis=0), jnp.concatenate(totals, axis=1))


def attend_back(
    queries, keys_all, values_all, out_grad, totals, segment_row, fill_value, block_rows, scale
):
    length = queries.shape[0]
    position = jnp.arange(length, dtype=jnp.int32)
    key_sum = jnp.zeros(keys_all.shape, jnp.float32)
    value_sum = jnp.zeros(values_all.shape, jnp.float32)
    query_parts = []
    for start in range(0, length, block_rows):
        query_block = queries[start : start + block_rows]
        grad_block = out_grad[start : start + block_rows]
        allowed = row_mask(segment_row, fill_value, position, start, block_rows)
        scores = (
            jnp.einsum("ihd,jhd->hij", query_block, keys_all, preferred_element_type=jnp.float32)
            * scale
        )
        scores = jnp.where(allowed[None], scores, -1000000000.0)
        probability = jnp.exp(scores - totals[:, start : start + block_rows, None])
        prob_low = probability.astype(jnp.bfloat16)
        prob_grad = jnp.einsum(
            "ihd,jhd->hij", grad_block, values_all, preferred_element_type=jnp.float32
        )
        row_total = jnp.sum(prob_grad * probability, axis=-1, keepdims=True)
        score_grad = (probability * (prob_grad - row_total)).astype(jnp.bfloat16)
        query_part = (
            jnp.einsum("hij,jhd->ihd", score_grad, keys_all, preferred_element_type=jnp.float32)
            * scale
        )
        query_parts.append(query_part.astype(jnp.bfloat16))
        key_sum = key_sum + jnp.einsum(
            "hij,ihd->jhd", score_grad, query_block, preferred_element_type=jnp.float32
        )
        value_sum = value_sum + jnp.einsum(
            "hij,ihd->jhd", prob_low, grad_block, preferred_element_type=jnp.float32
        )
    return (jnp.concatenate(query_parts, axis=0), (key_sum * scale).astype(jnp.bfloat16), value_sum)


def on_device(
    block_input,
    skip_values,
    segment_ids,
    row_fill,
    query_weight,
    query_bias,
    key_weight,
    value_weight,
    value_bias,
    out_weight,
    out_bias,
    up_weight,
    up_bias,
    down_weight,
    down_bias,
    first_gain,
    first_shift,
    second_gain,
    second_shift,
    cotangent,
):
    rows_here = block_input.shape[0]
    width = block_input.shape[2]
    length = segment_ids.shape[1]
    local_heads = query_weight.shape[1] // DH
    half_heads = local_heads // 2
    tokens = rows_here * length
    block_rows = min(512, length)
    scale = DH ** (-0.5)
    share_input = block_input.astype(jnp.float32)
    normed_share = layer_norm(share_input, first_gain, first_shift).astype(jnp.bfloat16)
    normed, out_gathered = (
        lax.all_gather(normed_share, "tensor", axis=1, tiled=True),
        lax.all_gather(cotangent, "tensor", axis=1, tiled=True),
    )
    normed_flat = normed.reshape(tokens, width)
    queries = (
        (jnp.dot(normed_flat, query_weight, preferred_element_type=jnp.float32) + query_bias)
        .astype(jnp.bfloat16)
        .reshape(rows_here, length, local_heads, DH)
    )
    keys_all = (
        jnp.dot(normed_flat, key_weight, preferred_element_type=jnp.float32)
        .astype(jnp.bfloat16)
        .reshape(rows_here, length, local_heads, DH)
    )
    fresh_values = (
        (jnp.dot(normed_flat, value_weight, preferred_element_type=jnp.float32) + value_bias)
        .astype(jnp.bfloat16)
        .reshape(rows_here, length, half_heads, DH)
    )
    values_all = jnp.stack(
        [fresh_values, skip_values.reshape(rows_here, length, half_heads, DH)], axis=3
    ).reshape(rows_here, length, local_heads, DH)

    def forward_row(element):
        return attend_row(
            element[0], element[1], element[2], element[3], element[4], block_rows, scale
        )

    head_mixed, totals = lax.map(
        forward_row, (queries, keys_all, values_all, segment_ids, row_fill)
    )
    mixed_flat = head_mixed.reshape(tokens, local_heads * DH)
    attn_part = jnp.dot(mixed_flat, out_weight, preferred_element_type=jnp.float32).reshape(
        rows_here, length, width
    )
    attn_total = lax.psum_scatter(attn_part, "tensor", scatter_dimension=1, tiled=True)
    hidden_share = share_input + (attn_total + out_bias)
    second_share = layer_norm(hidden_share, second_gain, second_shift).astype(jnp.bfloat16)
    second_all = lax.all_gather(second_share, "tensor", axis=1, tiled=True).reshape(tokens, width)
    upward = jnp.dot(second_all, up_weight, preferred_element_type=jnp.float32) + up_bias
    activated = gelu_tanh(upward).astype(jnp.bfloat16)
    down_part = jnp.dot(activated, down_weight, preferred_element_type=jnp.float32).reshape(
        rows_here, length, width
    )
    down_total = lax.psum_scatter(
        down_part.astype(jnp.bfloat16), "tensor", scatter_dimension=1, tiled=True
    ).astype(jnp.float32)
    block_output = hidden_share + (down_total + down_bias)
    out_share = cotangent.astype(jnp.float32)
    out_all = out_gathered.reshape(tokens, width)
    down_weight_grad = jnp.einsum(
        "nf,nd->fd", activated, out_all, preferred_element_type=jnp.float32
    )
    down_bias_grad = jnp.sum(out_share, axis=(0, 1))
    act_grad = jnp.einsum("nd,fd->nf", out_all, down_weight, preferred_element_type=jnp.float32)
    gelu_out, gelu_pull = jax.vjp(gelu_tanh, upward)
    up_grad = gelu_pull(act_grad)[0].astype(jnp.bfloat16)
    up_weight_grad = jnp.einsum(
        "nd,nf->df", second_all, up_grad, preferred_element_type=jnp.float32
    )
    up_bias_grad = jnp.sum(up_grad.astype(jnp.float32), axis=0)
    second_part = jnp.einsum(
        "nf,df->nd", up_grad, up_weight, preferred_element_type=jnp.float32
    ).reshape(rows_here, length, width)
    second_grad = lax.psum_scatter(second_part, "tensor", scatter_dimension=1, tiled=True)
    second_out, second_pull = jax.vjp(layer_norm, hidden_share, second_gain, second_shift)
    hidden_part, second_gain_grad, second_shift_grad = second_pull(second_grad)
    hidden_grad = out_share + hidden_part
    hidden_low = hidden_grad.astype(jnp.bfloat16)
    hidden_all = lax.all_gather(hidden_low, "tensor", axis=1, tiled=True).reshape(tokens, width)
    out_weight_grad = jnp.einsum(
        "nk,nd->kd", mixed_flat, hidden_all, preferred_element_type=jnp.float32
    )
    out_bias_grad = jnp.sum(hidden_low.astype(jnp.float32), axis=(0, 1))
    mixed_grad = (
        jnp.einsum("nd,kd->nk", hidden_all, out_weight, preferred_element_type=jnp.float32)
        .astype(jnp.bfloat16)
        .reshape(rows_here, length, local_heads, DH)
    )

    def backward_row(element):
        return attend_back(
            element[0],
            element[1],
            element[2],
            element[3],
            element[4],
            element[5],
            element[6],
            block_rows,
            scale,
        )

    query_grad, key_grad, value_grad = lax.map(
        backward_row, (queries, keys_all, values_all, mixed_grad, totals, segment_ids, row_fill)
    )
    value_split = value_grad.reshape(rows_here, length, half_heads, 2, DH)
    fresh_grad = value_split[:, :, :, 0].astype(jnp.bfloat16).reshape(tokens, half_heads * DH)
    skip_grad = value_split[:, :, :, 1].reshape(rows_here, length, half_heads * DH)
    query_flat = query_grad.reshape(tokens, local_heads * DH)
    key_flat = key_grad.reshape(tokens, local_heads * DH)
    query_weight_grad = jnp.einsum(
        "nd,nk->dk", normed_flat, query_flat, preferred_element_type=jnp.float32
    )
    query_bias_grad = jnp.sum(query_flat.astype(jnp.float32), axis=0)
    key_weight_grad = jnp.einsum(
        "nd,nk->dk", normed_flat, key_flat, preferred_element_type=jnp.float32
    )
    value_weight_grad = jnp.einsum(
        "nd,nk->dk", normed_flat, fresh_grad, preferred_element_type=jnp.float32
    )
    value_bias_grad = jnp.sum(fresh_grad.astype(jnp.float32), axis=0)
    first_part = jnp.einsum(
        "nk,dk->nd", query_flat, query_weight, preferred_element_type=jnp.float32
    )
    first_part = first_part + jnp.einsum(
        "nk,dk->nd", key_flat, key_weight, preferred_element_type=jnp.float32
    )
    first_part = first_part + jnp.einsum(
        "nk,dk->nd", fresh_grad, value_weight, preferred_element_type=jnp.float32
    )
    first_part = first_part.reshape(rows_here, length, width)
    first_grad = lax.psum_scatter(
        first_part.astype(jnp.bfloat16), "tensor", scatter_dimension=1, tiled=True
    ).astype(jnp.float32)
    first_out, first_pull = jax.vjp(layer_norm, share_input, first_gain, first_shift)
    input_part, first_gain_grad, first_shift_grad = first_pull(first_grad)
    input_grad = hidden_grad + input_part
    (
        out_bias_grad,
        down_bias_grad,
        first_gain_grad,
        first_shift_grad,
        second_gain_grad,
        second_shift_grad,
    ) = lax.psum(
        (
            out_bias_grad,
            down_bias_grad,
            first_gain_grad,
            first_shift_grad,
            second_gain_grad,
            second_shift_grad,
        ),
        ("dp", "tensor"),
    )
    (
        query_weight_grad,
        query_bias_grad,
        key_weight_grad,
        value_weight_grad,
        value_bias_grad,
        out_weight_grad,
        up_weight_grad,
        up_bias_grad,
        down_weight_grad,
    ) = lax.psum(
        (
            query_weight_grad,
            query_bias_grad,
            key_weight_grad,
            value_weight_grad,
            value_bias_grad,
            out_weight_grad,
            up_weight_grad,
            up_bias_grad,
            down_weight_grad,
        ),
        "dp",
    )
    return (
        block_output,
        input_grad,
        skip_grad,
        query_weight_grad,
        query_bias_grad,
        key_weight_grad,
        value_weight_grad,
        value_bias_grad,
        out_weight_grad,
        out_bias_grad,
        up_weight_grad,
        up_bias_grad,
        down_weight_grad,
        down_bias_grad,
        first_gain_grad,
        first_shift_grad,
        second_gain_grad,
        second_shift_grad,
    )


def solution(mesh):
    in_specs = (
        P("dp", "tensor", None),
        P("dp", None, "tensor"),
        P("dp", None),
        P("dp"),
        P(None, "tensor"),
        P("tensor"),
        P(None, "tensor"),
        P(None, "tensor"),
        P("tensor"),
        P("tensor", None),
        P(),
        P(None, "tensor"),
        P("tensor"),
        P("tensor", None),
        P(),
        P(),
        P(),
        P(),
        P(),
        P("dp", "tensor", None),
    )
    out_specs = (
        P("dp", "tensor", None),
        P("dp", "tensor", None),
        P("dp", None, "tensor"),
        P(None, "tensor"),
        P("tensor"),
        P(None, "tensor"),
        P(None, "tensor"),
        P("tensor"),
        P("tensor", None),
        P(),
        P(None, "tensor"),
        P("tensor"),
        P("tensor", None),
        P(),
        P(),
        P(),
        P(),
        P(),
    )
    return jax.shard_map(
        on_device, mesh=mesh, in_specs=in_specs, out_specs=out_specs, check_vma=False
    )
```

profile of v0, /device:TPU:0, one launch (start us, length us, event | category | flops | bytes accessed | tf_op | source)
XLA Modules:
  0.0 1030.4 jit_solution(6304505587329444324)
XLA Ops:
  16.2 45.8 %all-gather.5.cloned.1.call-done = bf16[2,1024,768]{2,1,0:T(8,128)(2,1)} async-done(((bf16[2,512,768]{2,1,0:T(8,128)(2,1)}), bf16[2,1024,768]{2,1,0:T(8,128)(2,1)}) %all-gather.5.cloned.1.call-update) | async-done | bytes 3145744 | tf_op jit(solution)/shard_map/all_gather | solution.py:126
  100.8 52.4 %while.26 = (s32[]{:T(128)}, bf16[2,1024,6,64]{1,3,2,0:T(8,128)(2,1)}, f32[2,6,1024]{2,1,0:T(8,128)S(1)}, bf16[2,1024,6,64]{1,3,2,0:T(8,128)(2,1)}, s32[2,1024]{...) while((s32[]{:T(128)}, ...), condition=%wide.region_7.8_spmd, body=%wide.region_2.7_spmd.sunk | while | flops 1694368768 | bytes 111477520 | solution.py:154
  111.3 6.6 fusion.202
  137.4 6.6 fusion.202
  153.3 5.9 fusion.111
  159.3 77.2 %reduce-scatter.5.cloned.1.call-done = f32[2,512,768]{2,1,0:T(8,128)} async-done(((f32[2,1024,768]{2,1,0:T(8,128)}), f32[2,512,768]{2,1,0:T(8,128)}) %reduce-scatter.5.cloned.1.call-update) | async-done | bytes 3145744 | tf_op jit(solution)/shard_map/reduce_scatter | solution.py:161
  243.3 44.5 %all-gather.7.cloned.1.call-done = bf16[2,1024,768]{2,1,0:T(8,128)(2,1)} async-done(((bf16[2,512,768]{2,1,0:T(8,128)(2,1)}), bf16[2,1024,768]{2,1,0:T(8,128)(2,1)}) %all-gather.7.cloned.1.call-update) | async-done | bytes 3145744 | tf_op jit(solution)/shard_map/all_gather | solution.py:164
  287.8 13.3 %multiply_convert_fusion.3 = (bf16[2048,1536]{1,0:T(8,128)(2,1)}, f32[2048,1536]{1,0:T(8,128)}) fusion(f32[1536]{0:T(1024)S(1)} %copy-done.67, bf16[2048,768]{1,0:T(8,128)(2,1)} %bitcast.304, bf16[768,1536]{1,0:T(8,128)(2,1)S(1)} %copy-done), kind=kOutput, calls=%fused_computation.138 | convolution fusion | flops 4863295488 | bytes 24385536 | tf_op jit(solution)/shard_map/dot_general | solution.py:165
  301.1 33.1 %all-gather.9.cloned.1.call-done = bf16[2,1024,768]{2,1,0:T(8,128)(2,1)} async-done(((bf16[2,512,768]{2,1,0:T(8,128)(2,1)}), bf16[2,1024,768]{2,1,0:T(8,128)(2,1)}) %all-gather.9.cloned.1.call-update) | async-done | bytes 3145744 | tf_op jit(solution)/shard_map/all_gather | solution.py:127
  334.2 17.3 %convert_reduce_fusion = (f32[1536]{0:T(1024)}, bf16[2048,1536]{1,0:T(8,128)(2,1)S(1)}) fusion(f32[2048,1536]{1,0:T(8,128)} %get-tuple-element.257, f32[1536]{0:T(1024)S(1)} %copy-done.67, bf16[2048,768]{1,0:T(8,128)(2,1)} %bitcast.306, bf16[1536,768]{1,0:T(8,128)(2,1)} %param.37), kind=kOutput, calls=%fused_computation.137 | convolution fusion | flops 4904188416 | bytes 24391680 | tf_op jit(solution)/shard_map/nd,fd->nf/dot_general | solution.py:180
  351.4 6.9 fusion.119
  360.1 9.6 convolution_convert_fusion
  369.8 65.8 %reduce-scatter.9.cloned.1.call-done = f32[2,512,768]{2,1,0:T(8,128)} async-done(((f32[2,1024,768]{2,1,0:T(8,128)}), f32[2,512,768]{2,1,0:T(8,128)}) %reduce-scatter.9.cloned.1.call-update) | async-done | bytes 3145744 | tf_op jit(solution)/shard_map/reduce_scatter | solution.py:190
  439.7 42.0 %reduce-scatter.7.cloned.1.call-done = bf16[2,512,768]{2,1,0:T(8,128)(2,1)} async-done(((bf16[2,1024,768]{2,1,0:T(8,128)(2,1)}), bf16[2,512,768]{2,1,0:T(8,128)(2,1)}) %reduce-scatter.7.cloned.1.call-update) | async-done | bytes 1572880 | tf_op jit(solution)/shard_map/reduce_scatter | solution.py:170
  481.7 5.1 fusion.116
  489.6 45.0 %all-gather.11.cloned.1.call-done = bf16[2,1024,768]{2,1,0:T(8,128)(2,1)} async-done(((bf16[2,512,768]{2,1,0:T(8,128)(2,1)}), bf16[2,1024,768]{2,1,0:T(8,128)(2,1)}) %all-gather.11.cloned.1.call-update) | async-done | bytes 3145744 | tf_op jit(solution)/shard_map/all_gather | solution.py:195
  549.5 144.7 %while.27 = (s32[]{:T(128)}, bf16[2,1024,6,64]{1,3,2,0:T(8,128)(2,1)}, bf16[2,1024,6,64]{1,3,2,0:T(8,128)(2,1)}, f32[2,1024,6,64]{1,3,2,0:T(8,128)}, bf16[2,1024...) while((s32[]{:T(128)}, ...), condition=%wide.region_18.19_spmd, body=%wide.region_15.18_spmd.sunk | while | flops 4131122176 | bytes 300185536 | solution.py:219
  555.9 6.4 fusion.217
  562.3 6.4 fusion.226
  573.4 10.0 multiply_reduce_fusion.7
  583.3 7.5 multiply_reduce_fusion.8
  590.8 17.6 %multiply_convert_fusion.5 = (bf16[6,512,1024]{2,1,0:T(8,128)(2,1)}, bf16[6,512,1024]{2,1,0:T(8,128)(2,1)}) fusion(f32[6,512,1024]{2,1,0:T(8,128)} %get-tuple-element.412, f32[6,512,1024]{2,1,0:T(8,128)} %fusion.217, f32[6,512]{1,0:T(8,128)S(1)} %get-tuple-element.413, f32[6,512]{1,0:T(8,128)S(1)} %get-tuple-element.408, ...), kind=kLoop, calls=%fused_computation.55.clone.1 | loop fusion | flops 37748736 | bytes 64012288 | tf_op jit(solution)/shard_map/while/body/eval_jaxpr/convert_element_type | solution.py:78
  628.0 6.4 fusion.217
  634.4 6.4 fusion.226
  645.5 10.0 multiply_reduce_fusion.7
  655.4 7.5 multiply_reduce_fusion.8
  662.9 17.6 %multiply_convert_fusion.5 = (bf16[6,512,1024]{2,1,0:T(8,128)(2,1)}, bf16[6,512,1024]{2,1,0:T(8,128)(2,1)}) fusion(f32[6,512,1024]{2,1,0:T(8,128)} %get-tuple-element.412, f32[6,512,1024]{2,1,0:T(8,128)} %fusion.217, f32[6,512]{1,0:T(8,128)S(1)} %get-tuple-element.413, f32[6,512]{1,0:T(8,128)S(1)} %get-tuple-element.408, ...), kind=kLoop, calls=%fused_computation.55.clone.1 | loop fusion | flops 37748736 | bytes 64012288 | tf_op jit(solution)/shard_map/while/body/eval_jaxpr/convert_element_type | solution.py:78
  713.6 10.2 fusion.125
  723.8 6.8 fusion.126
  743.8 63.5 %all-reduce.1 = (f32[384]{0:T(512)}, f32[192]{0:T(256)}, f32[1536]{0:T(1024)}) all-reduce(f32[384]{0:T(512)S(1)} %reduce_sum.209, f32[192]{0:T(256)S(1)} %reduce_sum.214, f32[1536]{0:T(1024)S(1)} %copy-done.58), channel_id=1, replica_groups=mesh['dp'=16,'tensor'=2] {'dp'}, use_global_device_ids=true, to_apply=%region_24.25 | all-reduce | flops 2112 | bytes 16896 | tf_op jit(solution)/shard_map/psum | solution.py:282
  816.3 39.1 %all-reduce = (f32[768]{0:T(1024)}, f32[768]{0:T(1024)}, f32[768]{0:T(1024)}, f32[768]{0:T(1024)}, f32[768]{0:T(1024)}, /*index=5*/f32[768]{0:T(1024)}) all-reduce(f32[768]{0:T(1024)S(1)} %copy-done.57, f32[768]{0:T(1024)S(1)} %get-tuple-element.254, ...), channel_id=1, replica_groups=mesh['dp'=16,'tensor'=2] {'dp','tensor'}, use_global_device_ids=true, to_apply=%region_31.32 | all-reduce | flops 4608 | bytes 36864 | tf_op jit(solution)/shard_map/psum | solution.py:261
  855.4 157.5 %all-reduce.5.cloned.1.call-done = (f32[768,384]{1,0:T(8,128)}, f32[768,384]{1,0:T(8,128)}, f32[768,192]{0,1:T(8,128)}, f32[384,768]{1,0:T(8,128)}, f32[768,1536]{1,0:T(8,128)}, /*index=5*/f32[1536,768]{1,0:T(8,128)}) async-done(((f32[768,384]{1,0:T(8,128)}, f32[768,384]{1,0:T(8,128)}, f32[768,192]{0,1:T(8,128)}, f32[384,768]{1,0:T(8,128)}, f32[768,1536]{1,0:T(8,128)}, /*index=5*/f32[1536,768]{1,0:T(8,128)}), ...) | async-done | bytes 13565968 | tf_op jit(solution)/shard_map/psum | solution.py:282
  (344 shorter events, 216.5 us)
Async XLA Ops:
  7.2 280.6 %copy-start = (bf16[768,1536]{1,0:T(8,128)(2,1)S(1)}, bf16[768,1536]{1,0:T(8,128)(2,1)}, u32[]{:S(2)}) copy-start(bf16[768,1536]{1,0:T(8,128)(2,1)} %param.35) | copy-start | bytes 7077892
  7.2 54.7 %all-gather.5.cloned.1.call-start = ((), (), s32[]{:S(2)}) async-start(), calls=%async_computation.4 | async-start | bytes 4718592 | tf_op jit(solution)/shard_map/all_gather | solution.py:126
  12.4 49.6 %copy-start.69 = (f32[192]{0:T(256)S(1)}, f32[192]{0:T(256)}, u32[]{:S(2)}) copy-start(f32[192]{0:T(256)} %param.32) | copy-start | bytes 2308
  14.2 222.2 %reduce-scatter.5.cloned.1.call-start = ((), (), s32[]{:S(2)}) async-start(), calls=%async_computation.5 | async-start | bytes 9437184 | tf_op jit(solution)/shard_map/reduce_scatter | solution.py:161
  80.0 7.1 copy-start.38
  80.0 7.1 copy-start.68
  100.8 52.4 %copy-start.37 = (bf16[384,768]{1,0:T(8,128)(2,1)S(1)}, bf16[384,768]{1,0:T(8,128)(2,1)}, u32[]{:S(2)}) copy-start(bf16[384,768]{1,0:T(8,128)(2,1)} %param.33) | copy-start | bytes 1769476
  111.3 6.6 copy-start.9
  137.4 6.6 copy-start.9
  159.2 77.2 %copy-start.60 = (f32[768]{0:T(1024)S(1)}, f32[768]{0:T(1024)}, u32[]{:S(2)}) copy-start(f32[768]{0:T(1024)} %param.34) | copy-start | bytes 9220
  159.2 128.5 %all-gather.7.cloned.1.call-start = ((), (), s32[]{:S(2)}) async-start(), calls=%async_computation.6 | async-start | bytes 4718592 | tf_op jit(solution)/shard_map/all_gather | solution.py:164
  240.9 46.8 %copy-start.67 = (f32[1536]{0:T(1024)S(1)}, f32[1536]{0:T(1024)}, u32[]{:S(2)}) copy-start(f32[1536]{0:T(1024)} %param.36) | copy-start | bytes 18436
  242.7 91.5 %all-gather.9.cloned.1.call-start = ((), (), s32[]{:S(2)}) async-start(), calls=%async_computation.8 | async-start | bytes 4718592 | tf_op jit(solution)/shard_map/all_gather | solution.py:127
  243.2 192.4 %reduce-scatter.9.cloned.1.call-start = ((), (), s32[]{:S(2)}) async-start(), calls=%async_computation.9 | async-start | bytes 9437184 | tf_op jit(solution)/shard_map/reduce_scatter | solution.py:190
  351.4 7.0 copy-start.71
  358.4 123.3 %reduce-scatter.7.cloned.1.call-start = ((), (), s32[]{:S(2)}) async-start(), calls=%async_computation.7 | async-start | bytes 4718592 | tf_op jit(solution)/shard_map/reduce_scatter | solution.py:170
  369.7 112.0 %copy-start.62 = (f32[768]{0:T(1024)S(1)}, f32[768]{0:T(1024)}, u32[]{:S(2)}) copy-start(f32[768]{0:T(1024)} %param.38) | copy-start | bytes 9220
  369.7 164.8 %all-gather.11.cloned.1.call-start = ((), (), s32[]{:S(2)}) async-start(), calls=%async_computation.10 | async-start | bytes 4718592 | tf_op jit(solution)/shard_map/all_gather | solution.py:195
  439.7 47.2 %copy-start.21 = (bf16[2,512,768]{2,1,0:T(8,128)(2,1)S(1)}, bf16[2,512,768]{2,1,0:T(8,128)(2,1)}, u32[]{:S(2)}) copy-start(bf16[2,512,768]{2,1,0:T(8,128)(2,1)} %param.43) | copy-start | bytes 4718596
  489.5 317.9 %reduce-scatter.11.cloned.1.call-start = ((), (), s32[]{:S(2)}) async-start(), calls=%async_computation.11 | async-start | bytes 4718592 | tf_op jit(solution)/shard_map/reduce_scatter | solution.py:248
  555.9 6.4 copy-start.13
  628.0 6.4 copy-start.13
  710.1 302.9 %all-reduce.5.cloned.1.call-start = ((), (), s32[]{:S(2)}) async-start(), calls=%async_computation.12 | async-start | bytes 27131904 | tf_op jit(solution)/shard_map/psum | solution.py:282
  713.1 10.7 %slice-start.4 = ((s8[6291456]{0:T(1024)(128)(4,1)}), s8[4194304]{0:T(1024)(128)(4,1)S(1)}, s32[]{:S(2)}) async-start(s8[6291456]{0:T(1024)(128)(4,1)} %bitcast.310), calls=%async_computation.17 | async-start | bytes 8388608
  713.6 10.2 copy-start.64
  713.6 10.2 slice-start.5
  723.8 6.8 copy-start.33
  740.5 66.9 %copy-start.8 = (bf16[2,512,768]{2,1,0:T(8,128)(2,1)S(1)}, bf16[2,512,768]{2,1,0:T(8,128)(2,1)}, u32[]{:S(2)}) copy-start(bf16[2,512,768]{2,1,0:T(8,128)(2,1)} %param.24) | copy-start | bytes 4718596
  740.5 66.9 %copy-start.45 = (f32[2,512]{1,0:T(2,128)S(1)}, f32[2,512]{1,0:T(2,128)}, u32[]{:S(2)}) copy-start(f32[2,512]{1,0:T(2,128)} %copy-done.44) | copy-start | bytes 12292
  740.5 66.9 %copy-start.47 = (f32[768]{0:T(1024)S(1)}, f32[768]{0:T(1024)}, u32[]{:S(2)}) copy-start(f32[768]{0:T(1024)} %param.39) | copy-start | bytes 9220
  743.4 66.8 %copy-start.53 = (f32[2,512]{1,0:T(2,128)S(1)}, f32[2,512]{1,0:T(2,128)}, u32[]{:S(2)}) copy-start(f32[2,512]{1,0:T(2,128)} %copy-done.52) | copy-start | bytes 12292
  743.4 66.8 %copy-start.49 = (f32[2,512]{1,0:T(2,128)S(1)}, f32[2,512]{1,0:T(2,128)}, u32[]{:S(2)}) copy-start(f32[2,512]{1,0:T(2,128)} %copy-done.48) | copy-start | bytes 12292
  (69 other events, 218.1 us)
Sparse Core Ops, SparseCore 0:
  14.3 47.6 all-gather.4
  159.3 77.0 reduce-scatter.4
  242.8 44.9 all-gather.6
  289.2 44.9 all-gather.8
  358.5 77.0 reduce-scatter.8
  438.3 43.3 reduce-scatter.6
  489.6 44.9 all-gather.10
  710.2 43.3 reduce-scatter.10
  760.1 252.8 all-reduce.4
where the time goes:
time: 1040 us; the launch traced here: 1030 us
  waiting for transfers between devices  512 us (49%)
  matrix products  226 us (22%)
  blocking collectives  103 us (10%)
  other arithmetic  94.8 us (9%)
  local copies, waits for them, and re-layouts  78.9 us (8%)
  between operations  14.7 us (1%)
    psum x1, waiting for transfers between devices, on_device(): lax.psum((query_weight_grad, query_bias_grad, key_weight_grad, value_weig...  158 us
    reduce_scatter x1, waiting for transfers between devices, on_device(): lax.psum_scatter(attn_part, 'tensor', scatter_dimension=1, tiled=True)  77.2 us
    reduce_scatter x1, waiting for transfers between devices, on_device(): lax.psum_scatter(second_part, 'tensor', scatter_dimension=1, tiled=True)  65.8 us
    psum x1, blocking collectives, on_device(): lax.psum((query_weight_grad, query_bias_grad, key_weight_grad, value_weig...  63.5 us
    all_gather x1, waiting for transfers between devices, on_device(): lax.all_gather(normed_share, 'tensor', axis=1, tiled=True)  45.8 us
    all_gather x1, waiting for transfers between devices, on_device(): lax.all_gather(hidden_low, 'tensor', axis=1, tiled=True)  45 us
    all_gather x1, waiting for transfers between devices, on_device(): lax.all_gather(second_share, 'tensor', axis=1, tiled=True)  44.5 us
    reduce_scatter x1, waiting for transfers between devices, on_device(): lax.psum_scatter(down_part.astype(jnp.bfloat16), 'tensor', scatter_dimens...  42 us
  transfers between devices with their start and end apart: 9, of which 8 were waited for; matrix products, arithmetic and copies ran while one was open for 7% of the time, Pallas kernels for 0%

commit v1 on v0

v1 whole, which is shorter than its diff:
```python
import functools

import jax
import jax.numpy as jnp
from jax import lax
from jax.experimental import pallas as pl
from jax.experimental.pallas import tpu as pltpu
from jax.sharding import PartitionSpec as P

DH = 64
BF = jnp.bfloat16
F32 = jnp.float32
SPAN = 256
QB = 128
WIN = SPAN + QB
TH = 256
RC = 256
NEG = -1000000000.0


def layer_norm(values, gain_row, shift_row):
    center = values - jnp.mean(values, axis=-1, keepdims=True)
    variance = jnp.mean(center * center, axis=-1, keepdims=True)
    return center * lax.rsqrt(variance + 1e-05) * gain_row + shift_row


def dot_nn(a, b):
    return lax.dot_general(a, b, (((1,), (0,)), ((), ())), preferred_element_type=F32)


def dot_nt(a, b):
    return lax.dot_general(a, b, (((1,), (1,)), ((), ())), preferred_element_type=F32)


def dot_tn(a, b):
    return lax.dot_general(a, b, (((0,), (0,)), ((), ())), preferred_element_type=F32)


def split_pair(block, low_lane):
    zero = jnp.zeros_like(block)
    return jnp.concatenate(
        [jnp.where(low_lane, block, zero), jnp.where(low_lane, zero, block)], axis=0
    )


def window_bias(kseg_ref, qseg_ref, start):
    key_at = lax.broadcasted_iota(jnp.int32, (WIN, QB), 0)
    query_at = lax.broadcasted_iota(jnp.int32, (WIN, QB), 1) + SPAN
    kseg = kseg_ref[0, start : start + WIN, :]
    qseg = qseg_ref[0, :, start : start + QB]
    allowed = ((kseg == qseg) & (key_at <= query_at)) | (key_at == query_at)
    bias = jnp.where(allowed, 0.0, NEG).astype(F32)
    return jnp.concatenate([bias, bias], axis=1)


def fill_keys(k_s, v_s, ko_ref, kh_ref, fo_ref, fh_ref, so_ref, sh_ref):
    span = kh_ref.shape[0]
    length = ko_ref.shape[0]
    for pair in range(2):
        cols = slice(pair * 128, pair * 128 + 128)
        k_s[pair, :span] = kh_ref[:, cols]
        k_s[pair, span:] = ko_ref[:, cols]
        for at, size, f_ref, s_ref in ((0, span, fh_ref, sh_ref), (span, length, fo_ref, so_ref)):
            fresh = f_ref[...]
            reused = s_ref[...]
            low = lax.broadcasted_iota(jnp.int32, (size, 128), 1) < DH
            if pair == 0:
                both = jnp.where(low, fresh, pltpu.roll(reused.astype(F32), DH, 1).astype(BF))
            else:
                both = jnp.where(low, pltpu.roll(fresh.astype(F32), DH, 1).astype(BF), reused)
            v_s[pair, at : at + size] = both


def attend_forward_kernel(
    q_ref, ko_ref, kh_ref, fo_ref, fh_ref, so_ref, sh_ref, kseg_ref, qseg_ref, o_ref, lse_ref, k_s, v_s
):
    fill_keys(k_s, v_s, ko_ref, kh_ref, fo_ref, fh_ref, so_ref, sh_ref)
    low = lax.broadcasted_iota(jnp.int32, (QB, 128), 1) < DH
    turned = [v_s[pair].T for pair in range(2)]
    for start in range(0, q_ref.shape[0], QB):
        bias = window_bias(kseg_ref, qseg_ref, start)
        for pair in range(2):
            cols = slice(pair * 128, pair * 128 + 128)
            queries = split_pair(q_ref[start : start + QB, cols], low)
            scores = dot_nt(k_s[pair, start : start + WIN], queries) + bias
            largest = jnp.max(scores, axis=0, keepdims=True)
            expon = jnp.exp(scores - largest)
            total = jnp.sum(expon, axis=0, keepdims=True)
            probs = (expon * (1.0 / total)).astype(BF)
            out = dot_nn(turned[pair][:, start : start + WIN], probs)
            out = jnp.concatenate([out[:DH, :QB], out[DH:, QB:]], axis=0)
            o_ref[start : start + QB, cols] = out.T.astype(BF)
            sums = largest + jnp.log(total)
            lse_ref[0, 0, 2 * pair : 2 * pair + 1, start : start + QB] = sums[:, :QB]
            lse_ref[0, 0, 2 * pair + 1 : 2 * pair + 2, start : start + QB] = sums[:, QB:]


def attend_backward_kernel(
    q_ref,
    ko_ref,
    kh_ref,
    fo_ref,
    fh_ref,
    so_ref,
    sh_ref,
    kseg_ref,
    qseg_ref,
    lse_ref,
    g_ref,
    dq_ref,
    dko_ref,
    dkh_ref,
    dfo_ref,
    dfh_ref,
    dso_ref,
    dsh_ref,
    k_s,
    v_s,
    dk_s,
    dv_s,
):
    fill_keys(k_s, v_s, ko_ref, kh_ref, fo_ref, fh_ref, so_ref, sh_ref)
    span = kh_ref.shape[0]
    length = ko_ref.shape[0]
    low = lax.broadcasted_iota(jnp.int32, (QB, 128), 1) < DH
    turned = [k_s[pair].T for pair in range(2)]
    dk_s[...] = jnp.zeros_like(dk_s)
    dv_s[...] = jnp.zeros_like(dv_s)
    for start in range(0, length, QB):
        bias = window_bias(kseg_ref, qseg_ref, start)
        rows = slice(start, start + QB)
        win = slice(start, start + WIN)
        for pair in range(2):
            cols = slice(pair * 128, pair * 128 + 128)
            queries = split_pair(q_ref[rows, cols], low)
            grads = split_pair(g_ref[rows, cols], low)
            sums = jnp.concatenate(
                [
                    lse_ref[0, 0, 2 * pair : 2 * pair + 1, rows],
                    lse_ref[0, 0, 2 * pair + 1 : 2 * pair + 2, rows],
                ],
                axis=1,
            )
            scores = dot_nt(k_s[pair, win], queries) + bias
            probs = jnp.exp(scores - sums)
            prob_grad = dot_nt(v_s[pair, win], grads)
            row_total = jnp.sum(probs * prob_grad, axis=0, keepdims=True)
            score_grad = (probs * (prob_grad - row_total)).astype(BF)
            dv_s[pair, win] += dot_nn(probs.astype(BF), grads)
            dk_s[pair, win] += dot_nn(score_grad, queries)
            out = dot_nn(turned[pair][:, win], score_grad)
            out = jnp.concatenate([out[:DH, :QB], out[DH:, QB:]], axis=0)
            dq_ref[rows, cols] = (out.T * (DH**-0.5)).astype(BF)
    for pair in range(2):
        cols = slice(pair * 128, pair * 128 + 128)
        dkh_ref[:, cols] = dk_s[pair, :span].astype(BF)
        dko_ref[:, cols] = dk_s[pair, span:].astype(BF)
    for at, size, f_ref, s_ref in ((0, span, dfh_ref, dsh_ref), (span, length, dfo_ref, dso_ref)):
        rows = slice(at, at + size)
        low = lax.broadcasted_iota(jnp.int32, (size, 128), 1) < DH
        first, second = dv_s[0, rows], dv_s[1, rows]
        f_ref[...] = jnp.where(low, first, pltpu.roll(second, DH, 1)).astype(BF)
        s_ref[...] = jnp.where(low, pltpu.roll(first, DH, 1), second).astype(BF)


def attention_specs(rows, length, heads):
    width = heads * DH
    quads = width // 256
    q_spec = pl.BlockSpec((length, 256), lambda r, j: (r, j))
    ko_spec = pl.BlockSpec((length, 256), lambda r, j: (r, quads + j))
    kh_spec = pl.BlockSpec((SPAN, 256), lambda r, j: (r, j))
    fo_spec = pl.BlockSpec((length, 128), lambda r, j: (r, 4 * quads + j))
    fh_spec = pl.BlockSpec((SPAN, 128), lambda r, j: (r, 2 * quads + j))
    so_spec = pl.BlockSpec((length, 128), lambda r, j: (r, j))
    sh_spec = pl.BlockSpec((SPAN, 128), lambda r, j: (r, j))
    kseg_spec = pl.BlockSpec((1, SPAN + length, 1), lambda r, j: (r, 0, 0))
    qseg_spec = pl.BlockSpec((1, 1, length), lambda r, j: (r, 0, 0))
    lse_spec = pl.BlockSpec((1, 1, 4, length), lambda r, j: (r, j, 0, 0))
    ins = [q_spec, ko_spec, kh_spec, fo_spec, fh_spec, so_spec, sh_spec, kseg_spec, qseg_spec]
    return quads, ins, lse_spec


def attend_forward(qkv, kv_halo, skip_own, skip_halo, kseg, qseg, rows, length, heads):
    quads, ins, lse_spec = attention_specs(rows, length, heads)
    pairs = rows * heads * length * WIN
    return pl.pallas_call(
        attend_forward_kernel,
        grid=(rows, quads),
        in_specs=ins,
        out_specs=[pl.BlockSpec((length, 256), lambda r, j: (r, j)), lse_spec],
        out_shape=[
            jax.ShapeDtypeStruct((rows * length, heads * DH), BF),
            jax.ShapeDtypeStruct((rows, quads, 4, length), F32),
        ],
        scratch_shapes=[
            pltpu.VMEM((2, SPAN + length, 128), BF),
            pltpu.VMEM((2, SPAN + length, 128), BF),
        ],
        cost_estimate=pl.CostEstimate(
            flops=pairs * DH * 16, bytes_accessed=10 << 20, transcendentals=pairs
        ),
        name="attend_forward",
    )(qkv, qkv, kv_halo, qkv, kv_halo, skip_own, skip_halo, kseg, qseg)


def attend_backward(
    qkv, kv_halo, skip_own, skip_halo, kseg, qseg, sums, grads, rows, length, heads
):
    quads, ins, lse_spec = attention_specs(rows, length, heads)
    pairs = rows * heads * length * WIN
    own = pl.BlockSpec((length, 256), lambda r, j: (r, j))
    halo = pl.BlockSpec((SPAN, 256), lambda r, j: (r, j))
    own_half = pl.BlockSpec((length, 128), lambda r, j: (r, j))
    halo_half = pl.BlockSpec((SPAN, 128), lambda r, j: (r, j))
    width = heads * DH

    def shape(count, columns):
        return jax.ShapeDtypeStruct((rows * count, columns), BF)

    return pl.pallas_call(
        attend_backward_kernel,
        grid=(rows, quads),
        in_specs=ins + [lse_spec, own],
        out_specs=[own, own, halo, own_half, halo_half, own_half, halo_half],
        out_shape=[
            shape(length, width),
            shape(length, width),
            shape(SPAN, width),
            shape(length, width // 2),
            shape(SPAN, width // 2),
            shape(length, width // 2),
            shape(SPAN, width // 2),
        ],
        scratch_shapes=[
            pltpu.VMEM((2, SPAN + length, 128), BF),
            pltpu.VMEM((2, SPAN + length, 128), BF),
            pltpu.VMEM((2, SPAN + length, 128), F32),
            pltpu.VMEM((2, SPAN + length, 128), F32),
        ],
        cost_estimate=pl.CostEstimate(
            flops=pairs * DH * 40, bytes_accessed=18 << 20, transcendentals=pairs
        ),
        name="attend_backward",
    )(qkv, qkv, kv_halo, qkv, kv_halo, skip_own, skip_halo, kseg, qseg, sums, grads)


def feed_kernel(
    core_ref,
    n_ref,
    g_ref,
    ua_ref,
    ub_ref,
    ba_ref,
    bb_ref,
    da_ref,
    db_ref,
    wua_ref,
    wub_ref,
    wda_ref,
    wdb_ref,
    ga_ref,
    gb_ref,
    down_ref,
    second_ref,
    turned_s,
    act_s,
    upg_s,
):
    step = pl.program_id(0)
    half = pl.num_programs(0) // 2
    first = step < half

    @pl.when(step == 0)
    def _():
        turned_s[...] = n_ref[...].T
        down_ref[...] = jnp.zeros_like(down_ref)
        second_ref[...] = jnp.zeros_like(second_ref)

    up_tile = jnp.where(first, ua_ref[...], ub_ref[...])
    down_tile = jnp.where(first, da_ref[...], db_ref[...])
    bias = jnp.where(first, ba_ref[...], bb_ref[...])
    root = 0.7978845608028654
    for start in range(0, n_ref.shape[0], RC):
        rows = slice(start, start + RC)
        upward = dot_nn(n_ref[rows, :], up_tile) + bias
        act_grad = dot_nt(g_ref[rows, :], down_tile)
        square = upward * upward
        bent = jnp.tanh(root * upward * (1.0 + 0.044715 * square))
        gate = 0.5 * (1.0 + bent)
        slope = gate + 0.5 * root * upward * (1.0 - bent * bent) * (1.0 + 0.134145 * square)
        act = (upward * gate).astype(BF)
        upg = (act_grad * slope).astype(BF)
        act_s[rows, :] = act
        upg_s[rows, :] = upg
        down_ref[rows, :] += dot_nn(act, down_tile)
        second_ref[rows, :] += dot_nt(upg, up_tile)
    up_weight_grad = dot_nn(turned_s[...], upg_s[...]).astype(BF)
    down_weight_grad = dot_tn(act_s[...], g_ref[...]).astype(BF)
    bias_grad = jnp.sum(upg_s[...].astype(F32), axis=0, keepdims=True)

    @pl.when(first)
    def _():
        wua_ref[...] = up_weight_grad
        wda_ref[...] = down_weight_grad
        ga_ref[...] = bias_grad

    @pl.when(jnp.logical_not(first))
    def _():
        wub_ref[...] = up_weight_grad
        wdb_ref[...] = down_weight_grad
        gb_ref[...] = bias_grad


def feed(core, normed, grads, up_a, up_b, bias_a, bias_b, down_a, down_b, whole):
    tokens, width = normed.shape
    piece = up_a.shape[1] // 2 if whole else up_a.shape[1]
    tiles = piece // TH

    def a_at(i, c):
        at = jnp.minimum(i, tiles - 1)
        return at + (1 - c[0]) * tiles if whole else at

    def b_at(i, c):
        at = jnp.maximum(i - tiles, 0)
        return at + c[0] * tiles if whole else at

    def out_a(i, c):
        return jnp.minimum(i, tiles - 1)

    def out_b(i, c):
        return jnp.maximum(i - tiles, 0)

    resident = pl.BlockSpec((tokens, width), lambda i, c: (0, 0))
    once = pl.BlockSpec((tokens, width), lambda i, c: (0, 0))
    in_specs = [
        resident,
        resident,
        pl.BlockSpec((width, TH), lambda i, c: (0, a_at(i, c))),
        pl.BlockSpec((width, TH), lambda i, c: (0, b_at(i, c))),
        pl.BlockSpec((1, TH), lambda i, c: (0, a_at(i, c))),
        pl.BlockSpec((1, TH), lambda i, c: (0, b_at(i, c))),
        pl.BlockSpec((TH, width), lambda i, c: (a_at(i, c), 0)),
        pl.BlockSpec((TH, width), lambda i, c: (b_at(i, c), 0)),
    ]
    out_specs = [
        pl.BlockSpec((width, TH), lambda i, c: (0, out_a(i, c))),
        pl.BlockSpec((width, TH), lambda i, c: (0, out_b(i, c))),
        pl.BlockSpec((TH, width), lambda i, c: (out_a(i, c), 0)),
        pl.BlockSpec((TH, width), lambda i, c: (out_b(i, c), 0)),
        pl.BlockSpec((1, TH), lambda i, c: (0, out_a(i, c))),
        pl.BlockSpec((1, TH), lambda i, c: (0, out_b(i, c))),
        once,
        once,
    ]
    out_shape = [
        jax.ShapeDtypeStruct((width, piece), BF),
        jax.ShapeDtypeStruct((width, piece), BF),
        jax.ShapeDtypeStruct((piece, width), BF),
        jax.ShapeDtypeStruct((piece, width), BF),
        jax.ShapeDtypeStruct((1, piece), F32),
        jax.ShapeDtypeStruct((1, piece), F32),
        jax.ShapeDtypeStruct((tokens, width), F32),
        jax.ShapeDtypeStruct((tokens, width), F32),
    ]
    return pl.pallas_call(
        feed_kernel,
        grid_spec=pltpu.PrefetchScalarGridSpec(
            num_scalar_prefetch=1,
            grid=(2 * tiles,),
            in_specs=in_specs,
            out_specs=out_specs,
            scratch_shapes=[
                pltpu.VMEM((width, tokens), BF),
                pltpu.VMEM((tokens, TH), BF),
                pltpu.VMEM((tokens, TH), BF),
            ],
        ),
        out_shape=out_shape,
        compiler_params=pltpu.CompilerParams(vmem_limit_bytes=56 << 20),
        cost_estimate=pl.CostEstimate(
            flops=24 * tokens * width * piece,
            bytes_accessed=20 << 20,
            transcendentals=2 * tokens * piece,
        ),
        name="feed",
    )(core, normed, grads, up_a, up_b, bias_a, bias_b, down_a, down_b)


def swap_perm(count):
    return [(i, i ^ 1) for i in range(count)]


class Ring:
    def __init__(self, count):
        self.count = count
        chips = count // 2
        self.factors = []
        if (chips.bit_length() - 1) % 2:
            self.factors.append(2)
            chips //= 2
        while chips > 1:
            self.factors.append(4)
            chips //= 4
        self.index = lax.axis_index("dp")
        self.core = self.index % 2

    def swap_core(self, value):
        return lax.ppermute(value, "dp", swap_perm(self.count))

    def shift(self, value, stride, factor, by):
        perm = []
        for i in range(self.count):
            digit = (i // stride) % factor
            perm.append((i, i + (((digit + by) % factor) - digit) * stride))
        return lax.ppermute(value, "dp", perm)

    def stages(self):
        stride = 2
        for factor in self.factors:
            yield stride, factor, (self.index // stride) % factor
            stride *= factor

    def sum_chips(self, value):
        stages = list(self.stages())
        for stride, factor, digit in stages:
            rows = value.shape[0] // factor
            total = lax.dynamic_slice_in_dim(value, digit * rows, rows, 0).astype(F32)
            for by in range(1, factor):
                part = lax.dynamic_slice_in_dim(value, ((digit + by) % factor) * rows, rows, 0)
                total = total + self.shift(part, stride, factor, by).astype(F32)
            value = total.astype(BF)
        for stride, factor, digit in reversed(stages):
            parts = [value] + [self.shift(value, stride, factor, by) for by in range(1, factor)]
            value = jnp.concatenate(
                [lax.select_n((digit - at) % factor, *parts)
                 if factor > 2 else jnp.where(digit == at, parts[0], parts[1])
                 for at in range(factor)],
                axis=0,
            )
        return value

    def sum_small(self, value):
        value = value + self.swap_core(value)
        for stride, factor, digit in self.stages():
            total = value
            for by in range(1, factor):
                total = total + self.shift(value, stride, factor, by)
            value = total
        return value


def swap_tensor(value):
    return lax.ppermute(value, "tensor", [(0, 1), (1, 0)])


def own_half(value, at, axis):
    size = value.shape[axis] // 2
    return lax.dynamic_slice_in_dim(value, at * size, size, axis)


def in_order(core, mine, other, axis):
    return jnp.concatenate(
        [jnp.where(core == 0, mine, other), jnp.where(core == 0, other, mine)], axis=axis
    )


def on_device(
    dp_count,
    block_input,
    skip_values,
    segment_ids,
    row_fill,
    query_weight,
    query_bias,
    key_weight,
    value_weight,
    value_bias,
    out_weight,
    out_bias,
    up_weight,
    up_bias,
    down_weight,
    down_bias,
    first_gain,
    first_shift,
    second_gain,
    second_shift,
    cotangent,
):
    ring = Ring(dp_count)
    core = ring.core
    side = lax.axis_index("tensor")
    rows, length, width = block_input.shape
    tokens = rows * length
    local = query_weight.shape[1]
    local_half = local // 2
    heads = 2 * local // DH
    hidden_local = up_weight.shape[1]

    share_input = block_input.astype(F32)
    normed = layer_norm(share_input, first_gain, first_shift).astype(BF)
    normed_halo = lax.ppermute(normed[:, length - SPAN :], "tensor", [(0, 1)])
    normed = normed.reshape(tokens, width)
    normed_halo = normed_halo.reshape(rows * SPAN, width)

    def fetch(weight, axis):
        mine = swap_tensor(own_half(weight, core, axis))
        return mine, ring.swap_core(mine)

    qkv_own = jnp.concatenate([query_weight, key_weight, value_weight], axis=1)
    qkv_other = in_order(core, *fetch(qkv_own, 0), 0)
    cuts = (0, local, 2 * local, 2 * local + local_half)
    qkv_weight = jnp.concatenate(
        [
            piece[:, cuts[n] : cuts[n + 1]]
            for n in range(3)
            for piece in (qkv_own, qkv_other)
        ],
        axis=1,
    )
    small_other = swap_tensor(jnp.concatenate([query_bias, value_bias, up_bias]))
    query_bias_all = jnp.concatenate([query_bias, small_other[:local]])
    value_bias_all = jnp.concatenate([value_bias, small_other[local : local + local_half]])
    up_bias_other = small_other[local + local_half :]

    skip_mid = skip_values[:, length - SPAN : length]
    skip_send = jnp.concatenate(
        [skip_mid, lax.dynamic_slice_in_dim(skip_values, (1 - side) * length, length, 1)], axis=1
    )
    skip_got = swap_tensor(skip_send)
    skip_own = jnp.concatenate(
        [lax.dynamic_slice_in_dim(skip_values, side * length, length, 1), skip_got[:, SPAN:]],
        axis=2,
    ).reshape(tokens, local)
    skip_halo = jnp.concatenate([skip_mid, skip_got[:, :SPAN]], axis=2).reshape(rows * SPAN, local)

    position = jnp.arange(segment_ids.shape[1], dtype=jnp.int32)
    usable = jnp.where(position[None] < row_fill[:, None], segment_ids, -1)
    query_seg = lax.dynamic_slice_in_dim(segment_ids, side * length, length, 1)
    key_seg = jnp.concatenate(
        [
            jnp.where(side == 0, -1, usable[:, length - SPAN : length]),
            lax.dynamic_slice_in_dim(usable, side * length, length, 1),
        ],
        axis=1,
    )
    query_seg = query_seg.reshape(rows, 1, length)
    key_seg = key_seg.reshape(rows, SPAN + length, 1)

    scale = jnp.concatenate([jnp.full((2 * local,), DH**-0.5, F32), jnp.ones((3 * local,), F32)])
    qkv_bias = jnp.concatenate([query_bias_all, jnp.zeros((2 * local,), F32), value_bias_all])
    qkv = ((dot_nn(normed, qkv_weight) + qkv_bias) * scale).astype(BF)
    kv_halo = (dot_nn(normed_halo, qkv_weight[:, 2 * local :]) + qkv_bias[2 * local :]).astype(BF)
    mixed, sums = attend_forward(
        qkv, kv_halo, skip_own, skip_halo, key_seg, query_seg, rows, length, heads
    )
    out_other = in_order(core, *fetch(out_weight, 0), 0)
    out_all = jnp.concatenate([out_weight, out_other], axis=0)
    hidden = share_input.reshape(tokens, width) + (dot_nn(mixed, out_all) + out_bias)
    normed_two = layer_norm(hidden, second_gain, second_shift).astype(BF)

    out_grad = cotangent.reshape(tokens, width)
    core_at = core.reshape(1).astype(jnp.int32)
    up_mine, up_theirs = fetch(up_weight, 1)
    down_mine, down_theirs = fetch(down_weight, 0)
    bias_row = up_bias.reshape(1, hidden_local)
    (up_l2, up_l1, down_l2, down_l1, bias_l2, bias_l1, down_sum_l, second_sum_l) = feed(
        core_at, normed_two, out_grad, up_weight, up_weight, bias_row, bias_row,
        down_weight, down_weight, True,
    )
    (up_r2, up_r1, down_r2, down_r1, bias_r2, bias_r1, down_sum_r, second_sum_r) = feed(
        core_at, normed_two, out_grad, up_theirs, up_mine,
        own_half(up_bias_other, 1 - core, 0).reshape(1, -1),
        own_half(up_bias_other, core, 0).reshape(1, -1),
        down_theirs, down_mine, False,
    )
    block_output = hidden + (down_sum_l + down_sum_r + down_bias)
    cot = out_grad.astype(F32)
    down_bias_grad = jnp.sum(cot, axis=0)
    second_grad = second_sum_l + second_sum_r
    _, second_pull = jax.vjp(layer_norm, hidden, second_gain, second_shift)
    hidden_part, second_gain_grad, second_shift_grad = second_pull(second_grad)
    hidden_grad = cot + hidden_part
    hidden_low = hidden_grad.astype(BF)
    out_bias_grad = jnp.sum(hidden_low.astype(F32), axis=0)

    def sum_pieces(l1, l2, r1, r2):
        r1 = (r1.astype(F32) + ring.swap_core(r2).astype(F32)).astype(BF)
        l1 = l1.astype(F32) + ring.swap_core(l2).astype(F32)
        mine = ring.sum_chips((l1 + swap_tensor(r1).astype(F32)).astype(BF))
        return mine.astype(F32), ring.swap_core(mine).astype(F32)

    up_weight_grad = in_order(core, *sum_pieces(up_l1, up_l2, up_r1, up_r2), 1)
    down_weight_grad = in_order(core, *sum_pieces(down_l1, down_l2, down_r1, down_r2), 0)

    mixed_grad = dot_nt(hidden_low, out_all).astype(BF)
    out_grad_all = dot_tn(mixed, hidden_low).astype(BF)

    def cut(value, axis):
        return own_half(value, core, axis), own_half(value, 1 - core, axis)

    out_weight_grad = in_order(
        core, *sum_pieces(*cut(out_grad_all[:local], 1), *cut(out_grad_all[local:], 1)), 1
    )

    (query_g, key_g, key_g_halo, fresh_g, fresh_g_halo, skip_g, skip_g_halo) = attend_backward(
        qkv, kv_halo, skip_own, skip_halo, key_seg, query_seg, sums, mixed_grad, rows, length, heads
    )
    first_halo = dot_nt(key_g_halo, qkv_weight[:, 2 * local : 4 * local]) + dot_nt(
        fresh_g_halo, qkv_weight[:, 4 * local :]
    )
    first_got = lax.ppermute(first_halo.astype(BF), "tensor", [(1, 0)])
    first_grad = (
        dot_nt(query_g, qkv_weight[:, : 2 * local])
        + dot_nt(key_g, qkv_weight[:, 2 * local : 4 * local])
        + dot_nt(fresh_g, qkv_weight[:, 4 * local :])
    )
    first_grad = first_grad.reshape(rows, length, width) + jnp.pad(
        first_got.astype(F32).reshape(rows, SPAN, width), ((0, 0), (length - SPAN, 0), (0, 0))
    )
    _, first_pull = jax.vjp(layer_norm, share_input, first_gain, first_shift)
    input_part, first_gain_grad, first_shift_grad = first_pull(first_grad)
    input_grad = hidden_grad.reshape(rows, length, width) + input_part

    query_w = dot_tn(normed, query_g)
    key_w = dot_tn(normed, key_g) + dot_tn(normed_halo, key_g_halo)
    fresh_w = dot_tn(normed, fresh_g) + dot_tn(normed_halo, fresh_g_halo)
    own_w = jnp.concatenate([query_w[:, :local], key_w[:, :local], fresh_w[:, :local_half]], axis=1)
    other_w = jnp.concatenate([query_w[:, local:], key_w[:, local:], fresh_w[:, local_half:]], axis=1)
    qkv_grad = in_order(
        core, *sum_pieces(*cut(own_w.astype(BF), 0), *cut(other_w.astype(BF), 0)), 0
    )

    skip_g = skip_g.reshape(rows, length, local)
    skip_g_halo = skip_g_halo.reshape(rows, SPAN, local)
    got = swap_tensor(
        jnp.concatenate([skip_g_halo[:, :, local_half:], skip_g[:, :, local_half:]], axis=1)
    ).astype(F32)
    mine = skip_g[:, :, :local_half].astype(F32)
    extra = skip_g_halo[:, :, :local_half].astype(F32) + got[:, :SPAN]
    low = jnp.where(side == 0, mine, got[:, SPAN:])
    high = jnp.where(side == 0, got[:, SPAN:], mine)
    low = jnp.concatenate([low[:, : length - SPAN], low[:, length - SPAN :] + extra], axis=1)
    skip_grad = jnp.concatenate([low, high], axis=1)

    query_b = jnp.sum(query_g.astype(F32), axis=0)
    fresh_b = jnp.sum(fresh_g.astype(F32), axis=0) + jnp.sum(fresh_g_halo.astype(F32), axis=0)
    up_b_own = in_order(core, bias_l1[0], bias_l2[0], 0)
    up_b_other = in_order(core, bias_r1[0], bias_r2[0], 0)
    common = jnp.concatenate(
        [
            out_bias_grad,
            down_bias_grad,
            first_gain_grad,
            first_shift_grad,
            second_gain_grad,
            second_shift_grad,
        ]
    )
    own_small = jnp.concatenate([common, query_b[:local], fresh_b[:local_half], up_b_own])
    other_small = jnp.concatenate([common, query_b[local:], fresh_b[local_half:], up_b_other])
    small = ring.sum_small(own_small + swap_tensor(other_small))
    common = [small[n * width : (n + 1) * width] for n in range(6)]
    at = 6 * width

    return (
        block_output.reshape(rows, length, width),
        input_grad,
        skip_grad,
        qkv_grad[:, :local],
        small[at : at + local],
        qkv_grad[:, local : 2 * local],
        qkv_grad[:, 2 * local :],
        small[at + local : at + local + local_half],
        out_weight_grad,
        common[0],
        up_weight_grad,
        small[at + local + local_half :],
        down_weight_grad,
        common[1],
        common[2],
        common[3],
        common[4],
        common[5],
    )


def solution(mesh):
    in_specs = (
        P("dp", "tensor", None),
        P("dp", None, "tensor"),
        P("dp", None),
        P("dp"),
        P(None, "tensor"),
        P("tensor"),
        P(None, "tensor"),
        P(None, "tensor"),
        P("tensor"),
        P("tensor", None),
        P(),
        P(None, "tensor"),
        P("tensor"),
        P("tensor", None),
        P(),
        P(),
        P(),
        P(),
        P(),
        P("dp", "tensor", None),
    )
    out_specs = (
        P("dp", "tensor", None),
        P("dp", "tensor", None),
        P("dp", None, "tensor"),
        P(None, "tensor"),
        P("tensor"),
        P(None, "tensor"),
        P(None, "tensor"),
        P("tensor"),
        P("tensor", None),
        P(),
        P(None, "tensor"),
        P("tensor"),
        P("tensor", None),
        P(),
        P(),
        P(),
        P(),
        P(),
    )
    return jax.shard_map(
        functools.partial(on_device, mesh.shape["dp"]),
        mesh=mesh,
        in_specs=in_specs,
        out_specs=out_specs,
        check_vma=False,
    )
```

time: 1040 us -> 533 us (0.51)
  waiting for transfers between devices: 512 us -> 187 us
  matrix products: 226 us -> 35.2 us
  Pallas kernels: 0 us -> 104 us
  blocking collectives: 103 us -> 0 us
  starting transfers between devices: 0.54 us -> 74.7 us
  local copies, waits for them, and re-layouts: 78.9 us -> 52.5 us
  other arithmetic: 94.8 us -> 69.1 us
  between operations: 14.7 us -> 2.16 us
    dot_general x46 -> x15, matrix products: 226 us -> 35.2 us  [the longest x6 12.7 us: dot_tn(): lax.dot_general(a, b, (((0,), (0,)), ((), ())), preferred_element_type=F32)]
    ppermute x0 -> x67, waiting for transfers between devices: none -> 187 us  [the longest x36 95.7 us: shift(): return lax.ppermute(value, 'dp', perm)]
    reduce_scatter x4 -> x0, waiting for transfers between devices: 185 us -> none  [the longest x1 77.2 us: on_device(): lax.psum_scatter(attn_part, 'tensor', scatter_dimension=1, tiled=True)]
    all_gather x4 -> x0, waiting for transfers between devices: 168 us -> none  [the longest x1 45.8 us: on_device(): lax.all_gather(normed_share, 'tensor', axis=1, tiled=True)]
    psum x1 -> x0, waiting for transfers between devices: 158 us -> none  [on_device(): lax.psum((query_weight_grad, query_bias_grad, key_weight_grad, value_weig...]
    pallas_call x0 -> x4, Pallas kernels: none -> 104 us  [the longest x2 56.2 us: feed(): pl.pallas_call(feed_kernel, grid_spec=pltpu.PrefetchScalarGridSpec(num_sc...]
    psum x2 -> x0, blocking collectives: 103 us -> none  [the longest x1 63.5 us: on_device(): lax.psum((query_weight_grad, query_bias_grad, key_weight_grad, value_weig...]
    ppermute x0 -> x67, starting transfers between devices: none -> 74.7 us  [the longest x36 54.8 us: shift(): return lax.ppermute(value, 'dp', perm)]
  transfers between devices with their start and end apart: 9 -> 67, of which waited for: 8 -> 22; matrix products, arithmetic and copies ran while one was open for 7% -> 22% of each run, Pallas kernels for 0% -> 10%
where the time goes in v1:
time: 533 us; the launch traced here: 525 us
  waiting for transfers between devices  187 us (35%)
  Pallas kernels  104 us (20%)
  starting transfers between devices  74.7 us (14%)
  other arithmetic  69.1 us (13%)
  local copies, waits for them, and re-layouts  52.5 us (10%)
  matrix products  35.2 us (7%)
    ppermute x36, waiting for transfers between devices, shift(): return lax.ppermute(value, 'dp', perm)  95.7 us
    ppermute x12, waiting for transfers between devices, swap_tensor(): return lax.ppermute(value, 'tensor', [(0, 1), (1, 0)])  91.4 us
    pallas_call x2, Pallas kernels, feed(): pl.pallas_call(feed_kernel, grid_spec=pltpu.PrefetchScalarGridSpec(num_sc...  56.2 us
    ppermute x36, starting transfers between devices, shift(): return lax.ppermute(value, 'dp', perm)  54.8 us
    pallas_call x1, Pallas kernels, attend_forward(): pl.pallas_call(attend_forward_kernel, grid=(rows, quads), in_specs=ins, o...  24.7 us
    pallas_call x1, Pallas kernels, attend_backward(): pl.pallas_call(attend_backward_kernel, grid=(rows, quads), in_specs=ins +...  23.1 us
    unnamed x183, local copies, waits for them, and re-layouts  20.2 us
    ppermute x12, starting transfers between devices, swap_tensor(): return lax.ppermute(value, 'tensor', [(0, 1), (1, 0)])  13.7 us
  transfers between devices with their start and end apart: 67, of which 22 were waited for; matrix products, arithmetic and copies ran while one was open for 22% of the time, Pallas kernels for 10%

profile of v1, /device:TPU:0, one launch (start us, length us, event | category | flops | bytes accessed | tf_op | source)
XLA Modules:
  0.0 524.9 jit_solution(12819803603595087170)
XLA Ops:
  1.6 3.0 collective-permute-start.2
  28.8 66.1 %collective-permute-done.5 = bf16[192,768]{1,0:T(8,128)(2,1)} collective-permute-done((bf16[192,768]{1,0:T(8,128)(2,1)}, bf16[192,768]{1,0:T(8,128)(2,1)}, u32[]{:S(2)}, u32[]{:S(2)}) %collective-permute-start.5) | collective-permute-done | bytes 294944 | tf_op jit(solution)/shard_map/ppermute | solution.py:453
  113.1 5.1 multiply_convert_fusion.q_ref.ko_ref.fo_ref
  120.5 24.7 %attend_forward.1 = (bf16[1024,768]{1,0:T(8,128)(2,1)}, f32[2,3,4,512]{3,2,1,0:T(4,128)}) custom-call(bf16[1024,1920]{1,0:T(8,128)(2,1)} %multiply_convert_fusion.q_ref.ko_ref.fo_ref, bf16[1024,1920]{1,0:T(8,128)(2,1)} %multiply_convert_fusion.q_ref.ko_ref.fo_ref, bf16[512,1152]{1,0:T(8,128)(2,1)} %fusion.kh_ref.fh_ref, ...), custom_call_target="tpu_custom_call" | custom-call | flops 4831838208 | bytes 10485760 | tf_op jit(solution)/shard_map/attend_forward/pallas_call | solution.py:186
  145.2 3.2 fusion.54
  150.8 28.1 %feed.2 = (bf16[768,768]{1,0:T(8,128)(2,1)}, bf16[768,768]{1,0:T(8,128)(2,1)}, bf16[768,768]{1,0:T(8,128)(2,1)}, bf16[768,768]{1,0:T(8,128)(2,1)}, f32[1,768]{1,...) custom-call(s32[1]{0:T(128)} %bitcast.6.core_ref, ...), custom_call_target="tpu_custom_call" | custom-call | flops 14495514624 | bytes 20971520 | tf_op jit(solution)/shard_map/feed/pallas_call | solution.py:365
  180.3 28.1 %feed.3 = (bf16[768,768]{1,0:T(8,128)(2,1)}, bf16[768,768]{1,0:T(8,128)(2,1)}, bf16[768,768]{1,0:T(8,128)(2,1)}, bf16[768,768]{1,0:T(8,128)(2,1)}, f32[1,768]{1,...) custom-call(s32[1]{0:T(128)} %bitcast.6.core_ref, ...), custom_call_target="tpu_custom_call" | custom-call | flops 14495514624 | bytes 20971520 | tf_op jit(solution)/shard_map/feed/pallas_call | solution.py:365
  208.4 4.4 multiply_reduce_fusion
  222.6 23.1 %attend_backward.1 = (bf16[1024,768]{1,0:T(8,128)(2,1)}, bf16[1024,768]{1,0:T(8,128)(2,1)}, bf16[512,768]{1,0:T(8,128)(2,1)}, bf16[1024,384]{1,0:T(8,128)(2,1)},...) custom-call(bf16[1024,1920]{1,0:T(8,128)(2,1)} %multiply_convert_fusion.q_ref.ko_ref.fo_ref, ...), custom_call_target="tpu_custom_call" | custom-call | flops 12079595520 | bytes 18874368 | tf_op jit(solution)/shard_map/attend_backward/pallas_call | solution.py:220
  248.1 4.0 convolution_convert_fusion.2
  257.0 3.1 fusion.17
  269.1 3.0 fusion.12
  286.1 3.5 collective-permute-start.33
  293.7 14.2 %collective-permute-done.33 = bf16[384,384]{1,0:T(8,128)(2,1)} collective-permute-done((bf16[384,384]{1,0:T(8,128)(2,1)}, bf16[384,384]{1,0:T(8,128)(2,1)}, u32[]{:S(2)}, u32[]{:S(2)}) %collective-permute-start.33) | collective-permute-done | bytes 294944 | tf_op jit(solution)/shard_map/ppermute | solution.py:453
  342.8 4.5 add_add_fusion.2
  347.5 4.7 collective-permute-done.29
  352.3 5.6 %collective-permute-done.28 = f32[6720]{0:T(1024)S(1)} collective-permute-done((f32[6720]{0:T(1024)S(1)}, f32[6720]{0:T(1024)S(1)}, u32[]{:S(2)}, u32[]{:S(2)}) %collective-permute-start.28) | collective-permute-done | bytes 26912 | tf_op jit(solution)/shard_map/ppermute | solution.py:415
  364.1 10.8 %collective-permute-done.16 = bf16[192,960]{0,1:T(8,128)(2,1)S(1)} collective-permute-done((bf16[192,960]{0,1:T(8,128)(2,1)S(1)}, bf16[192,960]{0,1:T(8,128)(2,1)S(1)}, u32[]{:S(2)}, u32[]{:S(2)}) %collective-permute-start.16) | collective-permute-done | bytes 368672 | tf_op jit(solution)/shard_map/ppermute | solution.py:415
  378.9 7.7 %collective-permute-done.17 = bf16[48,960]{0,1:T(8,128)(2,1)S(1)} collective-permute-done((bf16[48,960]{0,1:T(8,128)(2,1)S(1)}, bf16[48,960]{0,1:T(8,128)(2,1)S(1)}, u32[]{:S(2)}, u32[]{:S(2)}) %collective-permute-start.17) | collective-permute-done | bytes 92192 | tf_op jit(solution)/shard_map/ppermute | solution.py:415
  386.6 6.6 %collective-permute-done.19 = bf16[48,960]{0,1:T(8,128)(2,1)S(1)} collective-permute-done((bf16[48,960]{0,1:T(8,128)(2,1)S(1)}, bf16[48,960]{0,1:T(8,128)(2,1)S(1)}, u32[]{:S(2)}, u32[]{:S(2)}) %collective-permute-start.19) | collective-permute-done | bytes 92192 | tf_op jit(solution)/shard_map/ppermute | solution.py:415
  393.2 9.7 %collective-permute-done.18 = bf16[48,960]{0,1:T(8,128)(2,1)S(1)} collective-permute-done((bf16[48,960]{0,1:T(8,128)(2,1)S(1)}, bf16[48,960]{0,1:T(8,128)(2,1)S(1)}, u32[]{:S(2)}, u32[]{:S(2)}) %collective-permute-start.18) | collective-permute-done | bytes 92192 | tf_op jit(solution)/shard_map/ppermute | solution.py:415
  405.4 10.3 %collective-permute-done.57 = bf16[768,768]{1,0:T(8,128)(2,1)S(1)} collective-permute-done((bf16[768,768]{1,0:T(8,128)(2,1)S(1)}, bf16[768,768]{1,0:T(8,128)(2,1)S(1)}, u32[]{:S(2)}, u32[]{:S(2)}) %collective-permute-start.57) | collective-permute-done | bytes 1179680 | tf_op jit(solution)/shard_map/ppermute | solution.py:453
  419.5 11.6 %collective-permute-done.21 = bf16[48,960]{0,1:T(8,128)(2,1)S(1)} collective-permute-done((bf16[48,960]{0,1:T(8,128)(2,1)S(1)}, bf16[48,960]{0,1:T(8,128)(2,1)S(1)}, u32[]{:S(2)}, u32[]{:S(2)}) %collective-permute-start.21) | collective-permute-done | bytes 92192 | tf_op jit(solution)/shard_map/ppermute | solution.py:415
  437.4 8.2 %collective-permute-done.46 = bf16[384,768]{1,0:T(8,128)(2,1)S(1)} collective-permute-done((bf16[384,768]{1,0:T(8,128)(2,1)S(1)}, bf16[384,768]{1,0:T(8,128)(2,1)S(1)}, u32[]{:S(2)}, u32[]{:S(2)}) %collective-permute-start.46) | collective-permute-done | bytes 589856 | tf_op jit(solution)/shard_map/ppermute | solution.py:415
  452.5 5.7 %collective-permute-done.60 = bf16[96,768]{1,0:T(8,128)(2,1)S(1)} collective-permute-done((bf16[96,768]{1,0:T(8,128)(2,1)S(1)}, bf16[96,768]{1,0:T(8,128)(2,1)S(1)}, u32[]{:S(2)}, u32[]{:S(2)}) %collective-permute-start.60) | collective-permute-done | bytes 147488 | tf_op jit(solution)/shard_map/ppermute | solution.py:415
  458.3 4.1 collective-permute-start.64
  462.4 6.8 %collective-permute-start.63 = (bf16[96,768]{1,0:T(8,128)(2,1)S(1)}, bf16[96,768]{1,0:T(8,128)(2,1)S(1)}, u32[]{:S(2)}, u32[]{:S(2)}) collective-permute-start(bf16[96,768]{1,0:T(8,128)(2,1)S(1)} %add_convert_fusion.16), channel_id=1, source_target_pairs={{0,16},{2,18},{4,20},{6,22},{8,24},{10,26},{12,28},{14,30},{16,0},... | collective-permute-start | bytes 442376 | tf_op jit(solution)/shard_map/ppermute | solution.py:415
  473.5 4.7 collective-permute-start.52
  478.3 4.6 collective-permute-done.63
  485.7 3.3 collective-permute-done.51
  492.8 4.4 collective-permute-done.65
  499.9 5.9 %collective-permute-done.53 = bf16[384,768]{1,0:T(8,128)(2,1)S(1)} collective-permute-done((bf16[384,768]{1,0:T(8,128)(2,1)S(1)}, bf16[384,768]{1,0:T(8,128)(2,1)S(1)}, u32[]{:S(2)}, u32[]{:S(2)}) %collective-permute-start.53) | collective-permute-done | bytes 589856 | tf_op jit(solution)/shard_map/ppermute | solution.py:415
  (444 shorter events, 189.8 us)
Async XLA Ops:
  1.6 25.2 %collective-permute-start.2 = (f32[2112]{0:T(1024)S(1)}, f32[2112]{0:T(1024)S(1)}, u32[]{:S(2)}, u32[]{:S(2)}) collective-permute-start(f32[2112]{0:T(1024)S(1)} %concatenate.107), channel_id=1, source_target_pairs={{0,1},{1,0},{2,3},{3,2},{4,5},{5,4},{6,7},{7,6},{8,9},{9,8},{10,11... | collective-permute-start | bytes 25352 | tf_op jit(solution)/shard_map/ppermute | solution.py:453
  7.1 20.5 %collective-permute-start = (bf16[384,960]{0,1:T(8,128)(2,1)}, bf16[384,960]{0,1:T(8,128)(2,1)}, u32[]{:S(2)}, u32[]{:S(2)}) collective-permute-start(bf16[384,960]{0,1:T(8,128)(2,1)} %fusion.19), channel_id=1, source_target_pairs={{0,1},{1,0},{2,3},{3,2},{4,5},{5,4},{6,7},{7,6},{8,9},{9,8},{10,11... | collective-permute-start | bytes 2211848 | tf_op jit(solution)/shard_map/ppermute | solution.py:453
  9.3 87.0 %collective-permute-start.4 = (bf16[2,768,192]{1,2,0:T(8,128)(2,1)}, bf16[2,768,192]{1,2,0:T(8,128)(2,1)}, u32[]{:S(2)}, u32[]{:S(2)}) collective-permute-start(bf16[2,768,192]{1,2,0:T(8,128)(2,1)} %pad_maximum_fusion.15), channel_id=1, source_target_pairs={{0,1},{1,0},{2,3},{3,2},{4,5},{5,4},{6,7},{7,6},{8,9},{9,8},{10,11... | collective-permute-start | bytes 1769480 | tf_op jit(solution)/shard_map/ppermute | solution.py:453
  13.2 94.5 %collective-permute-start.9 = (bf16[768,768]{1,0:T(8,128)(2,1)}, bf16[768,768]{1,0:T(8,128)(2,1)}, u32[]{:S(2)}, u32[]{:S(2)}) collective-permute-start(bf16[768,768]{1,0:T(8,128)(2,1)} %constant_dynamic-slice_fusion.20), channel_id=1, source_target_pairs={{0,1},{1,0},{2,3},{3,2},{4,5},{5,4},{6,7},{7,6},{8,9},{9,8},{10,11... | collective-permute-start | bytes 3538952 | tf_op jit(solution)/shard_map/ppermute | solution.py:453
  16.1 91.9 %collective-permute-start.7 = (bf16[768,768]{1,0:T(8,128)(2,1)}, bf16[768,768]{1,0:T(8,128)(2,1)}, u32[]{:S(2)}, u32[]{:S(2)}) collective-permute-start(bf16[768,768]{1,0:T(8,128)(2,1)} %constant_dynamic-slice_fusion.21), channel_id=1, source_target_pairs={{0,1},{1,0},{2,3},{3,2},{4,5},{5,4},{6,7},{7,6},{8,9},{9,8},{10,11... | collective-permute-start | bytes 3538952 | tf_op jit(solution)/shard_map/ppermute | solution.py:453
  26.7 68.1 %collective-permute-start.5 = (bf16[192,768]{1,0:T(8,128)(2,1)}, bf16[192,768]{1,0:T(8,128)(2,1)}, u32[]{:S(2)}, u32[]{:S(2)}) collective-permute-start(bf16[192,768]{1,0:T(8,128)(2,1)} %constant_dynamic-slice_fusion.22), channel_id=1, source_target_pairs={{0,1},{1,0},{2,3},{3,2},{4,5},{5,4},{6,7},{7,6},{8,9},{9,8},{10,11... | collective-permute-start | bytes 884744 | tf_op jit(solution)/shard_map/ppermute | solution.py:453
  27.6 80.7 %collective-permute-start.1 = (bf16[384,960]{0,1:T(8,128)(2,1)}, bf16[384,960]{0,1:T(8,128)(2,1)}, u32[]{:S(2)}, u32[]{:S(2)}) collective-permute-start(bf16[384,960]{0,1:T(8,128)(2,1)} %collective-permute-done), channel_id=1, source_target_pairs={{0,2},{2,0},{4,6},{6,4},{8,10},{10,8},{12,14},{14,12},{16,18},{18,... | collective-permute-start | bytes 2211848 | tf_op jit(solution)/shard_map/ppermute | solution.py:408
  96.3 21.9 %collective-permute-start.3 = (bf16[2,256,768]{2,1,0:T(8,128)(2,1)}, bf16[2,256,768]{2,1,0:T(8,128)(2,1)S(1)}, u32[]{:S(2)}, u32[]{:S(2)}) collective-permute-start(bf16[2,256,768]{2,1,0:T(8,128)(2,1)} %slice.197), channel_id=1, source_target_pairs={{0,1},{2,3},{4,5},{6,7},{8,9},{10,11},{12,13},{14,15},{16,17},{18,... | collective-permute-start | bytes 2359304 | tf_op jit(solution)/shard_map/ppermute | solution.py:502
  107.7 72.6 %collective-permute-start.10 = (bf16[768,768]{1,0:T(8,128)(2,1)}, bf16[768,768]{1,0:T(8,128)(2,1)}, u32[]{:S(2)}, u32[]{:S(2)}) collective-permute-start(bf16[768,768]{1,0:T(8,128)(2,1)} %collective-permute-done.9.db_ref), channel_id=1, source_target_pairs={{0,2},{2,0},{4,6},{6,4},{8,10},{10,8},{12,14},{14,12},{16,18},{18,... | collective-permute-start | bytes 3538952 | tf_op jit(solution)/shard_map/ppermute | solution.py:408
  108.0 72.3 %collective-permute-start.8 = (bf16[768,768]{1,0:T(8,128)(2,1)}, bf16[768,768]{1,0:T(8,128)(2,1)}, u32[]{:S(2)}, u32[]{:S(2)}) collective-permute-start(bf16[768,768]{1,0:T(8,128)(2,1)} %collective-permute-done.7.ub_ref), channel_id=1, source_target_pairs={{0,2},{2,0},{4,6},{6,4},{8,10},{10,8},{12,14},{14,12},{16,18},{18,... | collective-permute-start | bytes 3538952 | tf_op jit(solution)/shard_map/ppermute | solution.py:408
  260.1 100.5 %collective-permute-start.44 = (bf16[768,768]{1,0:T(8,128)(2,1)}, bf16[768,768]{1,0:T(8,128)(2,1)}, u32[]{:S(2)}, u32[]{:S(2)}) collective-permute-start(bf16[768,768]{1,0:T(8,128)(2,1)} %get-tuple-element.63), channel_id=1, source_target_pairs={{0,2},{2,0},{4,6},{6,4},{8,10},{10,8},{12,14},{14,12},{16,18},{18,... | collective-permute-start | bytes 3538952 | tf_op jit(solution)/shard_map/ppermute | solution.py:408
  262.7 21.6 %collective-permute-start.32 = (bf16[384,384]{1,0:T(8,128)(2,1)}, bf16[384,384]{1,0:T(8,128)(2,1)}, u32[]{:S(2)}, u32[]{:S(2)}) collective-permute-start(bf16[384,384]{1,0:T(8,128)(2,1)} %constant_dynamic-slice_fusion.12), channel_id=1, source_target_pairs={{0,2},{2,0},{4,6},{6,4},{8,10},{10,8},{12,14},{14,12},{16,18},{18,... | collective-permute-start | bytes 884744 | tf_op jit(solution)/shard_map/ppermute | solution.py:408
  263.0 30.6 %collective-permute-start.31 = (bf16[384,384]{1,0:T(8,128)(2,1)}, bf16[384,384]{1,0:T(8,128)(2,1)}, u32[]{:S(2)}, u32[]{:S(2)}) collective-permute-start(bf16[384,384]{1,0:T(8,128)(2,1)} %constant_dynamic-slice_fusion.13), channel_id=1, source_target_pairs={{0,2},{2,0},{4,6},{6,4},{8,10},{10,8},{12,14},{14,12},{16,18},{18,... | collective-permute-start | bytes 884744 | tf_op jit(solution)/shard_map/ppermute | solution.py:408
  268.8 42.1 %collective-permute-start.12 = (bf16[2,768,192]{1,2,0:T(8,128)(2,1)}, bf16[2,768,192]{1,2,0:T(8,128)(2,1)}, u32[]{:S(2)}, u32[]{:S(2)}) collective-permute-start(bf16[2,768,192]{1,2,0:T(8,128)(2,1)} %pad_maximum_fusion.17), channel_id=1, source_target_pairs={{0,1},{1,0},{2,3},{3,2},{4,5},{5,4},{6,7},{7,6},{8,9},{9,8},{10,11... | collective-permute-start | bytes 1769480 | tf_op jit(solution)/shard_map/ppermute | solution.py:453
  279.1 39.5 %collective-permute-start.11 = (bf16[512,768]{1,0:T(8,128)(2,1)}, bf16[512,768]{1,0:T(8,128)(2,1)}, u32[]{:S(2)}, u32[]{:S(2)}) collective-permute-start(bf16[512,768]{1,0:T(8,128)(2,1)} %add_convert_fusion.7), channel_id=1, source_target_pairs={{1,0},{3,2},{5,4},{7,6},{9,8},{11,10},{13,12},{15,14},{17,16},{19,... | collective-permute-start | bytes 2359304 | tf_op jit(solution)/shard_map/ppermute | solution.py:612
  286.1 21.7 %collective-permute-start.33 = (bf16[384,384]{1,0:T(8,128)(2,1)}, bf16[384,384]{1,0:T(8,128)(2,1)}, u32[]{:S(2)}, u32[]{:S(2)}) collective-permute-start(bf16[384,384]{1,0:T(8,128)(2,1)} %add_convert_fusion.14), channel_id=1, source_target_pairs={{0,1},{1,0},{2,3},{3,2},{4,5},{5,4},{6,7},{7,6},{8,9},{9,8},{10,11... | collective-permute-start | bytes 884744 | tf_op jit(solution)/shard_map/ppermute | solution.py:453
  293.7 30.9 %collective-permute-start.14 = (bf16[384,960]{0,1:T(8,128)(2,1)}, bf16[384,960]{0,1:T(8,128)(2,1)}, u32[]{:S(2)}, u32[]{:S(2)}) collective-permute-start(bf16[384,960]{0,1:T(8,128)(2,1)} %constant_dynamic-slice_fusion.18), channel_id=1, source_target_pairs={{0,2},{2,0},{4,6},{6,4},{8,10},{10,8},{12,14},{14,12},{16,18},{18,... | collective-permute-start | bytes 2211848 | tf_op jit(solution)/shard_map/ppermute | solution.py:408
  328.5 29.4 %collective-permute-start.13 = (bf16[384,960]{0,1:T(8,128)(2,1)}, bf16[384,960]{0,1:T(8,128)(2,1)S(1)}, u32[]{:S(2)}, u32[]{:S(2)}) collective-permute-start(bf16[384,960]{0,1:T(8,128)(2,1)} %constant_dynamic-slice_fusion.19), channel_id=1, source_target_pairs={{0,2},{2,0},{4,6},{6,4},{8,10},{10,8},{12,14},{14,12},{16,18},{18,... | collective-permute-start | bytes 2211848 | tf_op jit(solution)/shard_map/ppermute | solution.py:408
  337.7 20.9 %collective-permute-start.15 = (bf16[384,960]{0,1:T(8,128)(2,1)}, bf16[384,960]{0,1:T(8,128)(2,1)S(1)}, u32[]{:S(2)}, u32[]{:S(2)}) collective-permute-start(bf16[384,960]{0,1:T(8,128)(2,1)} %add_convert_fusion.9), channel_id=1, source_target_pairs={{0,1},{1,0},{2,3},{3,2},{4,5},{5,4},{6,7},{7,6},{8,9},{9,8},{10,11... | collective-permute-start | bytes 2211848 | tf_op jit(solution)/shard_map/ppermute | solution.py:453
  357.9 58.3 %collective-permute-start.43 = (bf16[768,768]{1,0:T(8,128)(2,1)S(1)}, bf16[768,768]{1,0:T(8,128)(2,1)S(1)}, u32[]{:S(2)}, u32[]{:S(2)}) collective-permute-start(bf16[768,768]{1,0:T(8,128)(2,1)S(1)} %copy-done.79), channel_id=1, source_target_pairs={{0,2},{2,0},{4,6},{6,4},{8,10},{10,8},{12,14},{14,12},{16,18},{18,... | collective-permute-start | bytes 3538952 | tf_op jit(solution)/shard_map/ppermute | solution.py:408
  358.0 45.1 %collective-permute-start.55 = (bf16[768,768]{1,0:T(8,128)(2,1)S(1)}, bf16[768,768]{1,0:T(8,128)(2,1)S(1)}, u32[]{:S(2)}, u32[]{:S(2)}) collective-permute-start(bf16[768,768]{1,0:T(8,128)(2,1)S(1)} %copy-done.80), channel_id=1, source_target_pairs={{0,2},{2,0},{4,6},{6,4},{8,10},{10,8},{12,14},{14,12},{16,18},{18,... | collective-permute-start | bytes 3538952 | tf_op jit(solution)/shard_map/ppermute | solution.py:408
  358.5 17.8 %collective-permute-start.41 = (bf16[192,384]{1,0:T(8,128)(2,1)S(1)}, bf16[192,384]{1,0:T(8,128)(2,1)S(1)}, u32[]{:S(2)}, u32[]{:S(2)}) collective-permute-start(bf16[192,384]{1,0:T(8,128)(2,1)S(1)} %pad_maximum_fusion.28), channel_id=1, source_target_pairs={{0,4},{2,6},{4,0},{6,2},{8,12},{10,14},{12,8},{14,10},{16,20},{18,... | collective-permute-start | bytes 442376 | tf_op jit(solution)/shard_map/ppermute | solution.py:415
  362.9 53.9 %collective-permute-start.45 = (bf16[768,768]{1,0:T(8,128)(2,1)S(1)}, bf16[768,768]{1,0:T(8,128)(2,1)S(1)}, u32[]{:S(2)}, u32[]{:S(2)}) collective-permute-start(bf16[768,768]{1,0:T(8,128)(2,1)S(1)} %add_convert_fusion.5), channel_id=1, source_target_pairs={{0,1},{1,0},{2,3},{3,2},{4,5},{5,4},{6,7},{7,6},{8,9},{9,8},{10,11... | collective-permute-start | bytes 3538952 | tf_op jit(solution)/shard_map/ppermute | solution.py:453
  374.9 40.7 %collective-permute-start.57 = (bf16[768,768]{1,0:T(8,128)(2,1)S(1)}, bf16[768,768]{1,0:T(8,128)(2,1)S(1)}, u32[]{:S(2)}, u32[]{:S(2)}) collective-permute-start(bf16[768,768]{1,0:T(8,128)(2,1)S(1)} %add_convert_fusion.3), channel_id=1, source_target_pairs={{0,1},{1,0},{2,3},{3,2},{4,5},{5,4},{6,7},{7,6},{8,9},{9,8},{10,11... | collective-permute-start | bytes 3538952 | tf_op jit(solution)/shard_map/ppermute | solution.py:453
  402.9 95.8 %collective-permute-start.42 = (bf16[384,384]{1,0:T(8,128)(2,1)S(1)}, bf16[384,384]{1,0:T(8,128)(2,1)S(1)}, u32[]{:S(2)}, u32[]{:S(2)}) collective-permute-start(bf16[384,384]{1,0:T(8,128)(2,1)S(1)} %pad_maximum_fusion.27), channel_id=1, source_target_pairs={{0,2},{2,0},{4,6},{6,4},{8,10},{10,8},{12,14},{14,12},{16,18},{18,... | collective-permute-start | bytes 884744 | tf_op jit(solution)/shard_map/ppermute | solution.py:408
  403.1 15.7 %collective-permute-start.22 = (bf16[48,960]{0,1:T(8,128)(2,1)S(1)}, bf16[48,960]{0,1:T(8,128)(2,1)S(1)}, u32[]{:S(2)}, u32[]{:S(2)}) collective-permute-start(bf16[48,960]{0,1:T(8,128)(2,1)S(1)} %add_convert_fusion.15), channel_id=1, source_target_pairs={{0,24},{2,26},{4,28},{6,30},{8,0},{10,2},{12,4},{14,6},{16,8},{18,... | collective-permute-start | bytes 276488 | tf_op jit(solution)/shard_map/ppermute | solution.py:415
  416.8 16.6 %collective-permute-start.58 = (bf16[384,768]{1,0:T(8,128)(2,1)S(1)}, bf16[384,768]{1,0:T(8,128)(2,1)S(1)}, u32[]{:S(2)}, u32[]{:S(2)}) collective-permute-start(bf16[384,768]{1,0:T(8,128)(2,1)S(1)} %constant_dynamic-slice_fusion.3), channel_id=1, source_target_pairs={{0,4},{2,6},{4,0},{6,2},{8,12},{10,14},{12,8},{14,10},{16,20},{18,... | collective-permute-start | bytes 1769480 | tf_op jit(solution)/shard_map/ppermute | solution.py:415
  418.8 26.9 %collective-permute-start.46 = (bf16[384,768]{1,0:T(8,128)(2,1)S(1)}, bf16[384,768]{1,0:T(8,128)(2,1)S(1)}, u32[]{:S(2)}, u32[]{:S(2)}) collective-permute-start(bf16[384,768]{1,0:T(8,128)(2,1)S(1)} %constant_dynamic-slice_fusion.7), channel_id=1, source_target_pairs={{0,4},{2,6},{4,0},{6,2},{8,12},{10,14},{12,8},{14,10},{16,20},{18,... | collective-permute-start | bytes 1769480 | tf_op jit(solution)/shard_map/ppermute | solution.py:415
  431.8 51.4 %collective-permute-start.23 = (bf16[192,960]{0,1:T(8,128)(2,1)S(1)}, bf16[192,960]{0,1:T(8,128)(2,1)S(1)}, u32[]{:S(2)}, u32[]{:S(2)}) collective-permute-start(bf16[192,960]{0,1:T(8,128)(2,1)S(1)} %pad_maximum_fusion.20), channel_id=1, source_target_pairs={{0,4},{2,6},{4,0},{6,2},{8,12},{10,14},{12,8},{14,10},{16,20},{18,... | collective-permute-start | bytes 1105928 | tf_op jit(solution)/shard_map/ppermute | solution.py:415
  462.4 20.5 %collective-permute-start.63 = (bf16[96,768]{1,0:T(8,128)(2,1)S(1)}, bf16[96,768]{1,0:T(8,128)(2,1)S(1)}, u32[]{:S(2)}, u32[]{:S(2)}) collective-permute-start(bf16[96,768]{1,0:T(8,128)(2,1)S(1)} %add_convert_fusion.16), channel_id=1, source_target_pairs={{0,16},{2,18},{4,20},{6,22},{8,24},{10,26},{12,28},{14,30},{16,0},... | collective-permute-start | bytes 442376 | tf_op jit(solution)/shard_map/ppermute | solution.py:415
  485.6 21.8 %collective-permute-start.24 = (bf16[384,960]{0,1:T(8,128)(2,1)S(1)}, bf16[384,960]{0,1:T(8,128)(2,1)S(1)}, u32[]{:S(2)}, u32[]{:S(2)}) collective-permute-start(bf16[384,960]{0,1:T(8,128)(2,1)S(1)} %pad_maximum_fusion.13), channel_id=1, source_target_pairs={{0,2},{2,0},{4,6},{6,4},{8,10},{10,8},{12,14},{14,12},{16,18},{18,... | collective-permute-start | bytes 2211848 | tf_op jit(solution)/shard_map/ppermute | solution.py:408
  498.7 16.8 %collective-permute-start.66 = (bf16[768,768]{1,0:T(8,128)(2,1)}, bf16[768,768]{1,0:T(8,128)(2,1)}, u32[]{:S(2)}, u32[]{:S(2)}) collective-permute-start(bf16[768,768]{1,0:T(8,128)(2,1)} %pad_maximum_fusion.9), channel_id=1, source_target_pairs={{0,2},{2,0},{4,6},{6,4},{8,10},{10,8},{12,14},{14,12},{16,18},{18,... | collective-permute-start | bytes 3538952 | tf_op jit(solution)/shard_map/ppermute | solution.py:408
  (121 other events, 847.0 us)

commit v2 on v1

v2 whole, which is shorter than its diff:
```python
import functools
import itertools

import jax
import jax.numpy as jnp
from jax import lax
from jax.experimental import pallas as pl
from jax.experimental.pallas import tpu as pltpu
from jax.sharding import PartitionSpec as P

DH = 64
BF = jnp.bfloat16
F32 = jnp.float32
SPAN = 256
QB = 128
WIN = SPAN + QB
TH = 256
RC = 256
NEG = -1000000000.0
COST = pl.CostEstimate(flops=1 << 20, bytes_accessed=1 << 20, transcendentals=0)


def dot_nn(a, b):
    return lax.dot_general(a, b, (((1,), (0,)), ((), ())), preferred_element_type=F32)


def dot_nt(a, b):
    return lax.dot_general(a, b, (((1,), (1,)), ((), ())), preferred_element_type=F32)


def dot_tn(a, b):
    return lax.dot_general(a, b, (((0,), (0,)), ((), ())), preferred_element_type=F32)


def split_pair(block, low_lane):
    zero = jnp.zeros_like(block)
    return jnp.concatenate(
        [jnp.where(low_lane, block, zero), jnp.where(low_lane, zero, block)], axis=0
    )


def window_bias(kseg_ref, qseg_ref, start):
    key_at = lax.broadcasted_iota(jnp.int32, (WIN, QB), 0)
    query_at = lax.broadcasted_iota(jnp.int32, (WIN, QB), 1) + SPAN
    kseg = kseg_ref[0, start : start + WIN, :]
    qseg = qseg_ref[0, :, start : start + QB]
    allowed = ((kseg == qseg) & (key_at <= query_at)) | (key_at == query_at)
    bias = jnp.where(allowed, 0.0, NEG).astype(F32)
    return jnp.concatenate([bias, bias], axis=1)


def pair_values(x_ref, s_ref, t_s, pairs):
    base = 4 * pairs * DH
    for at in range(0, pairs, 2):
        fresh = x_ref[:, base + at * DH : base + at * DH + 128].T
        for pair in range(at, min(at + 2, pairs)):
            t_s[pair, :DH, :] = fresh[(pair - at) * DH : (pair - at + 1) * DH, :]
            t_s[pair, DH:, :] = s_ref[pair * DH : (pair + 1) * DH, :]


def attend_forward_kernel(pairs, x_ref, s_ref, kseg_ref, qseg_ref, o_ref, lse_ref, t_s):
    o_blocks = o_ref.shape[0] // QB
    pair_values(x_ref, s_ref, t_s, pairs)

    low = lax.broadcasted_iota(jnp.int32, (QB, 128), 1) < DH
    for block, pair in itertools.product(range(o_blocks), range(pairs)):
        start = block * QB
        if pair == 0:
            bias = window_bias(kseg_ref, qseg_ref, start)
        win = slice(start, start + WIN)
        rows = slice(start + SPAN, start + SPAN + QB)
        here = slice(start, start + QB)
        cols = slice(pair * 128, pair * 128 + 128)
        key_cols = slice((pairs + pair) * 128, (pairs + pair) * 128 + 128)
        queries = split_pair(x_ref[rows, cols], low)
        scores = dot_nt(x_ref[win, key_cols], queries) + bias
        largest = jnp.max(scores, axis=0, keepdims=True)
        expon = jnp.exp(scores - largest)
        total = jnp.sum(expon, axis=0, keepdims=True)
        probs = (expon * (1.0 / total)).astype(BF)
        out = dot_nn(t_s[pair, :, win], probs)
        out = jnp.concatenate([out[:DH, :QB], out[DH:, QB:]], axis=0)
        o_ref[here, cols] = out.T.astype(BF)
        lse_ref[0, block, pair : pair + 1, :] = largest + jnp.log(total)


def attend_backward_kernel(
    pairs, x_ref, s_ref, kseg_ref, qseg_ref, lse_ref, g_ref, dx_ref, ds_ref, v_s, t_s, dk_s, dv_s
):
    o_blocks = g_ref.shape[0] // QB
    pair_values(x_ref, s_ref, t_s, pairs)
    for pair in range(pairs):
        v_s[pair] = t_s[pair].T
        key_cols = slice((pairs + pair) * 128, (pairs + pair) * 128 + 128)
        t_s[pair] = x_ref[:, key_cols].T
    dk_s[...] = jnp.zeros_like(dk_s)
    dv_s[...] = jnp.zeros_like(dv_s)
    dx_ref[:SPAN, : pairs * 128] = jnp.zeros((SPAN, pairs * 128), BF)

    low = lax.broadcasted_iota(jnp.int32, (QB, 128), 1) < DH
    for block, pair in itertools.product(range(o_blocks), range(pairs)):
        start = block * QB
        if pair == 0:
            bias = window_bias(kseg_ref, qseg_ref, start)
        win = slice(start, start + WIN)
        rows = slice(start + SPAN, start + SPAN + QB)
        here = slice(start, start + QB)
        cols = slice(pair * 128, pair * 128 + 128)
        key_cols = slice((pairs + pair) * 128, (pairs + pair) * 128 + 128)
        queries = split_pair(x_ref[rows, cols], low)
        grads = split_pair(g_ref[here, cols], low)
        scores = dot_nt(x_ref[win, key_cols], queries) + bias
        probs = jnp.exp(scores - lse_ref[0, block, pair : pair + 1, :])
        prob_grad = dot_nt(v_s[pair, win], grads)
        row_total = jnp.sum(probs * prob_grad, axis=0, keepdims=True)
        score_grad = (probs * (prob_grad - row_total)).astype(BF)
        dv_s[pair, win] += dot_nn(probs.astype(BF), grads)
        dk_s[pair, win] += dot_nn(score_grad, queries)
        out = dot_nn(t_s[pair, :, win], score_grad)
        out = jnp.concatenate([out[:DH, :QB], out[DH:, QB:]], axis=0)
        dx_ref[rows, cols] = (out.T * (DH**-0.5)).astype(BF)

    base = 4 * pairs * DH
    low_all = lax.broadcasted_iota(jnp.int32, (x_ref.shape[0], 128), 1) < DH
    for pair in range(pairs):
        key_cols = slice((pairs + pair) * 128, (pairs + pair) * 128 + 128)
        dx_ref[:, key_cols] = dk_s[pair].astype(BF)
        ds_ref[pair * DH : (pair + 1) * DH, :] = dv_s[pair].astype(BF).T[DH:, :]
    for at in range(0, pairs, 2):
        second = pltpu.roll(dv_s[at + 1], DH, 1) if at + 1 < pairs else jnp.zeros_like(dv_s[at])
        dx_ref[:, base + at * DH : base + at * DH + 128] = jnp.where(
            low_all, dv_s[at], second
        ).astype(BF)


def attention_specs(rows, blocks, columns, pairs):
    extended = SPAN + blocks * QB
    x_spec = pl.BlockSpec((extended, columns), lambda r: (r, 0))
    s_spec = pl.BlockSpec((pairs * DH, extended), lambda r: (r, 0))
    kseg_spec = pl.BlockSpec((1, extended, 1), lambda r: (r, 0, 0))
    qseg_spec = pl.BlockSpec((1, 1, blocks * QB), lambda r: (r, 0, 0))
    o_spec = pl.BlockSpec((blocks * QB, pairs * 128), lambda r: (r, 0))
    lse_spec = pl.BlockSpec((1, blocks, pairs, 2 * QB), lambda r: (r, 0, 0, 0))
    return extended, x_spec, s_spec, kseg_spec, qseg_spec, o_spec, lse_spec


def attend_forward(extended_qkv, skip, kseg, qseg):
    rows, blocks, pairs = qseg.shape[0], qseg.shape[2] // QB, skip.shape[0] // DH // qseg.shape[0]
    columns = extended_qkv.shape[1]
    extended, x_spec, s_spec, kseg_spec, qseg_spec, o_spec, lse_spec = attention_specs(
        rows, blocks, columns, pairs
    )
    return pl.pallas_call(
        functools.partial(attend_forward_kernel, pairs),
        grid=(rows,),
        in_specs=[x_spec, s_spec, kseg_spec, qseg_spec],
        out_specs=[o_spec, lse_spec],
        out_shape=[
            jax.ShapeDtypeStruct((rows * blocks * QB, pairs * 128), BF),
            jax.ShapeDtypeStruct((rows, blocks, pairs, 2 * QB), F32),
        ],
        scratch_shapes=[
            pltpu.VMEM((pairs, 128, extended), BF),
        ],
        cost_estimate=COST,
        name="attend_forward",
    )(extended_qkv, skip, kseg, qseg)


def attend_backward(extended_qkv, skip, kseg, qseg, sums, grads):
    rows, blocks, pairs = qseg.shape[0], qseg.shape[2] // QB, skip.shape[0] // DH // qseg.shape[0]
    columns = extended_qkv.shape[1]
    extended, x_spec, s_spec, kseg_spec, qseg_spec, o_spec, lse_spec = attention_specs(
        rows, blocks, columns, pairs
    )
    return pl.pallas_call(
        functools.partial(attend_backward_kernel, pairs),
        grid=(rows,),
        in_specs=[x_spec, s_spec, kseg_spec, qseg_spec, lse_spec, o_spec],
        out_specs=[x_spec, s_spec],
        out_shape=[
            jax.ShapeDtypeStruct((rows * extended, columns), BF),
            jax.ShapeDtypeStruct((rows * pairs * DH, extended), BF),
        ],
        scratch_shapes=[
            pltpu.VMEM((pairs, extended, 128), BF),
            pltpu.VMEM((pairs, 128, extended), BF),
            pltpu.VMEM((pairs, extended, 128), F32),
            pltpu.VMEM((pairs, extended, 128), F32),
        ],
        cost_estimate=COST,
        name="attend_backward",
    )(extended_qkv, skip, kseg, qseg, sums, grads)


def feed_kernel(
    core_ref,
    n_ref,
    g_ref,
    ua_ref,
    ub_ref,
    ba_ref,
    bb_ref,
    da_ref,
    db_ref,
    wua_ref,
    wub_ref,
    wda_ref,
    wdb_ref,
    ga_ref,
    gb_ref,
    down_ref,
    second_ref,
    turned_s,
    act_s,
    upg_s,
):
    step = pl.program_id(0)
    half = pl.num_programs(0) // 2
    first = step < half

    @pl.when(step == 0)
    def _():
        turned_s[...] = n_ref[...].T
        down_ref[...] = jnp.zeros_like(down_ref)
        second_ref[...] = jnp.zeros_like(second_ref)

    up_tile = jnp.where(first, ua_ref[...], ub_ref[...])
    down_tile = jnp.where(first, da_ref[...], db_ref[...])
    bias = jnp.where(first, ba_ref[...], bb_ref[...])
    root = 0.7978845608028654
    for start in range(0, n_ref.shape[0], RC):
        rows = slice(start, start + RC)
        upward = dot_nn(n_ref[rows, :], up_tile) + bias
        act_grad = dot_nt(g_ref[rows, :], down_tile)
        square = upward * upward
        bent = jnp.tanh(root * upward * (1.0 + 0.044715 * square))
        gate = 0.5 * (1.0 + bent)
        slope = gate + 0.5 * root * upward * (1.0 - bent * bent) * (1.0 + 0.134145 * square)
        act = (upward * gate).astype(BF)
        upg = (act_grad * slope).astype(BF)
        act_s[rows, :] = act
        upg_s[rows, :] = upg
        down_ref[rows, :] += dot_nn(act, down_tile)
        second_ref[rows, :] += dot_nt(upg, up_tile)
    up_weight_grad = dot_nn(turned_s[...], upg_s[...]).astype(BF)
    down_weight_grad = dot_tn(act_s[...], g_ref[...]).astype(BF)
    bias_grad = jnp.sum(upg_s[...].astype(F32), axis=0, keepdims=True)

    @pl.when(first)
    def _():
        wua_ref[...] = up_weight_grad
        wda_ref[...] = down_weight_grad
        ga_ref[...] = bias_grad

    @pl.when(jnp.logical_not(first))
    def _():
        wub_ref[...] = up_weight_grad
        wdb_ref[...] = down_weight_grad
        gb_ref[...] = bias_grad


def feed(at, normed, grads, up_a, up_b, bias, down_a, down_b, whole):
    tokens, width = normed.shape
    piece = up_a.shape[1] // 2 if whole else up_a.shape[1]
    tiles = piece // TH

    def a_at(i, c):
        at = jnp.minimum(i, tiles - 1)
        return at + (1 - c[0]) * tiles if whole else at

    def b_at(i, c):
        at = jnp.maximum(i - tiles, 0)
        return at + c[0] * tiles if whole else at

    def out_a(i, c):
        return jnp.minimum(i, tiles - 1)

    def out_b(i, c):
        return jnp.maximum(i - tiles, 0)

    resident = pl.BlockSpec((tokens, width), lambda i, c: (0, 0))
    once = pl.BlockSpec((tokens, width), lambda i, c: (0, 0))
    in_specs = [
        resident,
        resident,
        pl.BlockSpec((width, TH), lambda i, c: (0, a_at(i, c))),
        pl.BlockSpec((width, TH), lambda i, c: (0, b_at(i, c))),
        pl.BlockSpec((1, TH), lambda i, c: (0, out_a(i, c) + (1 - c[0]) * tiles)),
        pl.BlockSpec((1, TH), lambda i, c: (0, out_b(i, c) + c[0] * tiles)),
        pl.BlockSpec((TH, width), lambda i, c: (a_at(i, c), 0)),
        pl.BlockSpec((TH, width), lambda i, c: (b_at(i, c), 0)),
    ]
    out_specs = [
        pl.BlockSpec((width, TH), lambda i, c: (0, out_a(i, c))),
        pl.BlockSpec((width, TH), lambda i, c: (0, out_b(i, c))),
        pl.BlockSpec((TH, width), lambda i, c: (out_a(i, c), 0)),
        pl.BlockSpec((TH, width), lambda i, c: (out_b(i, c), 0)),
        pl.BlockSpec((1, TH), lambda i, c: (0, out_a(i, c))),
        pl.BlockSpec((1, TH), lambda i, c: (0, out_b(i, c))),
        once,
        once,
    ]
    out_shape = [
        jax.ShapeDtypeStruct((width, piece), BF),
        jax.ShapeDtypeStruct((width, piece), BF),
        jax.ShapeDtypeStruct((piece, width), BF),
        jax.ShapeDtypeStruct((piece, width), BF),
        jax.ShapeDtypeStruct((1, piece), F32),
        jax.ShapeDtypeStruct((1, piece), F32),
        jax.ShapeDtypeStruct((tokens, width), F32),
        jax.ShapeDtypeStruct((tokens, width), F32),
    ]
    return pl.pallas_call(
        feed_kernel,
        grid_spec=pltpu.PrefetchScalarGridSpec(
            num_scalar_prefetch=1,
            grid=(2 * tiles,),
            in_specs=in_specs,
            out_specs=out_specs,
            scratch_shapes=[
                pltpu.VMEM((width, tokens), BF),
                pltpu.VMEM((tokens, TH), BF),
                pltpu.VMEM((tokens, TH), BF),
            ],
        ),
        out_shape=out_shape,
        compiler_params=pltpu.CompilerParams(vmem_limit_bytes=56 << 20),
        cost_estimate=COST,
        name="feed",
    )(at, normed, grads, up_a, up_b, bias, bias, down_a, down_b)


def norm_rows(values, gain_row, shift_row):
    center = values - jnp.mean(values, axis=-1, keepdims=True)
    variance = jnp.mean(center * center, axis=-1, keepdims=True)
    return center * lax.rsqrt(variance + 1e-05) * gain_row + shift_row


def whole_spec(value):
    zeros = (0,) * value.ndim
    return pl.BlockSpec(value.shape, lambda *_: zeros)


def open_kernel(
    at_ref, qw_ref, kw_ref, vw_ref, x_ref, s_ref, w_ref, w_send_ref, halo_ref, s_send_ref, s_own_ref
):
    side = at_ref[1]
    rows, length, width = x_ref.shape
    local, half = qw_ref.shape[1], vw_ref.shape[0]
    depth = w_send_ref.shape[0]
    cut = pl.ds(pl.multiple_of(at_ref[2] * depth, depth), depth)
    w_ref[:, :local] = qw_ref[...]
    w_ref[:, local : 2 * local] = kw_ref[...]
    w_ref[:, 2 * local : 2 * local + half] = vw_ref[...].T
    w_ref[:, 2 * local + half :] = jnp.zeros((width, w_ref.shape[1] - 2 * local - half), BF)
    w_send_ref[...] = w_ref[cut, :]
    own = pl.ds(pl.multiple_of(side * length, length), length)
    other = pl.ds(pl.multiple_of((1 - side) * length, length), length)
    for row in range(rows):
        halo_ref[row * SPAN : (row + 1) * SPAN, :] = x_ref[row, length - SPAN :, :]
        lines = slice(row * half, (row + 1) * half)
        middle = s_ref[row, :, length - SPAN : length]
        s_send_ref[lines, :SPAN] = middle
        s_own_ref[lines, :SPAN] = middle
        s_send_ref[lines, SPAN:] = s_ref[row, :, other]
        s_own_ref[lines, SPAN:] = s_ref[row, :, own]


def open_step(at, qw, kw, vw, x, skip):
    rows, length, width = x.shape
    local, half = qw.shape[1], vw.shape[0]
    columns = -(-(2 * local + half) // 256) * 256
    shapes = [
        (width, columns),
        (width // 4, columns),
        (rows * SPAN, width),
        (rows * half, SPAN + length),
        (rows * half, SPAN + length),
    ]
    return pl.pallas_call(
        open_kernel,
        grid_spec=pltpu.PrefetchScalarGridSpec(
            num_scalar_prefetch=1,
            grid=(1,),
            in_specs=[whole_spec(v) for v in (qw, kw, vw, x, skip)],
            out_specs=[pl.BlockSpec(shape, lambda *_: (0, 0)) for shape in shapes],
        ),
        out_shape=[jax.ShapeDtypeStruct(shape, BF) for shape in shapes],
        cost_estimate=COST,
        name="open",
    )(at, qw, kw, vw, x, skip)


class Rows:
    def __init__(self, width, local, hidden):
        half = local // 2
        self.up = slice(0, hidden)
        self.query = slice(hidden, hidden + local)
        self.value = slice(hidden + local, hidden + local + half)
        start = -(-self.value.stop // 128) * 128
        self.pad = start - self.value.stop
        self.gain_1, self.shift_1, self.gain_2, self.shift_2, self.out, self.down = (
            slice(start + n * width, start + (n + 1) * width) for n in range(6)
        )
        self.size = start + 6 * width


def store_projection(o_ref, values, q_bias, v_bias):
    local, half = q_bias.shape[1], v_bias.shape[1]
    o_ref[:, :local] = ((values[:, :local] + q_bias) * (DH**-0.5)).astype(BF)
    o_ref[:, local : 2 * local] = values[:, local : 2 * local].astype(BF)
    stop = 2 * local + half
    o_ref[:, 2 * local : stop] = (values[:, 2 * local : stop] + v_bias).astype(BF)
    o_ref[:, stop:] = values[:, stop:].astype(BF)


def project_own_kernel(where, n_ref, h_ref, rows_ref, w_ref, ne_ref, o_ref):
    @pl.when(pl.program_id(1) == 0)
    def _():
        ne_ref[...] = norm_rows(
            h_ref[...].astype(F32), rows_ref[:, where.gain_1], rows_ref[:, where.shift_1]
        ).astype(BF)

    @pl.when(pl.program_id(1) > 0)
    def _():
        ne_ref[...] = n_ref[...]

    store_projection(
        o_ref, dot_nn(ne_ref[...], w_ref[...]), rows_ref[:, where.query], rows_ref[:, where.value]
    )


def project_own(where, normed, halo, row_vectors, weight, rows):
    width, columns = weight.shape
    blocks = normed.shape[0] // SPAN // rows
    extended = lambda cols: pl.BlockSpec((SPAN, cols), lambda r, j: (r * (blocks + 1) + j, 0))
    size = rows * (blocks + 1) * SPAN
    return pl.pallas_call(
        functools.partial(project_own_kernel, where),
        grid=(rows, blocks + 1),
        in_specs=[
            pl.BlockSpec((SPAN, width), lambda r, j: (r * blocks + jnp.maximum(j - 1, 0), 0)),
            pl.BlockSpec((SPAN, width), lambda r, j: (r, 0)),
            whole_spec(row_vectors),
            whole_spec(weight),
        ],
        out_specs=[extended(width), extended(columns)],
        out_shape=[
            jax.ShapeDtypeStruct((size, width), BF),
            jax.ShapeDtypeStruct((size, columns), BF),
        ],
        cost_estimate=COST,
        name="project_own",
    )(normed, halo, row_vectors, weight)


def join_cores(at_ref, mine_ref, other_ref, scratch):
    depth = mine_ref.shape[0]
    core = at_ref[0]
    scratch[pl.ds(pl.multiple_of(core * depth, depth), depth), :] = mine_ref[...]
    scratch[pl.ds(pl.multiple_of((1 - core) * depth, depth), depth), :] = other_ref[...]


def project_other_kernel(where, at_ref, ne_ref, mine_ref, other_ref, rows_ref, o_ref, w_s):
    @pl.when(pl.program_id(0) == 0)
    def _():
        join_cores(at_ref, mine_ref, other_ref, w_s)

    store_projection(
        o_ref, dot_nn(ne_ref[...], w_s[...]), rows_ref[:, where.query], rows_ref[:, where.value]
    )


def project_other(where, at, normed_ext, mine, other, row_vectors):
    size, width = normed_ext.shape
    columns = mine.shape[1]
    return pl.pallas_call(
        functools.partial(project_other_kernel, where),
        grid_spec=pltpu.PrefetchScalarGridSpec(
            num_scalar_prefetch=1,
            grid=(size // SPAN,),
            in_specs=[
                pl.BlockSpec((SPAN, width), lambda i, a: (i, 0)),
                *[whole_spec(v) for v in (mine, other, row_vectors)],
            ],
            out_specs=pl.BlockSpec((SPAN, columns), lambda i, a: (i, 0)),
            scratch_shapes=[pltpu.VMEM((width, columns), BF)],
        ),
        out_shape=jax.ShapeDtypeStruct((size, columns), BF),
        cost_estimate=COST,
        name="project_other",
    )(at, normed_ext, mine, other, row_vectors)


def middle_kernel(
    where, at_ref, ml_ref, mr_ref, wl_ref, w1_ref, w2_ref, x_ref, rows_ref, hidden_ref, n_ref, wr_ref
):
    @pl.when(pl.program_id(0) == 0)
    def _():
        join_cores(at_ref, w1_ref, w2_ref, wr_ref)

    values = dot_nn(ml_ref[...], wl_ref[...]) + dot_nn(mr_ref[...], wr_ref[...])
    hidden = x_ref[...].astype(F32) + (values + rows_ref[:, where.out])
    hidden_ref[...] = hidden
    n_ref[...] = norm_rows(hidden, rows_ref[:, where.gain_2], rows_ref[:, where.shift_2]).astype(BF)


def middle(where, at, mixed_l, mixed_r, own, mine, other, x, row_vectors):
    tokens, width = x.shape
    local = mixed_l.shape[1]
    tile = lambda columns: pl.BlockSpec((RC, columns), lambda i, a: (i, 0))
    return pl.pallas_call(
        functools.partial(middle_kernel, where),
        grid_spec=pltpu.PrefetchScalarGridSpec(
            num_scalar_prefetch=1,
            grid=(tokens // RC,),
            in_specs=[
                tile(local), tile(local), *[whole_spec(v) for v in (own, mine, other)],
                tile(width), whole_spec(row_vectors),
            ],
            out_specs=[tile(width), tile(width), whole_spec(own)],
        ),
        out_shape=[
            jax.ShapeDtypeStruct((tokens, width), F32),
            jax.ShapeDtypeStruct((tokens, width), BF),
            jax.ShapeDtypeStruct(own.shape, BF),
        ],
        cost_estimate=COST,
        name="middle",
    )(at, mixed_l, mixed_r, own, mine, other, x, row_vectors)


def norm_pull(values, grad, gain_row):
    center = values - jnp.mean(values, axis=-1, keepdims=True)
    variance = jnp.mean(center * center, axis=-1, keepdims=True)
    rstd = lax.rsqrt(variance + 1e-05)
    unit = center * rstd
    scaled = grad * gain_row
    back = rstd * (
        scaled
        - jnp.mean(scaled, axis=-1, keepdims=True)
        - unit * jnp.mean(scaled * unit, axis=-1, keepdims=True)
    )
    return back, grad * unit


def down_rows(values):
    return jnp.sum(values, axis=0, keepdims=True)


def middle_back_kernel(
    where, at_ref, bl_ref, br_ref, hidden_ref, g_ref, ml_ref, mr_ref, wl_ref, wr_ref, rows_ref,
    hg_ref, gl_ref, gr_ref, keep_l_ref, keep_r_ref, send_ref, sums_ref, acc_l, acc_r,
):
    step = pl.program_id(0)

    @pl.when(step == 0)
    def _():
        acc_l[...] = jnp.zeros_like(acc_l)
        acc_r[...] = jnp.zeros_like(acc_r)
        sums_ref[...] = jnp.zeros_like(sums_ref)

    grad = bl_ref[...] + br_ref[...]
    back, gain_term = norm_pull(hidden_ref[...], grad, rows_ref[:, where.gain_2])
    cot = g_ref[...].astype(F32)
    hidden_grad = cot + back
    low = hidden_grad.astype(BF)
    hg_ref[...] = hidden_grad
    gl_ref[...] = dot_nt(low, wl_ref[...]).astype(BF)
    gr_ref[...] = dot_nt(low, wr_ref[...]).astype(BF)
    acc_l[...] += dot_tn(ml_ref[...], low)
    acc_r[...] += dot_tn(mr_ref[...], low)
    for at, term in enumerate((low.astype(F32), cot, gain_term, grad)):
        sums_ref[at : at + 1, :] += down_rows(term)

    @pl.when(step == pl.num_programs(0) - 1)
    def _():
        depth = keep_l_ref.shape[0]
        core = at_ref[0]
        mine = pl.ds(pl.multiple_of(core * depth, depth), depth)
        other = pl.ds(pl.multiple_of((1 - core) * depth, depth), depth)
        keep_l_ref[...] = acc_l[mine, :].astype(BF)
        keep_r_ref[...] = acc_r[mine, :].astype(BF)
        send_ref[:depth, :] = acc_l[other, :].astype(BF)
        send_ref[depth:, :] = acc_r[other, :].astype(BF)


def middle_back(where, at, back_l, back_r, hidden, grads, mixed_l, mixed_r, own, other, row_vectors):
    tokens, width = hidden.shape
    local = mixed_l.shape[1]
    tile = lambda columns: pl.BlockSpec((RC, columns), lambda i, a: (i, 0))
    fixed = lambda rows: pl.BlockSpec((rows, width), lambda i, a: (0, 0))
    return pl.pallas_call(
        functools.partial(middle_back_kernel, where),
        grid_spec=pltpu.PrefetchScalarGridSpec(
            num_scalar_prefetch=1,
            grid=(tokens // RC,),
            in_specs=[
                tile(width), tile(width), tile(width), tile(width), tile(local), tile(local),
                whole_spec(own), whole_spec(other), whole_spec(row_vectors),
            ],
            out_specs=[
                tile(width), tile(local), tile(local),
                fixed(local // 2), fixed(local // 2), fixed(local), fixed(8),
            ],
            scratch_shapes=[pltpu.VMEM((local, width), F32), pltpu.VMEM((local, width), F32)],
        ),
        out_shape=[
            jax.ShapeDtypeStruct((tokens, width), F32),
            jax.ShapeDtypeStruct((tokens, local), BF),
            jax.ShapeDtypeStruct((tokens, local), BF),
            jax.ShapeDtypeStruct((local // 2, width), BF),
            jax.ShapeDtypeStruct((local // 2, width), BF),
            jax.ShapeDtypeStruct((local, width), BF),
            jax.ShapeDtypeStruct((8, width), F32),
        ],
        cost_estimate=COST,
        name="middle_back",
    )(at, back_l, back_r, hidden, grads, mixed_l, mixed_r, own, other, row_vectors)


def project_grad_kernel(at_ref, n_ref, d_ref, keep_ref, send_ref, sum_ref):
    values = dot_tn(n_ref[...], d_ref[...]).astype(BF)

    @pl.when(pl.program_id(0) == 0)
    def _():
        send_ref[...] = values
        sum_ref[...] = down_rows(d_ref[...].astype(F32))

    @pl.when(pl.program_id(0) == 1)
    def _():
        keep_ref[...] = values


def project_grad(at, normed_ext, grads):
    size, width = normed_ext.shape
    columns = grads.shape[1]
    fixed = pl.BlockSpec((width // 2, columns), lambda i, a: (0, 0))
    return pl.pallas_call(
        project_grad_kernel,
        grid_spec=pltpu.PrefetchScalarGridSpec(
            num_scalar_prefetch=1,
            grid=(2,),
            in_specs=[
                pl.BlockSpec((size, width // 2), lambda i, a: (0, i * a[0] + (1 - i) * (1 - a[0]))),
                whole_spec(grads),
            ],
            out_specs=[fixed, fixed, pl.BlockSpec((1, columns), lambda i, a: (0, 0))],
        ),
        out_shape=[
            jax.ShapeDtypeStruct((width // 2, columns), BF),
            jax.ShapeDtypeStruct((width // 2, columns), BF),
            jax.ShapeDtypeStruct((1, columns), F32),
        ],
        cost_estimate=COST,
        name="project_grad",
    )(at, normed_ext, grads)


def first_back_kernel(
    where, at_ref, dl_ref, dr_ref, wl_ref, mine_ref, other_ref, x_ref, h_ref, hg_ref, rows_ref,
    ig_ref, ih_ref, sums_ref, w_s,
):
    block = pl.program_id(1)

    @pl.when((pl.program_id(0) == 0) & (block == 0))
    def _():
        join_cores(at_ref, mine_ref, other_ref, w_s)
        sums_ref[...] = jnp.zeros_like(sums_ref)

    grad = dot_nt(dl_ref[...], wl_ref[...]) + dot_nt(dr_ref[...], w_s[...])
    values = jnp.where(block == 0, h_ref[...], x_ref[...]).astype(F32)
    back, gain_term = norm_pull(values, grad, rows_ref[:, where.gain_1])
    sums_ref[0:1, :] += down_rows(gain_term)
    sums_ref[1:2, :] += down_rows(grad)

    @pl.when(block == 0)
    def _():
        ih_ref[...] = back.astype(BF)

    @pl.when(block > 0)
    def _():
        ig_ref[...] = hg_ref[...] + back


def first_back(where, at, grads_l, grads_r, own, mine, other, x, halo, hidden_grad, row_vectors, rows):
    tokens, width = x.shape
    columns = grads_l.shape[1]
    blocks = tokens // SPAN // rows
    extended = pl.BlockSpec((SPAN, columns), lambda r, j, a: (r * (blocks + 1) + j, 0))
    inner = pl.BlockSpec((SPAN, width), lambda r, j, a: (r * blocks + jnp.maximum(j - 1, 0), 0))
    outer = pl.BlockSpec((SPAN, width), lambda r, j, a: (r, 0))
    return pl.pallas_call(
        functools.partial(first_back_kernel, where),
        grid_spec=pltpu.PrefetchScalarGridSpec(
            num_scalar_prefetch=1,
            grid=(rows, blocks + 1),
            in_specs=[
                extended, extended, *[whole_spec(v) for v in (own, mine, other)],
                inner, outer, inner, whole_spec(row_vectors),
            ],
            out_specs=[inner, outer, pl.BlockSpec((8, width), lambda r, j, a: (0, 0))],
            scratch_shapes=[pltpu.VMEM((width, columns), BF)],
        ),
        out_shape=[
            jax.ShapeDtypeStruct((tokens, width), F32),
            jax.ShapeDtypeStruct((rows * SPAN, width), BF),
            jax.ShapeDtypeStruct((8, width), F32),
        ],
        cost_estimate=COST,
        name="first_back",
    )(at, grads_l, grads_r, own, mine, other, x, halo, hidden_grad, row_vectors)


def add_halo_kernel(ig_ref, got_ref, o_ref):
    o_ref[...] = ig_ref[...] + got_ref[...].astype(F32)


def add_halo(input_grad, got, rows):
    width = got.shape[1]
    blocks = input_grad.shape[0] // SPAN // rows
    last = pl.BlockSpec((SPAN, width), lambda r: (r * blocks + blocks - 1, 0))
    return pl.pallas_call(
        add_halo_kernel,
        grid=(rows,),
        in_specs=[last, pl.BlockSpec((SPAN, width), lambda r: (r, 0))],
        out_specs=last,
        out_shape=jax.ShapeDtypeStruct(input_grad.shape, F32),
        input_output_aliases={0: 0},
        cost_estimate=COST,
        name="add_halo",
    )(input_grad, got)


def skip_grad_kernel(at_ref, mine_ref, got_ref, o_ref):
    side = at_ref[1]
    rows, half, total = o_ref.shape
    length = total // 2
    own = pl.ds(pl.multiple_of(side * length, length), length)
    other = pl.ds(pl.multiple_of((1 - side) * length, length), length)
    for row in range(rows):
        lines = slice(row * half, (row + 1) * half)
        o_ref[row, :, own] = mine_ref[lines, SPAN:].astype(F32)
        o_ref[row, :, other] = got_ref[lines, SPAN:].astype(F32)
        o_ref[row, :, length - SPAN : length] += mine_ref[lines, :SPAN].astype(F32) + got_ref[
            lines, :SPAN
        ].astype(F32)


def skip_grad_of(at, mine, got, rows):
    lines, size = mine.shape
    shape = (rows, lines // rows, 2 * (size - SPAN))
    return pl.pallas_call(
        skip_grad_kernel,
        grid_spec=pltpu.PrefetchScalarGridSpec(
            num_scalar_prefetch=1,
            grid=(1,),
            in_specs=[whole_spec(mine), whole_spec(got)],
            out_specs=pl.BlockSpec(shape, lambda i, a: (0, 0, 0)),
        ),
        out_shape=jax.ShapeDtypeStruct(shape, F32),
        cost_estimate=COST,
        name="skip_grad",
    )(at, mine, got)


def small_kernel(where, at_ref, m_ref, f_ref, ql_ref, qr_ref, l1_ref, l2_ref, r1_ref, r2_ref, own_ref, other_ref):
    core = at_ref[0]
    local = where.query.stop - where.query.start
    half = where.value.stop - where.value.start
    piece = l1_ref.shape[1]
    for o_ref, q_ref, one_ref, two_ref in (
        (own_ref, ql_ref, l1_ref, l2_ref), (other_ref, qr_ref, r1_ref, r2_ref)
    ):
        o_ref[...] = jnp.zeros_like(o_ref)
        o_ref[:, pl.ds(pl.multiple_of(core * piece, 128), piece)] = one_ref[...]
        o_ref[:, pl.ds(pl.multiple_of((1 - core) * piece, 128), piece)] = two_ref[...]
        o_ref[:, where.query] = q_ref[:, :local]
        o_ref[:, where.value] = q_ref[:, 2 * local : 2 * local + half]
        o_ref[:, where.out] = m_ref[0:1, :]
        o_ref[:, where.down] = m_ref[1:2, :]
        o_ref[:, where.gain_2] = m_ref[2:3, :]
        o_ref[:, where.shift_2] = m_ref[3:4, :]
        o_ref[:, where.gain_1] = f_ref[0:1, :]
        o_ref[:, where.shift_1] = f_ref[1:2, :]


def small_step(where, at, *values):
    return pl.pallas_call(
        functools.partial(small_kernel, where),
        grid_spec=pltpu.PrefetchScalarGridSpec(
            num_scalar_prefetch=1,
            grid=(1,),
            in_specs=[whole_spec(v) for v in values],
            out_specs=[pl.BlockSpec((1, where.size), lambda i, a: (0, 0))] * 2,
        ),
        out_shape=[jax.ShapeDtypeStruct((1, where.size), F32)] * 2,
        cost_estimate=COST,
        name="small",
    )(at, *values)


def feed_out_kernel(parts, factor, at_ref, mine_ref, other_ref, up_ref, down_ref, out_ref):
    core = at_ref[0]
    a, b, c = parts
    step = a + b + c
    piece = up_ref.shape[1] // 2
    for ref, at in ((mine_ref, core), (other_ref, 1 - core)):
        lanes = pl.ds(pl.multiple_of(at * piece, 128), piece)
        for digit in range(factor):
            start = digit * step
            up_ref[digit * a : (digit + 1) * a, lanes] = ref[start : start + a, :].astype(F32)
            rows = pl.ds(pl.multiple_of(at * factor * b, 8) + digit * b, b)
            down_ref[rows, :] = ref[start + a : start + a + b, :].astype(F32)
            rows = pl.ds(pl.multiple_of(at * factor * c, 8) + digit * c, c)
            out_ref[rows, :] = ref[start + a + b : start + step, :].astype(F32)


def feed_out(at, mine, other, parts, factor):
    a, b, c = parts
    width = mine.shape[1]
    shapes = [(factor * a, 2 * width), (2 * factor * b, width), (2 * factor * c, width)]
    return pl.pallas_call(
        functools.partial(feed_out_kernel, parts, factor),
        grid_spec=pltpu.PrefetchScalarGridSpec(
            num_scalar_prefetch=1,
            grid=(1,),
            in_specs=[whole_spec(mine), whole_spec(other)],
            out_specs=[pl.BlockSpec(s, lambda i, a: (0, 0)) for s in shapes],
        ),
        out_shape=[jax.ShapeDtypeStruct(s, F32) for s in shapes],
        cost_estimate=COST,
        name="feed_out",
    )(at, mine, other)


def project_out_kernel(at_ref, mine_ref, other_ref, q_ref, k_ref, v_ref):
    core = at_ref[0]
    depth = mine_ref.shape[0]
    local = q_ref.shape[1]
    for ref, at in ((mine_ref, core), (other_ref, 1 - core)):
        rows = pl.ds(pl.multiple_of(at * depth, depth), depth)
        q_ref[rows, :] = ref[:, :local].astype(F32)
        k_ref[rows, :] = ref[:, local : 2 * local].astype(F32)
        v_ref[:, rows] = ref[:, 2 * local : 2 * local + v_ref.shape[0]].astype(F32).T


def project_out(at, mine, other, local):
    depth = mine.shape[0]
    shapes = [(2 * depth, local), (2 * depth, local), (local // 2, 2 * depth)]
    return pl.pallas_call(
        project_out_kernel,
        grid_spec=pltpu.PrefetchScalarGridSpec(
            num_scalar_prefetch=1,
            grid=(1,),
            in_specs=[whole_spec(mine), whole_spec(other)],
            out_specs=[pl.BlockSpec(s, lambda i, a: (0, 0)) for s in shapes],
        ),
        out_shape=[jax.ShapeDtypeStruct(s, F32) for s in shapes],
        cost_estimate=COST,
        name="project_out",
    )(at, mine, other)


def after(value, *others):
    return lax.optimization_barrier((value, *others))[0]


def together(*values):
    return lax.optimization_barrier(values)


class Chips:
    def __init__(self, count):
        self.count = count
        chips = count // 2
        self.factors = []
        if (chips.bit_length() - 1) % 2:
            self.factors.append(2)
            chips //= 2
        while chips > 1:
            self.factors.append(4)
            chips //= 4
        self.index = lax.axis_index("dp")
        self.core = self.index % 2
        self.near = (self.index // 2) % 2

    def flip(self, value, bit):
        return lax.ppermute(value, "dp", [(i, i ^ bit) for i in range(self.count)])

    def swap_core(self, value):
        return self.flip(value, 1)

    def swap_near(self, value):
        return self.flip(value, 2)

    def shift(self, value, stride, factor, by):
        perm = []
        for i in range(self.count):
            digit = (i // stride) % factor
            perm.append((i, i + (((digit + by) % factor) - digit) * stride))
        return lax.ppermute(value, "dp", perm)

    def stages(self):
        stride = 2
        for factor in self.factors:
            yield stride, factor, (self.index // stride) % factor
            stride *= factor

    def scatter_start(self, value, stage):
        stride, factor, digit = stage
        rows = value.shape[0] // factor
        parts = [lax.dynamic_slice_in_dim(value, digit * rows, rows, 0)]
        for by in range(1, factor):
            part = lax.dynamic_slice_in_dim(value, ((digit + by) % factor) * rows, rows, 0)
            parts.append(self.shift(part, stride, factor, by))
        return tuple(parts)

    def scatter(self, value, stage):
        return add(*self.scatter_start(value, stage))

    def gather_start(self, value, stage):
        stride, factor, digit = stage
        return (value, *(self.shift(value, stride, factor, by) for by in range(1, factor)))

    def gather(self, value, stage):
        return self.gather_finish(self.gather_start(value, stage), stage)

    def gather_finish(self, parts, stage):
        stride, factor, digit = stage
        return jnp.concatenate(
            [
                lax.select_n((digit - at) % factor, *parts)
                if factor > 2
                else jnp.where(digit == at, parts[0], parts[1])
                for at in range(factor)
            ],
            axis=0,
        )

    def sum_small(self, value):
        value = value + self.swap_core(value)
        for stride, factor, digit in self.stages():
            total = value
            for by in range(1, factor):
                total = total + self.shift(value, stride, factor, by)
            value = total
        return value


def swap_tensor(value):
    return lax.ppermute(value, "tensor", [(0, 1), (1, 0)])


def block_of(value, at, count, axis):
    size = value.shape[axis] // count
    return lax.dynamic_slice_in_dim(value, at * size, size, axis)


def in_order(bit, mine, other, axis):
    return jnp.concatenate(
        [jnp.where(bit == 0, mine, other), jnp.where(bit == 0, other, mine)], axis=axis
    )


def add(*values):
    total = values[0].astype(F32)
    for value in values[1:]:
        total = total + value.astype(F32)
    return total.astype(BF)


def on_device(
    dp_count,
    block_input,
    skip_values,
    segment_ids,
    row_fill,
    query_weight,
    query_bias,
    key_weight,
    value_weight,
    value_bias,
    out_weight,
    out_bias,
    up_weight,
    up_bias,
    down_weight,
    down_bias,
    first_gain,
    first_shift,
    second_gain,
    second_shift,
    cotangent,
):
    chips = Chips(dp_count)
    core, near = chips.core, chips.near
    side = lax.axis_index("tensor")
    at = jnp.stack([core, side, 2 * core + near]).astype(jnp.int32)
    rows, length, width = block_input.shape
    tokens = rows * length
    local = query_weight.shape[1]
    local_half = local // 2
    hidden_local = up_weight.shape[1]
    piece = hidden_local // 2
    quarter = 2 * core + near
    stages = list(chips.stages())
    where = Rows(width, local, hidden_local)

    qkv_own, qkv_send, halo_send, skip_send, skip_own = open_step(
        at, query_weight, key_weight, value_weight.T, block_input, jnp.swapaxes(skip_values, 1, 2)
    )
    halo = lax.ppermute(halo_send, "tensor", [(0, 1)])
    qkv_tensor = swap_tensor(qkv_send)
    row_vectors = jnp.concatenate(
        [
            up_bias, query_bias, value_bias, jnp.zeros((where.pad,), F32),
            first_gain, first_shift, second_gain, second_shift, out_bias, down_bias,
        ]
    ).reshape(1, -1)
    rows_other = swap_tensor(after(row_vectors, qkv_send))
    normed = norm_rows(
        after(block_input, halo_send).astype(F32), first_gain, first_shift
    ).astype(BF).reshape(tokens, width)

    position = jnp.arange(segment_ids.shape[1], dtype=jnp.int32)
    usable = jnp.where(position[None] < row_fill[:, None], segment_ids, -1)
    query_seg = lax.dynamic_slice_in_dim(segment_ids, side * length, length, 1)
    key_seg = jnp.concatenate(
        [
            jnp.where(side == 0, -1, usable[:, length - SPAN : length]),
            lax.dynamic_slice_in_dim(usable, side * length, length, 1),
        ],
        axis=1,
    )
    query_seg = query_seg.reshape(rows, 1, length)
    key_seg = key_seg.reshape(rows, SPAN + length, 1)

    key_seg, query_seg, normed, row_vectors, qkv_tensor = together(
        key_seg, query_seg, normed, row_vectors, qkv_tensor
    )
    qkv_near = chips.swap_near(qkv_tensor)
    skip_got = swap_tensor(after(skip_send, qkv_tensor))

    normed_ext, qkv_l = project_own(where, normed, halo, row_vectors, qkv_own, rows)
    qkv_l, qkv_near, skip_got = together(qkv_l, qkv_near, skip_got)
    qkv_mine = in_order(near, qkv_tensor, qkv_near, 0)
    qkv_theirs = chips.swap_core(qkv_mine)
    down_tensor = swap_tensor(after(block_of(down_weight, quarter, 4, 0), qkv_near))
    out_mine = swap_tensor(after(block_of(out_weight, core, 2, 0), qkv_near))
    mixed_l, sums_l = attend_forward(after(qkv_l, qkv_mine), skip_own, key_seg, query_seg)
    mixed_l, qkv_theirs, out_mine, down_tensor, rows_other = together(
        mixed_l, qkv_theirs, out_mine, down_tensor, rows_other
    )
    up_mine = swap_tensor(after(block_of(up_weight, core, 2, 1), down_tensor))
    down_near = chips.swap_near(down_tensor)
    out_theirs = chips.swap_core(out_mine)
    qkv_r = project_other(where, at, after(normed_ext, mixed_l), qkv_mine, qkv_theirs, rows_other)
    mixed_r, sums_r = attend_forward(qkv_r, skip_got, key_seg, query_seg)
    mixed_r, down_near, out_theirs = together(mixed_r, down_near, out_theirs)
    down_r1 = in_order(near, down_tensor, down_near, 0)
    down_r2 = chips.swap_core(down_r1)
    hidden, normed_two, out_other = middle(
        where, at, mixed_l, mixed_r, out_weight, out_mine, out_theirs,
        after(block_input, down_r1).reshape(tokens, width), row_vectors,
    )
    normed_two, up_mine = together(normed_two, up_mine)
    up_r1 = up_mine
    up_r2 = chips.swap_core(up_r1)

    out_grad = cotangent.reshape(tokens, width)
    (up_g_l2, up_g_l1, down_g_l2, down_g_l1, bias_g_l2, bias_g_l1, f_l, b_l) = feed(
        at, normed_two, out_grad, up_weight, up_weight, row_vectors, down_weight, down_weight, True,
    )
    up_r2, down_r2, b_l, up_g_l2, down_g_l2 = together(up_r2, down_r2, b_l, up_g_l2, down_g_l2)
    up_c_l, down_c_l = chips.swap_core(up_g_l2), chips.swap_core(down_g_l2)
    (up_g_r2, up_g_r1, down_g_r2, down_g_r1, bias_g_r2, bias_g_r1, f_r, b_r) = feed(
        at, after(normed_two, b_l), out_grad, up_r2, up_r1, rows_other, down_r2, down_r1, False
    )
    up_g_r2, up_g_r1, down_g_r2, down_g_r1, b_r, up_c_l, down_c_l = together(
        up_g_r2, up_g_r1, down_g_r2, down_g_r1, b_r, up_c_l, down_c_l
    )

    up_c_r, down_c_r = chips.swap_core(up_g_r2), chips.swap_core(down_g_r2)
    up_l, down_l = add(up_g_l1, up_c_l), add(down_g_l1, down_c_l)
    down_lx = chips.scatter_start(down_l, stages[0])
    (hidden_grad, mixed_g_l, mixed_g_r, out_keep_l, out_keep_r, out_send, middle_sums) = middle_back(
        where, at, b_l, b_r, hidden, out_grad, mixed_l, mixed_r, out_weight, out_other, row_vectors
    )
    mixed_g_r, out_send, up_c_r, down_c_r, down_lx = together(
        mixed_g_r, out_send, up_c_r, down_c_r, down_lx
    )

    up_sum_r, down_sum_r = add(up_g_r1, up_c_r), add(down_g_r1, down_c_r)
    up_t = swap_tensor(up_sum_r)
    down_rx = chips.scatter_start(down_sum_r, stages[0])
    out_c = chips.swap_core(out_send)
    qkv_g_r, skip_g_r = attend_backward(
        qkv_r, skip_got, key_seg, query_seg, sums_r, after(mixed_g_r, up_sum_r, down_sum_r)
    )
    qkv_g_r, skip_g_r, down_rx, out_c = together(qkv_g_r, skip_g_r, down_rx, out_c)

    out_rows = local // 2
    down_y = add(*down_rx)
    down_t = swap_tensor(down_y)
    out_y = add(out_keep_r, out_c[out_rows:])
    out_t = swap_tensor(out_y)
    qkv_keep_r, qkv_send_r, qkv_sums_r = project_grad(
        at, after(normed_ext, down_y, out_y), qkv_g_r
    )
    qkv_keep_r, qkv_send_r, up_t = together(qkv_keep_r, qkv_send_r, up_t)
    qkv_c_r = chips.swap_core(qkv_send_r)
    up_1 = add(up_l, up_t)
    up_x = chips.scatter_start(up_1, stages[0])
    qkv_y = add(qkv_keep_r, qkv_c_r)
    qkv_t = swap_tensor(qkv_y)
    qkv_g_l, skip_g_l = attend_backward(
        qkv_l, skip_own, key_seg, query_seg, sums_l, after(mixed_g_l, up_1, qkv_y)
    )
    qkv_g_l, skip_g_l, up_x, down_t, out_t = together(qkv_g_l, skip_g_l, up_x, down_t, out_t)
    skip_back = swap_tensor(skip_g_r)
    out_x = chips.scatter_start(add(out_keep_l, out_c[:out_rows], out_t), stages[0])
    qkv_keep_l, qkv_send_l, qkv_sums_l = project_grad(at, normed_ext, qkv_g_l)
    qkv_c_l = chips.swap_core(qkv_send_l)
    up_2, down_2 = add(*up_x), add(*down_lx, down_t)
    qkv_keep_l, qkv_sums_l, out_x, up_2, down_2 = together(
        qkv_keep_l, qkv_sums_l, out_x, up_2, down_2
    )

    out_2 = add(*out_x)
    feed_2 = jnp.concatenate([up_2, down_2, out_2], axis=0)
    feed_x = chips.scatter_start(feed_2, stages[1])
    input_grad, halo_grad, first_sums = first_back(
        where, at, after(qkv_g_l, feed_2), qkv_g_r, qkv_own, qkv_mine, qkv_theirs,
        block_input.reshape(tokens, width), halo, hidden_grad, row_vectors, rows,
    )
    input_grad, halo_grad, first_sums, qkv_c_l, qkv_t = together(
        input_grad, halo_grad, first_sums, qkv_c_l, qkv_t
    )
    halo_got = lax.ppermute(halo_grad, "tensor", [(1, 0)])
    qkv_x = chips.scatter_start(add(qkv_keep_l, qkv_c_l, qkv_t), stages[0])

    own_small, other_small = small_step(
        where, at, middle_sums, first_sums, qkv_sums_l, qkv_sums_r,
        bias_g_l1, bias_g_l2, bias_g_r1, bias_g_r2,
    )
    small_t = swap_tensor(other_small)
    block_output = hidden + (f_l + after(f_r, input_grad) + down_bias)
    block_output, qkv_x, feed_x, small_t = together(block_output, qkv_x, feed_x, small_t)

    feed_3 = add(*feed_x)
    for stage in stages[2:]:
        feed_3 = chips.scatter(feed_3, stage)
    for stage in reversed(stages[2:]):
        feed_3 = chips.gather(feed_3, stage)
    qkv_2 = add(*qkv_x)
    qkv_x = chips.scatter_start(qkv_2, stages[1])
    feed_x = chips.gather_start(feed_3, stages[1])
    small = own_small + small_t
    small = small + chips.swap_core(small)
    skip_grad = skip_grad_of(at, after(skip_g_l, block_output), skip_back, rows)
    skip_grad, qkv_x, feed_x, small = together(skip_grad, qkv_x, feed_x, small)
    qkv_3 = add(*qkv_x)
    for stage in stages[2:]:
        qkv_3 = chips.scatter(qkv_3, stage)
    for stage in reversed(stages[2:]):
        qkv_3 = chips.gather(qkv_3, stage)
    qkv_x = chips.gather_start(qkv_3, stages[1])
    feed_4 = chips.gather_finish(feed_x, stages[1])
    feed_x = chips.gather_start(feed_4, stages[0])
    small_x = chips.gather_start(small, stages[0])
    input_grad = add_halo(after(input_grad, skip_grad), halo_got, rows)
    input_grad, qkv_x, small_x = together(input_grad, qkv_x, small_x)
    qkv_4 = chips.gather_finish(qkv_x, stages[1])
    qkv_x = chips.gather_start(qkv_4, stages[0])
    small = sum(small_x)
    for stage in stages[1:]:
        small = sum(chips.gather_start(small, stage))
    feed_x, qkv_x, small = together(feed_x, qkv_x, small)
    feed_4 = chips.gather_finish(feed_x, stages[0])
    feed_other = chips.swap_core(feed_4)
    qkv_4 = chips.gather_finish(qkv_x, stages[0])
    qkv_other = chips.swap_core(qkv_4)
    parts = up_2.shape[0], down_2.shape[0], out_2.shape[0]
    up_weight_grad, down_weight_grad, out_weight_grad = feed_out(
        at, feed_4, feed_other, parts, stages[0][1]
    )
    query_weight_grad, key_weight_grad, value_weight_grad = project_out(
        at, qkv_4, qkv_other, local
    )
    small = small[0]

    return (
        block_output.reshape(rows, length, width),
        input_grad.reshape(rows, length, width),
        jnp.swapaxes(skip_grad, 1, 2),
        query_weight_grad,
        small[where.query],
        key_weight_grad,
        value_weight_grad.T,
        small[where.value],
        out_weight_grad,
        small[where.out],
        up_weight_grad,
        small[where.up],
        down_weight_grad,
        small[where.down],
        small[where.gain_1],
        small[where.shift_1],
        small[where.gain_2],
        small[where.shift_2],
    )


def solution(mesh):
    in_specs = (
        P("dp", "tensor", None),
        P("dp", None, "tensor"),
        P("dp", None),
        P("dp"),
        P(None, "tensor"),
        P("tensor"),
        P(None, "tensor"),
        P(None, "tensor"),
        P("tensor"),
        P("tensor", None),
        P(),
        P(None, "tensor"),
        P("tensor"),
        P("tensor", None),
        P(),
        P(),
        P(),
        P(),
        P(),
        P("dp", "tensor", None),
    )
    out_specs = (
        P("dp", "tensor", None),
        P("dp", "tensor", None),
        P("dp", None, "tensor"),
        P(None, "tensor"),
        P("tensor"),
        P(None, "tensor"),
        P(None, "tensor"),
        P("tensor"),
        P("tensor", None),
        P(),
        P(None, "tensor"),
        P("tensor"),
        P("tensor", None),
        P(),
        P(),
        P(),
        P(),
        P(),
    )
    return jax.shard_map(
        functools.partial(on_device, mesh.shape["dp"]),
        mesh=mesh,
        in_specs=in_specs,
        out_specs=out_specs,
        check_vma=False,
    )
```

time: 533 us -> 395 us (0.74)
  waiting for transfers between devices: 187 us -> 88 us
  Pallas kernels: 104 us -> 200 us
  other arithmetic: 69.1 us -> 28.2 us
  matrix products: 35.2 us -> 0 us
  local copies, waits for them, and re-layouts: 52.5 us -> 17.3 us
  starting transfers between devices: 74.7 us -> 55.7 us
    pallas_call x2 -> x17, Pallas kernels: 47.8 us -> 142 us  [the longest x2 26.8 us: attend_backward(): pl.pallas_call(functools.partial(attend_backward_kernel, pairs), grid=(ro...]
    ppermute x12, waiting for transfers between devices: 91.4 us -> 14.1 us  [swap_tensor(): return lax.ppermute(value, 'tensor', [(0, 1), (1, 0)])]
    ppermute x36 -> x23, waiting for transfers between devices: 95.7 us -> 58.5 us  [shift(): return lax.ppermute(value, 'dp', perm)]
    dot_general x15 -> x0, matrix products: 35.2 us -> none  [the longest x6 12.7 us: dot_tn(): lax.dot_general(a, b, (((0,), (0,)), ((), ())), preferred_element_type=F32)]
    ppermute x36 -> x23, starting transfers between devices: 54.8 us -> 29.6 us  [shift(): return lax.ppermute(value, 'dp', perm)]
    concatenate x22 -> x7, other arithmetic: 18.4 us -> 0.56 us  [the longest x4 0.34 us: gather_finish(): jnp.concatenate([lax.select_n((digit - at) % factor, *parts) if factor >...]
    reduce_sum x12 -> x2, other arithmetic: 17.5 us -> 0.88 us  [the longest x1 0.6 us: norm_rows(): variance = jnp.mean(center * center, axis=-1, keepdims=True)]
    ppermute x19 -> x18, waiting for transfers between devices: 0.05 us -> 15.4 us  [the longest x1 13 us: on_device(): halo = lax.ppermute(halo_send, 'tensor', [(0, 1)])]
  transfers between devices with their start and end apart: 67 -> 53, of which waited for: 22 -> 15; matrix products, arithmetic and copies ran while one was open for 22% -> 9% of each run, Pallas kernels for 10% -> 48%
where the time goes in v2:
time: 395 us; the launch traced here: 391 us
  Pallas kernels  200 us (51%)
  waiting for transfers between devices  88 us (22%)
  starting transfers between devices  55.7 us (14%)
  other arithmetic  28.2 us (7%)
  local copies, waits for them, and re-layouts  17.3 us (4%)
    ppermute x23, waiting for transfers between devices, shift(): return lax.ppermute(value, 'dp', perm)  58.5 us
    pallas_call x2, Pallas kernels, feed(): pl.pallas_call(feed_kernel, grid_spec=pltpu.PrefetchScalarGridSpec(num_sc...  58 us
    ppermute x23, starting transfers between devices, shift(): return lax.ppermute(value, 'dp', perm)  29.6 us
    pallas_call x2, Pallas kernels, attend_backward(): pl.pallas_call(functools.partial(attend_backward_kernel, pairs), grid=(ro...  26.8 us
    pallas_call x2, Pallas kernels, attend_forward(): pl.pallas_call(functools.partial(attend_forward_kernel, pairs), grid=(row...  26 us
    ppermute x12, starting transfers between devices, swap_tensor(): return lax.ppermute(value, 'tensor', [(0, 1), (1, 0)])  17.8 us
    convert_element_type x15, other arithmetic, add(): return total.astype(BF)  15.6 us
    pallas_call x2, Pallas kernels, project_grad(): pl.pallas_call(project_grad_kernel, grid_spec=pltpu.PrefetchScalarGridSpe...  15.5 us
  transfers between devices with their start and end apart: 53, of which 15 were waited for; matrix products, arithmetic and copies ran while one was open for 9% of the time, Pallas kernels for 48%

profile of v2, /device:TPU:0, one launch (start us, length us, event | category | flops | bytes accessed | tf_op | source)
XLA Modules:
  0.0 391.0 jit_solution(5194632388920678177)
XLA Ops:
  1.3 5.0 %open.1 = (bf16[768,1024]{1,0:T(8,128)(2,1)}, bf16[192,1024]{1,0:T(8,128)(2,1)}, bf16[512,768]{1,0:T(8,128)(2,1)}, bf16[384,768]{1,0:T(8,128)(2,1)}, bf16[384,768]{1,0:T(8,128)(2,1)}) custom-call(s32[3]{0:T(128)} %pad_add_fusion.at_ref.core_ref, bf16[768,384]{1,0:T(8,128)(2,1)} %qw_ref.1, bf16[768,384]{1,0:T(8,128)(2,1)} %kw_ref.1, ...), custom_call_target="tpu_custom_call" | custom-call | flops 1048576 | bytes 1048576 | tf_op jit(solution)/shard_map/open/pallas_call | solution.py:381
  6.3 3.0 collective-permute-start
  15.5 3.6 collective-permute-done
  22.9 13.0 %collective-permute-done.1.h_ref = bf16[512,768]{1,0:T(8,128)(2,1)S(1)} collective-permute-done((bf16[512,768]{1,0:T(8,128)(2,1)}, bf16[512,768]{1,0:T(8,128)(2,1)S(1)}, u32[]{:S(2)}, u32[]{:S(2)}) %collective-permute-start.1) | collective-permute-done | bytes 786464 | tf_op jit(solution)/shard_map/ppermute | solution.py:1014
  36.8 8.4 %project_own.1 = (bf16[1536,768]{1,0:T(8,128)(2,1)}, bf16[1536,1024]{1,0:T(8,128)(2,1)}) custom-call(bf16[1024,768]{1,0:T(8,128)(2,1)} %bitcast.21, bf16[512,768]{1,0:T(8,128)(2,1)} %copy-done.6, f32[1,6784]{1,0:T(1,128)} %reshape.91.rows_ref.ba_ref.bb_ref, bf16[768,1024]{1,0:T(8,128)(2,1)} %get-tuple-element.189.w_ref.wl_ref), custom_call_target="tpu_custom_call" | custom-call | flops 1048576 | bytes 1048576 | tf_op jit(solution)/shard_map/project_own/pallas_call | solution.py:439
  58.4 13.0 %attend_forward.2 = (bf16[1024,384]{1,0:T(8,128)(2,1)}, f32[2,4,3,256]{3,2,1,0:T(4,128)}) custom-call(bf16[1536,1024]{1,0:T(8,128)(2,1)} %get-tuple-element.196.x_ref, bf16[384,768]{1,0:T(8,128)(2,1)} %get-tuple-element.197.s_ref, s32[2,768,1]{2,1,0:T(8,128)} %copy.39.kseg_ref, s32[2,1,512]{2,1,0:T(1,128)} %reshape.89.qseg_ref), custom_call_target="tpu_custom_call" | custom-call | flops 1048576 | bytes 1048576 | tf_op jit(solution)/shard_map/attend_forward/pallas_call | solution.py:153
  77.6 7.9 %project_other.1.x_ref = bf16[1536,1024]{1,0:T(8,128)(2,1)} custom-call(s32[3]{0:T(128)} %pad_add_fusion.at_ref.core_ref, bf16[1536,768]{1,0:T(8,128)(2,1)} %get-tuple-element.264.ne_ref.n_ref, bf16[384,1024]{1,0:T(8,128)(2,1)} %copy-done.4, bf16[384,1024]{1,0:T(8,128)(2,1)} %collective-permute-done.4.other_ref, f32[1,6784]{1,0:T(1,128)} %copy-done.30), custom_call_target="tpu_custom_call" | custom-call | flops 1048576 | bytes 1048576 | tf_op jit(solution)/shard_map/project_other/pallas_call | solution.py:478
  85.5 12.9 %attend_forward.3 = (bf16[1024,384]{1,0:T(8,128)(2,1)}, f32[2,4,3,256]{3,2,1,0:T(4,128)}) custom-call(bf16[1536,1024]{1,0:T(8,128)(2,1)} %project_other.1.x_ref, bf16[384,768]{1,0:T(8,128)(2,1)} %copy-done.9, s32[2,768,1]{2,1,0:T(8,128)} %copy.39.kseg_ref, s32[2,1,512]{2,1,0:T(1,128)} %reshape.89.qseg_ref), custom_call_target="tpu_custom_call" | custom-call | flops 1048576 | bytes 1048576 | tf_op jit(solution)/shard_map/attend_forward/pallas_call | solution.py:153
  100.4 7.1 %middle.1 = (f32[1024,768]{1,0:T(8,128)}, bf16[1024,768]{1,0:T(8,128)(2,1)}, bf16[384,768]{1,0:T(8,128)(2,1)}) custom-call(s32[3]{0:T(128)} %pad_add_fusion.at_ref.core_ref, bf16[1024,384]{1,0:T(8,128)(2,1)} %get-tuple-element.204.ml_ref, bf16[1024,384]{1,0:T(8,128)(2,1)} %get-tuple-element.213.mr_ref, bf16[384,768]{1,0:T(8,128)(2,1)} %wl_ref.3, ...), custom_call_target="tpu_custom_call" | custom-call | flops 1048576 | bytes 1048576 | tf_op jit(solution)/shard_map/middle/pallas_call | solution.py:513
  107.6 29.2 %feed.2 = (bf16[768,768]{1,0:T(8,128)(2,1)}, bf16[768,768]{1,0:T(8,128)(2,1)}, bf16[768,768]{1,0:T(8,128)(2,1)}, bf16[768,768]{1,0:T(8,128)(2,1)}, f32[1,768]{1,...) custom-call(s32[3]{0:T(128)} %pad_add_fusion.at_ref.core_ref, ...), custom_call_target="tpu_custom_call" | custom-call | flops 1048576 | bytes 1048576 | tf_op jit(solution)/shard_map/feed/pallas_call | solution.py:314
  138.0 28.8 %feed.3 = (bf16[768,768]{1,0:T(8,128)(2,1)}, bf16[768,768]{1,0:T(8,128)(2,1)}, bf16[768,768]{1,0:T(8,128)(2,1)}, bf16[768,768]{1,0:T(8,128)(2,1)}, f32[1,768]{1,...) custom-call(s32[3]{0:T(128)} %pad_add_fusion.at_ref.core_ref, ...), custom_call_target="tpu_custom_call" | custom-call | flops 1048576 | bytes 1048576 | tf_op jit(solution)/shard_map/feed/pallas_call | solution.py:314
  170.1 12.2 %middle_back.1 = (f32[1024,768]{1,0:T(8,128)}, bf16[1024,384]{1,0:T(8,128)(2,1)}, bf16[1024,384]{1,0:T(8,128)(2,1)}, bf16[192,768]{1,0:T(8,128)(2,1)}, bf16[192,...) custom-call(s32[3]{0:T(128)} %pad_add_fusion.at_ref.core_ref, f32[1024,768]{1,0:T(8,128)} %get-tuple-element.226.bl_ref, ...), custom_call_target="tpu_custom_call" | custom-call | flops 1048576 | bytes 1048576 | tf_op jit(solution)/shard_map/middle_back/pallas_call | solution.py:594
  182.2 3.2 collective-permute-done.17
  185.5 2.8 add_convert_fusion.2
  190.0 13.5 %attend_backward.2 = (bf16[1536,1024]{1,0:T(8,128)(2,1)}, bf16[384,768]{1,0:T(8,128)(2,1)}) custom-call(bf16[1536,1024]{1,0:T(8,128)(2,1)} %project_other.1.x_ref, bf16[384,768]{1,0:T(8,128)(2,1)} %copy-done.9, s32[2,768,1]{2,1,0:T(8,128)} %copy.39.kseg_ref, s32[2,1,512]{2,1,0:T(1,128)} %reshape.89.qseg_ref, f32[2,4,3,256]{3,2,1,0:T(4,128)} %get-tuple-element.244.lse_ref, ...), custom_call_target="tpu_custom_call" | custom-call | flops 1048576 | bytes 1048576 | tf_op jit(solution)/shard_map/attend_backward/pallas_call | solution.py:176
  207.3 7.8 %project_grad.2 = (bf16[384,1024]{1,0:T(8,128)(2,1)}, bf16[384,1024]{1,0:T(8,128)(2,1)}, f32[1,1024]{1,0:T(1,128)}) custom-call(s32[3]{0:T(128)} %pad_add_fusion.at_ref.core_ref, bf16[1536,768]{1,0:T(8,128)(2,1)} %get-tuple-element.264.ne_ref.n_ref, bf16[1536,1024]{1,0:T(8,128)(2,1)} %get-tuple-element.265.d_ref.dr_ref), custom_call_target="tpu_custom_call" | custom-call | flops 1048576 | bytes 1048576 | tf_op jit(solution)/shard_map/project_grad/pallas_call | solution.py:640
  224.5 13.2 %attend_backward.3 = (bf16[1536,1024]{1,0:T(8,128)(2,1)}, bf16[384,768]{1,0:T(8,128)(2,1)}) custom-call(bf16[1536,1024]{1,0:T(8,128)(2,1)} %get-tuple-element.196.x_ref, bf16[384,768]{1,0:T(8,128)(2,1)} %get-tuple-element.197.s_ref, s32[2,768,1]{2,1,0:T(8,128)} %copy.39.kseg_ref, s32[2,1,512]{2,1,0:T(1,128)} %reshape.89.qseg_ref, ...), custom_call_target="tpu_custom_call" | custom-call | flops 1048576 | bytes 1048576 | tf_op jit(solution)/shard_map/attend_backward/pallas_call | solution.py:176
  240.3 7.7 %project_grad.3 = (bf16[384,1024]{1,0:T(8,128)(2,1)}, bf16[384,1024]{1,0:T(8,128)(2,1)}, f32[1,1024]{1,0:T(1,128)}) custom-call(s32[3]{0:T(128)} %pad_add_fusion.at_ref.core_ref, bf16[1536,768]{1,0:T(8,128)(2,1)} %get-tuple-element.264.ne_ref.n_ref, bf16[1536,1024]{1,0:T(8,128)(2,1)} %get-tuple-element.288.d_ref.dl_ref), custom_call_target="tpu_custom_call" | custom-call | flops 1048576 | bytes 1048576 | tf_op jit(solution)/shard_map/project_grad/pallas_call | solution.py:640
  252.1 2.6 collective-permute-start.30
  256.1 13.9 %first_back.1 = (f32[1024,768]{1,0:T(8,128)}, bf16[512,768]{1,0:T(8,128)(2,1)}, f32[8,768]{1,0:T(8,128)}) custom-call(s32[3]{0:T(128)} %pad_add_fusion.at_ref.core_ref, bf16[1536,1024]{1,0:T(8,128)(2,1)} %get-tuple-element.288.d_ref.dl_ref, bf16[1536,1024]{1,0:T(8,128)(2,1)} %get-tuple-element.265.d_ref.dr_ref, ...), custom_call_target="tpu_custom_call" | custom-call | flops 1048576 | bytes 1048576 | tf_op jit(solution)/shard_map/first_back/pallas_call | solution.py:694
  275.5 4.5 %add_add_fusion = f32[1024,768]{1,0:T(8,128)} fusion(f32[1024,768]{1,0:T(8,128)S(1)} %copy-done.2, f32[1024,768]{1,0:T(8,128)S(1)} %copy-done.8, f32[1024,768]{1,0:T(8,128)} %get-tuple-element.295, f32[768]{0:T(1024)S(1)} %copy-done.35), kind=kLoop, calls=%fused_computation.8 | loop fusion | flops 2359296 | bytes 12585984 | tf_op jit(solution)/shard_map/add | solution.py:1149
  281.8 3.3 collective-permute-done.28
  290.6 3.8 collective-permute-done.33.got_ref
  295.4 18.6 %collective-permute-done.34 = bf16[48,1024]{1,0:T(8,128)(2,1)S(1)} collective-permute-done((bf16[48,1024]{1,0:T(8,128)(2,1)S(1)}, bf16[48,1024]{1,0:T(8,128)(2,1)S(1)}, u32[]{:S(2)}, u32[]{:S(2)}) %collective-permute-start.34) | collective-permute-done | bytes 98336 | tf_op jit(solution)/shard_map/ppermute | solution.py:903
  315.3 8.8 %collective-permute-done.35 = bf16[48,1024]{1,0:T(8,128)(2,1)S(1)} collective-permute-done((bf16[48,1024]{1,0:T(8,128)(2,1)S(1)}, bf16[48,1024]{1,0:T(8,128)(2,1)S(1)}, u32[]{:S(2)}, u32[]{:S(2)}) %collective-permute-start.35) | collective-permute-done | bytes 98336 | tf_op jit(solution)/shard_map/ppermute | solution.py:903
  324.5 3.2 skip_grad.1
  335.4 2.5 add_halo.1
  340.2 3.3 collective-permute-start.48
  345.1 2.8 collective-permute-start.50
  350.3 22.2 %collective-permute-done.47 = bf16[192,1024]{1,0:T(8,128)(2,1)S(1)} collective-permute-done((bf16[192,1024]{1,0:T(8,128)(2,1)S(1)}, bf16[192,1024]{1,0:T(8,128)(2,1)S(1)}, u32[]{:S(2)}, u32[]{:S(2)}) %collective-permute-start.47) | collective-permute-done | bytes 393248 | tf_op jit(solution)/shard_map/ppermute | solution.py:903
  379.2 3.8 project_out.1
  383.0 7.8 %feed_out.1 = (f32[768,1536]{1,0:T(8,128)}, f32[1536,768]{1,0:T(8,128)}, f32[384,768]{1,0:T(8,128)}) custom-call(s32[3]{0:T(128)} %pad_add_fusion.at_ref.core_ref, bf16[1728,768]{1,0:T(8,128)(2,1)} %copy-done.3, bf16[1728,768]{1,0:T(8,128)(2,1)} %collective-permute-done.52.other_ref), custom_call_target="tpu_custom_call" | custom-call | flops 1048576 | bytes 1048576 | tf_op jit(solution)/shard_map/feed_out/pallas_call | solution.py:824
  (247 shorter events, 95.8 us)
Async XLA Ops:
  9.2 26.7 %collective-permute-start.1 = (bf16[512,768]{1,0:T(8,128)(2,1)}, bf16[512,768]{1,0:T(8,128)(2,1)S(1)}, u32[]{:S(2)}, u32[]{:S(2)}) collective-permute-start(bf16[512,768]{1,0:T(8,128)(2,1)} %get-tuple-element.184), channel_id=1, source_target_pairs={{0,1},{2,3},{4,5},{6,7},{8,9},{10,11},{12,13},{14,15},{16,17},{18,... | collective-permute-start | bytes 2359304 | tf_op jit(solution)/shard_map/ppermute | solution.py:1014
  19.1 28.2 %collective-permute-start.3 = (bf16[384,768]{1,0:T(8,128)(2,1)S(1)}, bf16[384,768]{1,0:T(8,128)(2,1)S(1)}, u32[]{:S(2)}, u32[]{:S(2)}) collective-permute-start(bf16[384,768]{1,0:T(8,128)(2,1)S(1)} %copy-done.44), channel_id=1, source_target_pairs={{0,1},{1,0},{2,3},{3,2},{4,5},{5,4},{6,7},{7,6},{8,9},{9,8},{10,11... | collective-permute-start | bytes 1769480 | tf_op jit(solution)/shard_map/ppermute | solution.py:953
  21.5 23.8 %collective-permute-start.2 = (bf16[192,1024]{1,0:T(8,128)(2,1)S(1)}, bf16[192,1024]{1,0:T(8,128)(2,1)S(1)}, u32[]{:S(2)}, u32[]{:S(2)}) collective-permute-start(bf16[192,1024]{1,0:T(8,128)(2,1)S(1)} %collective-permute-done), channel_id=1, source_target_pairs={{0,4},{2,6},{4,0},{6,2},{8,12},{10,14},{12,8},{14,10},{16,20},{18,... | collective-permute-start | bytes 1179656 | tf_op jit(solution)/shard_map/ppermute | solution.py:890
  48.2 25.6 %collective-permute-start.4 = (bf16[384,1024]{1,0:T(8,128)(2,1)S(1)}, bf16[384,1024]{1,0:T(8,128)(2,1)}, u32[]{:S(2)}, u32[]{:S(2)}) collective-permute-start(bf16[384,1024]{1,0:T(8,128)(2,1)S(1)} %pad_maximum_fusion.4.mine_ref), channel_id=1, source_target_pairs={{0,2},{2,0},{4,6},{6,4},{8,10},{10,8},{12,14},{14,12},{16,18},{18,... | collective-permute-start | bytes 2359304 | tf_op jit(solution)/shard_map/ppermute | solution.py:890
  50.6 23.2 %collective-permute-start.6 = (bf16[384,768]{1,0:T(8,128)(2,1)}, bf16[384,768]{1,0:T(8,128)(2,1)}, u32[]{:S(2)}, u32[]{:S(2)}) collective-permute-start(bf16[384,768]{1,0:T(8,128)(2,1)} %constant_dynamic-slice_fusion.19), channel_id=1, source_target_pairs={{0,1},{1,0},{2,3},{3,2},{4,5},{5,4},{6,7},{7,6},{8,9},{9,8},{10,11... | collective-permute-start | bytes 1769480 | tf_op jit(solution)/shard_map/ppermute | solution.py:953
  54.0 19.7 %collective-permute-start.5 = (bf16[192,768]{1,0:T(8,128)(2,1)S(1)}, bf16[192,768]{1,0:T(8,128)(2,1)}, u32[]{:S(2)}, u32[]{:S(2)}) collective-permute-start(bf16[192,768]{1,0:T(8,128)(2,1)S(1)} %constant_dynamic-slice_fusion.20), channel_id=1, source_target_pairs={{0,1},{1,0},{2,3},{3,2},{4,5},{5,4},{6,7},{7,6},{8,9},{9,8},{10,11... | collective-permute-start | bytes 884744 | tf_op jit(solution)/shard_map/ppermute | solution.py:953
  54.1 19.6 %collective-permute-start.7 = (f32[1,6784]{1,0:T(1,128)S(1)}, f32[1,6784]{1,0:T(1,128)S(1)}, u32[]{:S(2)}, u32[]{:S(2)}) collective-permute-start(f32[1,6784]{1,0:T(1,128)S(1)} %copy-done.10), channel_id=1, source_target_pairs={{0,1},{1,0},{2,3},{3,2},{4,5},{5,4},{6,7},{7,6},{8,9},{9,8},{10,11... | collective-permute-start | bytes 81416 | tf_op jit(solution)/shard_map/ppermute | solution.py:953
  74.4 33.1 %collective-permute-start.10 = (bf16[768,768]{1,0:T(8,128)(2,1)S(1)}, bf16[768,768]{1,0:T(8,128)(2,1)S(1)}, u32[]{:S(2)}, u32[]{:S(2)}) collective-permute-start(bf16[768,768]{1,0:T(8,128)(2,1)S(1)} %copy-done.14), channel_id=1, source_target_pairs={{0,1},{1,0},{2,3},{3,2},{4,5},{5,4},{6,7},{7,6},{8,9},{9,8},{10,11... | collective-permute-start | bytes 3538952 | tf_op jit(solution)/shard_map/ppermute | solution.py:953
  76.1 22.3 %collective-permute-start.8 = (bf16[384,768]{1,0:T(8,128)(2,1)}, bf16[384,768]{1,0:T(8,128)(2,1)S(1)}, u32[]{:S(2)}, u32[]{:S(2)}) collective-permute-start(bf16[384,768]{1,0:T(8,128)(2,1)} %collective-permute-done.6), channel_id=1, source_target_pairs={{0,4},{2,6},{4,0},{6,2},{8,12},{10,14},{12,8},{14,10},{16,20},{18,... | collective-permute-start | bytes 1769480 | tf_op jit(solution)/shard_map/ppermute | solution.py:890
  77.6 20.8 %collective-permute-start.9 = (bf16[192,768]{1,0:T(8,128)(2,1)}, bf16[192,768]{1,0:T(8,128)(2,1)S(1)}, u32[]{:S(2)}, u32[]{:S(2)}) collective-permute-start(bf16[192,768]{1,0:T(8,128)(2,1)} %collective-permute-done.5.w1_ref), channel_id=1, source_target_pairs={{0,2},{2,0},{4,6},{6,4},{8,10},{10,8},{12,14},{14,12},{16,18},{18,... | collective-permute-start | bytes 884744 | tf_op jit(solution)/shard_map/ppermute | solution.py:890
  99.8 37.1 %collective-permute-start.12 = (bf16[768,768]{1,0:T(8,128)(2,1)S(1)}, bf16[768,768]{1,0:T(8,128)(2,1)}, u32[]{:S(2)}, u32[]{:S(2)}) collective-permute-start(bf16[768,768]{1,0:T(8,128)(2,1)S(1)} %pad_maximum_fusion.3.db_ref), channel_id=1, source_target_pairs={{0,2},{2,0},{4,6},{6,4},{8,10},{10,8},{12,14},{14,12},{16,18},{18,... | collective-permute-start | bytes 3538952 | tf_op jit(solution)/shard_map/ppermute | solution.py:890
  107.5 29.4 %collective-permute-start.11 = (bf16[768,768]{1,0:T(8,128)(2,1)S(1)}, bf16[768,768]{1,0:T(8,128)(2,1)S(1)}, u32[]{:S(2)}, u32[]{:S(2)}) collective-permute-start(bf16[768,768]{1,0:T(8,128)(2,1)S(1)} %collective-permute-done.10.ub_ref), channel_id=1, source_target_pairs={{0,2},{2,0},{4,6},{6,4},{8,10},{10,8},{12,14},{14,12},{16,18},{18,... | collective-permute-start | bytes 3538952 | tf_op jit(solution)/shard_map/ppermute | solution.py:890
  136.9 29.9 %collective-permute-start.13 = (bf16[768,768]{1,0:T(8,128)(2,1)}, bf16[768,768]{1,0:T(8,128)(2,1)S(1)}, u32[]{:S(2)}, u32[]{:S(2)}) collective-permute-start(bf16[768,768]{1,0:T(8,128)(2,1)} %get-tuple-element.237), channel_id=1, source_target_pairs={{0,2},{2,0},{4,6},{6,4},{8,10},{10,8},{12,14},{14,12},{16,18},{18,... | collective-permute-start | bytes 3538952 | tf_op jit(solution)/shard_map/ppermute | solution.py:890
  137.5 29.3 %collective-permute-start.14 = (bf16[768,768]{1,0:T(8,128)(2,1)}, bf16[768,768]{1,0:T(8,128)(2,1)S(1)}, u32[]{:S(2)}, u32[]{:S(2)}) collective-permute-start(bf16[768,768]{1,0:T(8,128)(2,1)} %get-tuple-element.238), channel_id=1, source_target_pairs={{0,2},{2,0},{4,6},{6,4},{8,10},{10,8},{12,14},{14,12},{16,18},{18,... | collective-permute-start | bytes 3538952 | tf_op jit(solution)/shard_map/ppermute | solution.py:890
  167.8 17.6 %collective-permute-start.15 = (bf16[768,768]{1,0:T(8,128)(2,1)}, bf16[768,768]{1,0:T(8,128)(2,1)}, u32[]{:S(2)}, u32[]{:S(2)}) collective-permute-start(bf16[768,768]{1,0:T(8,128)(2,1)} %get-tuple-element.247), channel_id=1, source_target_pairs={{0,2},{2,0},{4,6},{6,4},{8,10},{10,8},{12,14},{14,12},{16,18},{18,... | collective-permute-start | bytes 3538952 | tf_op jit(solution)/shard_map/ppermute | solution.py:890
  188.3 29.2 %collective-permute-start.20 = (bf16[768,768]{1,0:T(8,128)(2,1)}, bf16[768,768]{1,0:T(8,128)(2,1)}, u32[]{:S(2)}, u32[]{:S(2)}) collective-permute-start(bf16[768,768]{1,0:T(8,128)(2,1)} %add_convert_fusion.2), channel_id=1, source_target_pairs={{0,1},{1,0},{2,3},{3,2},{4,5},{5,4},{6,7},{7,6},{8,9},{9,8},{10,11... | collective-permute-start | bytes 3538952 | tf_op jit(solution)/shard_map/ppermute | solution.py:953
  204.8 33.0 %collective-permute-start.23 = (bf16[384,768]{1,0:T(8,128)(2,1)}, bf16[384,768]{1,0:T(8,128)(2,1)}, u32[]{:S(2)}, u32[]{:S(2)}) collective-permute-start(bf16[384,768]{1,0:T(8,128)(2,1)} %add_convert_fusion.9), channel_id=1, source_target_pairs={{0,1},{1,0},{2,3},{3,2},{4,5},{5,4},{6,7},{7,6},{8,9},{9,8},{10,11... | collective-permute-start | bytes 1769480 | tf_op jit(solution)/shard_map/ppermute | solution.py:953
  219.3 18.5 %collective-permute-start.22 = (bf16[384,768]{1,0:T(8,128)(2,1)S(1)}, bf16[384,768]{1,0:T(8,128)(2,1)S(1)}, u32[]{:S(2)}, u32[]{:S(2)}) collective-permute-start(bf16[384,768]{1,0:T(8,128)(2,1)S(1)} %get-tuple-element.366), channel_id=1, source_target_pairs={{0,4},{2,6},{4,0},{6,2},{8,12},{10,14},{12,8},{14,10},{16,20},{18,... | collective-permute-start | bytes 1769480 | tf_op jit(solution)/shard_map/ppermute | solution.py:903
  220.1 17.6 %collective-permute-start.24 = (bf16[192,768]{1,0:T(8,128)(2,1)S(1)}, bf16[192,768]{1,0:T(8,128)(2,1)}, u32[]{:S(2)}, u32[]{:S(2)}) collective-permute-start(bf16[192,768]{1,0:T(8,128)(2,1)S(1)} %copy-done.28), channel_id=1, source_target_pairs={{0,1},{1,0},{2,3},{3,2},{4,5},{5,4},{6,7},{7,6},{8,9},{9,8},{10,11... | collective-permute-start | bytes 884744 | tf_op jit(solution)/shard_map/ppermute | solution.py:953
  222.7 47.2 %collective-permute-start.27 = (bf16[384,1024]{1,0:T(8,128)(2,1)}, bf16[384,1024]{1,0:T(8,128)(2,1)}, u32[]{:S(2)}, u32[]{:S(2)}) collective-permute-start(bf16[384,1024]{1,0:T(8,128)(2,1)} %add_convert_fusion.6), channel_id=1, source_target_pairs={{0,1},{1,0},{2,3},{3,2},{4,5},{5,4},{6,7},{7,6},{8,9},{9,8},{10,11... | collective-permute-start | bytes 2359304 | tf_op jit(solution)/shard_map/ppermute | solution.py:953
  248.0 22.0 %collective-permute-start.26 = (bf16[384,1024]{1,0:T(8,128)(2,1)}, bf16[384,1024]{1,0:T(8,128)(2,1)}, u32[]{:S(2)}, u32[]{:S(2)}) collective-permute-start(bf16[384,1024]{1,0:T(8,128)(2,1)} %get-tuple-element.293), channel_id=1, source_target_pairs={{0,2},{2,0},{4,6},{6,4},{8,10},{10,8},{12,14},{14,12},{16,18},{18,... | collective-permute-start | bytes 2359304 | tf_op jit(solution)/shard_map/ppermute | solution.py:890
  250.6 29.4 %collective-permute-start.29 = (bf16[216,768]{1,0:T(8,128)(2,1)}, bf16[216,768]{1,0:T(8,128)(2,1)}, u32[]{:S(2)}, u32[]{:S(2)}) collective-permute-start(bf16[216,768]{1,0:T(8,128)(2,1)} %get-tuple-element.364), channel_id=1, source_target_pairs={{0,8},{2,10},{4,12},{6,14},{8,16},{10,18},{12,20},{14,22},{16,24},... | collective-permute-start | bytes 995336 | tf_op jit(solution)/shard_map/ppermute | solution.py:903
  252.1 29.7 %collective-permute-start.30 = (bf16[216,768]{1,0:T(8,128)(2,1)}, bf16[216,768]{1,0:T(8,128)(2,1)}, u32[]{:S(2)}, u32[]{:S(2)}) collective-permute-start(bf16[216,768]{1,0:T(8,128)(2,1)} %get-tuple-element.363), channel_id=1, source_target_pairs={{0,16},{2,18},{4,20},{6,22},{8,24},{10,26},{12,28},{14,30},{16,0},... | collective-permute-start | bytes 995336 | tf_op jit(solution)/shard_map/ppermute | solution.py:903
  254.7 27.1 %collective-permute-start.31 = (bf16[216,768]{1,0:T(8,128)(2,1)}, bf16[216,768]{1,0:T(8,128)(2,1)}, u32[]{:S(2)}, u32[]{:S(2)}) collective-permute-start(bf16[216,768]{1,0:T(8,128)(2,1)} %get-tuple-element.362), channel_id=1, source_target_pairs={{0,24},{2,26},{4,28},{6,30},{8,0},{10,2},{12,4},{14,6},{16,8},{18,... | collective-permute-start | bytes 995336 | tf_op jit(solution)/shard_map/ppermute | solution.py:903
  286.4 42.6 %collective-permute-start.37 = (bf16[216,768]{1,0:T(8,128)(2,1)S(1)}, bf16[216,768]{1,0:T(8,128)(2,1)S(1)}, u32[]{:S(2)}, u32[]{:S(2)}) collective-permute-start(bf16[216,768]{1,0:T(8,128)(2,1)S(1)} %add_convert_fusion.11), channel_id=1, source_target_pairs={{0,8},{2,10},{4,12},{6,14},{8,16},{10,18},{12,20},{14,22},{16,24},... | collective-permute-start | bytes 995336 | tf_op jit(solution)/shard_map/ppermute | solution.py:903
  287.1 41.9 %collective-permute-start.38 = (bf16[216,768]{1,0:T(8,128)(2,1)S(1)}, bf16[216,768]{1,0:T(8,128)(2,1)S(1)}, u32[]{:S(2)}, u32[]{:S(2)}) collective-permute-start(bf16[216,768]{1,0:T(8,128)(2,1)S(1)} %add_convert_fusion.11), channel_id=1, source_target_pairs={{0,16},{2,18},{4,20},{6,22},{8,24},{10,26},{12,28},{14,30},{16,0},... | collective-permute-start | bytes 995336 | tf_op jit(solution)/shard_map/ppermute | solution.py:903
  287.9 41.2 %collective-permute-start.39 = (bf16[216,768]{1,0:T(8,128)(2,1)S(1)}, bf16[216,768]{1,0:T(8,128)(2,1)S(1)}, u32[]{:S(2)}, u32[]{:S(2)}) collective-permute-start(bf16[216,768]{1,0:T(8,128)(2,1)S(1)} %add_convert_fusion.11), channel_id=1, source_target_pairs={{0,24},{2,26},{4,28},{6,30},{8,0},{10,2},{12,4},{14,6},{16,8},{18,... | collective-permute-start | bytes 995336 | tf_op jit(solution)/shard_map/ppermute | solution.py:903
  294.4 19.6 %collective-permute-start.34 = (bf16[48,1024]{1,0:T(8,128)(2,1)S(1)}, bf16[48,1024]{1,0:T(8,128)(2,1)S(1)}, u32[]{:S(2)}, u32[]{:S(2)}) collective-permute-start(bf16[48,1024]{1,0:T(8,128)(2,1)S(1)} %get-tuple-element.386), channel_id=1, source_target_pairs={{0,8},{2,10},{4,12},{6,14},{8,16},{10,18},{12,20},{14,22},{16,24},... | collective-permute-start | bytes 294920 | tf_op jit(solution)/shard_map/ppermute | solution.py:903
  295.1 29.0 %collective-permute-start.35 = (bf16[48,1024]{1,0:T(8,128)(2,1)S(1)}, bf16[48,1024]{1,0:T(8,128)(2,1)S(1)}, u32[]{:S(2)}, u32[]{:S(2)}) collective-permute-start(bf16[48,1024]{1,0:T(8,128)(2,1)S(1)} %get-tuple-element.385), channel_id=1, source_target_pairs={{0,16},{2,18},{4,20},{6,22},{8,24},{10,26},{12,28},{14,30},{16,0},... | collective-permute-start | bytes 294920 | tf_op jit(solution)/shard_map/ppermute | solution.py:903
  314.0 20.0 %collective-permute-start.41 = (bf16[512,768]{1,0:T(8,128)(2,1)}, bf16[512,768]{1,0:T(8,128)(2,1)S(1)}, u32[]{:S(2)}, u32[]{:S(2)}) collective-permute-start(bf16[512,768]{1,0:T(8,128)(2,1)} %get-tuple-element.322), channel_id=1, source_target_pairs={{1,0},{3,2},{5,4},{7,6},{9,8},{11,10},{13,12},{15,14},{17,16},{19,... | collective-permute-start | bytes 2359304 | tf_op jit(solution)/shard_map/ppermute | solution.py:1141
  334.1 38.5 %collective-permute-start.46 = (bf16[864,768]{1,0:T(8,128)(2,1)S(1)}, bf16[864,768]{1,0:T(8,128)(2,1)S(1)}, u32[]{:S(2)}, u32[]{:S(2)}) collective-permute-start(bf16[864,768]{1,0:T(8,128)(2,1)S(1)} %pad_maximum_fusion.2), channel_id=1, source_target_pairs={{0,4},{2,6},{4,0},{6,2},{8,12},{10,14},{12,8},{14,10},{16,20},{18,... | collective-permute-start | bytes 3981320 | tf_op jit(solution)/shard_map/ppermute | solution.py:903
  349.1 23.5 %collective-permute-start.47 = (bf16[192,1024]{1,0:T(8,128)(2,1)S(1)}, bf16[192,1024]{1,0:T(8,128)(2,1)S(1)}, u32[]{:S(2)}, u32[]{:S(2)}) collective-permute-start(bf16[192,1024]{1,0:T(8,128)(2,1)S(1)} %pad_maximum_fusion.6), channel_id=1, source_target_pairs={{0,4},{2,6},{4,0},{6,2},{8,12},{10,14},{12,8},{14,10},{16,20},{18,... | collective-permute-start | bytes 1179656 | tf_op jit(solution)/shard_map/ppermute | solution.py:903
  (67 other events, 498.4 us)

commit v3 on v2

--- a/solution.py
+++ b/solution.py
@@ -14,7 +14,7 @@
 SPAN = 256
 QB = 128
 WIN = SPAN + QB
-TH = 256
+TH = 768
 RC = 256
 NEG = -1000000000.0
 COST = pl.CostEstimate(flops=1 << 20, bytes_accessed=1 << 20, transcendentals=0)
@@ -349,7 +349,7 @@
     rows, length, width = x_ref.shape
     local, half = qw_ref.shape[1], vw_ref.shape[0]
     depth = w_send_ref.shape[0]
-    cut = pl.ds(pl.multiple_of(at_ref[2] * depth, depth), depth)
+    cut = pl.ds(pl.multiple_of(at_ref[0] * depth, depth), depth)
     w_ref[:, :local] = qw_ref[...]
     w_ref[:, local : 2 * local] = kw_ref[...]
     w_ref[:, 2 * local : 2 * local + half] = vw_ref[...].T
@@ -373,7 +373,7 @@
     columns = -(-(2 * local + half) // 256) * 256
     shapes = [
         (width, columns),
-        (width // 4, columns),
+        (width // 2, columns),
         (rows * SPAN, width),
         (rows * half, SPAN + length),
         (rows * half, SPAN + length),
@@ -416,16 +416,10 @@
 
 
 def project_own_kernel(where, n_ref, h_ref, rows_ref, w_ref, ne_ref, o_ref):
-    @pl.when(pl.program_id(1) == 0)
-    def _():
-        ne_ref[...] = norm_rows(
-            h_ref[...].astype(F32), rows_ref[:, where.gain_1], rows_ref[:, where.shift_1]
-        ).astype(BF)
-
-    @pl.when(pl.program_id(1) > 0)
-    def _():
-        ne_ref[...] = n_ref[...]
-
+    ne_ref[:SPAN, :] = norm_rows(
+        h_ref[...].astype(F32), rows_ref[:, where.gain_1], rows_ref[:, where.shift_1]
+    ).astype(BF)
+    ne_ref[SPAN:, :] = n_ref[...]
     store_projection(
         o_ref, dot_nn(ne_ref[...], w_ref[...]), rows_ref[:, where.query], rows_ref[:, where.value]
     )
@@ -433,22 +427,17 @@
 
 def project_own(where, normed, halo, row_vectors, weight, rows):
     width, columns = weight.shape
-    blocks = normed.shape[0] // SPAN // rows
-    extended = lambda cols: pl.BlockSpec((SPAN, cols), lambda r, j: (r * (blocks + 1) + j, 0))
-    size = rows * (blocks + 1) * SPAN
+    length = normed.shape[0] // rows
+    size = SPAN + length
+    row = lambda count, cols: pl.BlockSpec((count, cols), lambda r: (r, 0))
     return pl.pallas_call(
         functools.partial(project_own_kernel, where),
-        grid=(rows, blocks + 1),
-        in_specs=[
-            pl.BlockSpec((SPAN, width), lambda r, j: (r * blocks + jnp.maximum(j - 1, 0), 0)),
-            pl.BlockSpec((SPAN, width), lambda r, j: (r, 0)),
-            whole_spec(row_vectors),
-            whole_spec(weight),
-        ],
-        out_specs=[extended(width), extended(columns)],
+        grid=(rows,),
+        in_specs=[row(length, width), row(SPAN, width), whole_spec(row_vectors), whole_spec(weight)],
+        out_specs=[row(size, width), row(size, columns)],
         out_shape=[
-            jax.ShapeDtypeStruct((size, width), BF),
-            jax.ShapeDtypeStruct((size, columns), BF),
+            jax.ShapeDtypeStruct((rows * size, width), BF),
+            jax.ShapeDtypeStruct((rows * size, columns), BF),
         ],
         cost_estimate=COST,
         name="project_own",
@@ -472,19 +461,20 @@
     )
 
 
-def project_other(where, at, normed_ext, mine, other, row_vectors):
+def project_other(where, at, normed_ext, mine, other, row_vectors, rows):
     size, width = normed_ext.shape
+    step = size // rows
     columns = mine.shape[1]
     return pl.pallas_call(
         functools.partial(project_other_kernel, where),
         grid_spec=pltpu.PrefetchScalarGridSpec(
             num_scalar_prefetch=1,
-            grid=(size // SPAN,),
+            grid=(rows,),
             in_specs=[
-                pl.BlockSpec((SPAN, width), lambda i, a: (i, 0)),
+                pl.BlockSpec((step, width), lambda i, a: (i, 0)),
                 *[whole_spec(v) for v in (mine, other, row_vectors)],
             ],
-            out_specs=pl.BlockSpec((SPAN, columns), lambda i, a: (i, 0)),
+            out_specs=pl.BlockSpec((step, columns), lambda i, a: (i, 0)),
             scratch_shapes=[pltpu.VMEM((width, columns), BF)],
         ),
         out_shape=jax.ShapeDtypeStruct((size, columns), BF),
@@ -550,8 +540,8 @@
 
 
 def middle_back_kernel(
-    where, at_ref, bl_ref, br_ref, hidden_ref, g_ref, ml_ref, mr_ref, wl_ref, wr_ref, rows_ref,
-    hg_ref, gl_ref, gr_ref, keep_l_ref, keep_r_ref, send_ref, sums_ref, acc_l, acc_r,
+    where, bl_ref, br_ref, hidden_ref, g_ref, ml_ref, mr_ref, wl_ref, wr_ref, rows_ref,
+    hg_ref, gl_ref, gr_ref, ol_ref, or_ref, sums_ref, acc_l, acc_r,
 ):
     step = pl.program_id(0)
 
@@ -569,93 +559,89 @@
     hg_ref[...] = hidden_grad
     gl_ref[...] = dot_nt(low, wl_ref[...]).astype(BF)
     gr_ref[...] = dot_nt(low, wr_ref[...]).astype(BF)
-    acc_l[...] += dot_tn(ml_ref[...], low)
-    acc_r[...] += dot_tn(mr_ref[...], low)
+    turned = low.T
+    acc_l[...] += dot_nn(turned, ml_ref[...])
+    acc_r[...] += dot_nn(turned, mr_ref[...])
     for at, term in enumerate((low.astype(F32), cot, gain_term, grad)):
         sums_ref[at : at + 1, :] += down_rows(term)
 
     @pl.when(step == pl.num_programs(0) - 1)
     def _():
-        depth = keep_l_ref.shape[0]
-        core = at_ref[0]
-        mine = pl.ds(pl.multiple_of(core * depth, depth), depth)
-        other = pl.ds(pl.multiple_of((1 - core) * depth, depth), depth)
-        keep_l_ref[...] = acc_l[mine, :].astype(BF)
-        keep_r_ref[...] = acc_r[mine, :].astype(BF)
-        send_ref[:depth, :] = acc_l[other, :].astype(BF)
-        send_ref[depth:, :] = acc_r[other, :].astype(BF)
-
-
-def middle_back(where, at, back_l, back_r, hidden, grads, mixed_l, mixed_r, own, other, row_vectors):
+        ol_ref[...] = acc_l[...].astype(BF)
+        or_ref[...] = acc_r[...].astype(BF)
+
+
+def middle_back(where, back_l, back_r, hidden, grads, mixed_l, mixed_r, own, other, row_vectors):
     tokens, width = hidden.shape
     local = mixed_l.shape[1]
-    tile = lambda columns: pl.BlockSpec((RC, columns), lambda i, a: (i, 0))
-    fixed = lambda rows: pl.BlockSpec((rows, width), lambda i, a: (0, 0))
+    tile = lambda columns: pl.BlockSpec((RC, columns), lambda i: (i, 0))
+    fixed = lambda rows, columns: pl.BlockSpec((rows, columns), lambda i: (0, 0))
     return pl.pallas_call(
         functools.partial(middle_back_kernel, where),
-        grid_spec=pltpu.PrefetchScalarGridSpec(
-            num_scalar_prefetch=1,
-            grid=(tokens // RC,),
-            in_specs=[
-                tile(width), tile(width), tile(width), tile(width), tile(local), tile(local),
-                whole_spec(own), whole_spec(other), whole_spec(row_vectors),
-            ],
-            out_specs=[
-                tile(width), tile(local), tile(local),
-                fixed(local // 2), fixed(local // 2), fixed(local), fixed(8),
-            ],
-            scratch_shapes=[pltpu.VMEM((local, width), F32), pltpu.VMEM((local, width), F32)],
-        ),
+        grid=(tokens // RC,),
+        in_specs=[
+            tile(width), tile(width), tile(width), tile(width), tile(local), tile(local),
+            whole_spec(own), whole_spec(other), whole_spec(row_vectors),
+        ],
+        out_specs=[
+            tile(width), tile(local), tile(local),
+            fixed(width, local), fixed(width, local), fixed(8, width),
+        ],
+        scratch_shapes=[pltpu.VMEM((width, local), F32), pltpu.VMEM((width, local), F32)],
         out_shape=[
             jax.ShapeDtypeStruct((tokens, width), F32),
             jax.ShapeDtypeStruct((tokens, local), BF),
             jax.ShapeDtypeStruct((tokens, local), BF),
-            jax.ShapeDtypeStruct((local // 2, width), BF),
-            jax.ShapeDtypeStruct((local // 2, width), BF),
-            jax.ShapeDtypeStruct((local, width), BF),
+            jax.ShapeDtypeStruct((width, local), BF),
+            jax.ShapeDtypeStruct((width, local), BF),
             jax.ShapeDtypeStruct((8, width), F32),
         ],
         cost_estimate=COST,
         name="middle_back",
-    )(at, back_l, back_r, hidden, grads, mixed_l, mixed_r, own, other, row_vectors)
-
-
-def project_grad_kernel(at_ref, n_ref, d_ref, keep_ref, send_ref, sum_ref):
+    )(back_l, back_r, hidden, grads, mixed_l, mixed_r, own, other, row_vectors)
+
+
+def project_grad_kernel(at_ref, n_ref, d_ref, w_ref, keep_ref, send_ref, sum_ref):
     values = dot_tn(n_ref[...], d_ref[...]).astype(BF)
+    columns = d_ref.shape[1]
 
     @pl.when(pl.program_id(0) == 0)
     def _():
-        send_ref[...] = values
+        send_ref[:, :columns] = values
+        send_ref[:, columns:] = w_ref[...]
         sum_ref[...] = down_rows(d_ref[...].astype(F32))
 
     @pl.when(pl.program_id(0) == 1)
     def _():
-        keep_ref[...] = values
-
-
-def project_grad(at, normed_ext, grads):
+        keep_ref[:, :columns] = values
+        keep_ref[:, columns:] = w_ref[...]
+
+
+def project_grad(at, normed_ext, grads, out_grad):
     size, width = normed_ext.shape
-    columns = grads.shape[1]
-    fixed = pl.BlockSpec((width // 2, columns), lambda i, a: (0, 0))
+    columns, more = grads.shape[1], out_grad.shape[1]
+    fixed = pl.BlockSpec((width // 2, columns + more), lambda i, a: (0, 0))
+    half = lambda i, a: i * a[0] + (1 - i) * (1 - a[0])
     return pl.pallas_call(
         project_grad_kernel,
         grid_spec=pltpu.PrefetchScalarGridSpec(
             num_scalar_prefetch=1,
             grid=(2,),
             in_specs=[
-                pl.BlockSpec((size, width // 2), lambda i, a: (0, i * a[0] + (1 - i) * (1 - a[0]))),
+                pl.BlockSpec((size, width // 2), lambda i, a: (0, half(i, a))),
                 whole_spec(grads),
+                pl.BlockSpec((width // 2, more), lambda i, a: (half(i, a), 0)),
             ],
             out_specs=[fixed, fixed, pl.BlockSpec((1, columns), lambda i, a: (0, 0))],
         ),
         out_shape=[
-            jax.ShapeDtypeStruct((width // 2, columns), BF),
-            jax.ShapeDtypeStruct((width // 2, columns), BF),
+            jax.ShapeDtypeStruct((width // 2, columns + more), BF),
+            jax.ShapeDtypeStruct((width // 2, columns + more), BF),
             jax.ShapeDtypeStruct((1, columns), F32),
         ],
         cost_estimate=COST,
         name="project_grad",
-    )(at, normed_ext, grads)
+    )(at, normed_ext, grads, out_grad)
 
 
 def first_back_kernel(
@@ -801,28 +787,83 @@
     )(at, *values)
 
 
-def feed_out_kernel(parts, factor, at_ref, mine_ref, other_ref, up_ref, down_ref, out_ref):
+def down_out_kernel(at_ref, mine_ref, other_ref, o_ref):
+    is_mine = pl.program_id(0) // 2 == at_ref[0]
+    o_ref[...] = jnp.where(is_mine, mine_ref[...], other_ref[...]).astype(F32)
+
+
+def down_out(at, mine, other):
+    rows, width = mine.shape
+    block = pl.BlockSpec((rows // 2, width), lambda i, a: (i % 2, 0))
+    return pl.pallas_call(
+        down_out_kernel,
+        grid_spec=pltpu.PrefetchScalarGridSpec(
+            num_scalar_prefetch=1,
+            grid=(4,),
+            in_specs=[block, block],
+            out_specs=pl.BlockSpec((rows // 2, width), lambda i, a: (i, 0)),
+        ),
+        out_shape=jax.ShapeDtypeStruct((2 * rows, width), F32),
+        cost_estimate=COST,
+        name="down_out",
+    )(at, mine, other)
+
+
+def up_out_kernel(at_ref, mine_ref, other_ref, o_ref):
     core = at_ref[0]
-    a, b, c = parts
-    step = a + b + c
-    piece = up_ref.shape[1] // 2
+    piece = mine_ref.shape[1]
     for ref, at in ((mine_ref, core), (other_ref, 1 - core)):
-        lanes = pl.ds(pl.multiple_of(at * piece, 128), piece)
-        for digit in range(factor):
-            start = digit * step
-            up_ref[digit * a : (digit + 1) * a, lanes] = ref[start : start + a, :].astype(F32)
-            rows = pl.ds(pl.multiple_of(at * factor * b, 8) + digit * b, b)
-            down_ref[rows, :] = ref[start + a : start + a + b, :].astype(F32)
-            rows = pl.ds(pl.multiple_of(at * factor * c, 8) + digit * c, c)
-            out_ref[rows, :] = ref[start + a + b : start + step, :].astype(F32)
-
-
-def feed_out(at, mine, other, parts, factor):
-    a, b, c = parts
-    width = mine.shape[1]
-    shapes = [(factor * a, 2 * width), (2 * factor * b, width), (2 * factor * c, width)]
-    return pl.pallas_call(
-        functools.partial(feed_out_kernel, parts, factor),
+        o_ref[:, pl.ds(pl.multiple_of(at * piece, 128), piece)] = ref[...].astype(F32)
+
+
+def up_out(at, mine, other):
+    rows, width = mine.shape
+    block = pl.BlockSpec((rows // 4, width), lambda i, a: (i, 0))
+    return pl.pallas_call(
+        up_out_kernel,
+        grid_spec=pltpu.PrefetchScalarGridSpec(
+            num_scalar_prefetch=1,
+            grid=(4,),
+            in_specs=[block, block],
+            out_specs=pl.BlockSpec((rows // 4, 2 * width), lambda i, a: (i, 0)),
+        ),
+        out_shape=jax.ShapeDtypeStruct((rows, 2 * width), F32),
+        cost_estimate=COST,
+        name="up_out",
+    )(at, mine, other)
+
+
+def project_out_kernel(blocks, at_ref, mine_ref, other_ref, q_ref, k_ref, v_ref, out_ref, small_ref):
+    core = at_ref[0]
+    local = q_ref.shape[1]
+    depth = q_ref.shape[0] // 2
+    count = depth // blocks
+    step = mine_ref.shape[0] // blocks
+    columns = mine_ref.shape[1] - local
+    for ref, at in ((mine_ref, core), (other_ref, 1 - core)):
+        start = pl.multiple_of(at * depth, depth)
+        places = [(n % (blocks // 2)) * 2 + n // (blocks // 2) for n in range(blocks)]
+        parts = [ref[n * step : n * step + count, :].astype(F32) for n in places]
+        values = jnp.concatenate(parts, axis=0)
+        rows = pl.ds(start, depth)
+        q_ref[rows, :] = values[:, :local]
+        k_ref[rows, :] = values[:, local : 2 * local]
+        v_ref[:, rows] = values[:, 2 * local : 2 * local + v_ref.shape[0]].T
+        out_ref[:, rows] = values[:, columns:].T
+    small_ref[...] = sum(
+        mine_ref[n * step + count : (n + 1) * step, :].astype(F32) for n in range(blocks)
+    )
+
+
+def project_out(at, mine, other, local, depth, blocks):
+    columns = mine.shape[1]
+    rest = (mine.shape[0] - depth) // blocks
+    shapes = [
+        (2 * depth, local), (2 * depth, local), (local // 2, 2 * depth), (local, 2 * depth),
+        (rest, columns),
+    ]
+    return pl.pallas_call(
+        functools.partial(project_out_kernel, blocks),
         grid_spec=pltpu.PrefetchScalarGridSpec(
             num_scalar_prefetch=1,
             grid=(1,),
@@ -831,34 +872,6 @@
         ),
         out_shape=[jax.ShapeDtypeStruct(s, F32) for s in shapes],
         cost_estimate=COST,
-        name="feed_out",
-    )(at, mine, other)
-
-
-def project_out_kernel(at_ref, mine_ref, other_ref, q_ref, k_ref, v_ref):
-    core = at_ref[0]
-    depth = mine_ref.shape[0]
-    local = q_ref.shape[1]
-    for ref, at in ((mine_ref, core), (other_ref, 1 - core)):
-        rows = pl.ds(pl.multiple_of(at * depth, depth), depth)
-        q_ref[rows, :] = ref[:, :local].astype(F32)
-        k_ref[rows, :] = ref[:, local : 2 * local].astype(F32)
-        v_ref[:, rows] = ref[:, 2 * local : 2 * local + v_ref.shape[0]].astype(F32).T
-
-
-def project_out(at, mine, other, local):
-    depth = mine.shape[0]
-    shapes = [(2 * depth, local), (2 * depth, local), (local // 2, 2 * depth)]
-    return pl.pallas_call(
-        project_out_kernel,
-        grid_spec=pltpu.PrefetchScalarGridSpec(
-            num_scalar_prefetch=1,
-            grid=(1,),
-            in_specs=[whole_spec(mine), whole_spec(other)],
-            out_specs=[pl.BlockSpec(s, lambda i, a: (0, 0)) for s in shapes],
-        ),
-        out_shape=[jax.ShapeDtypeStruct(s, F32) for s in shapes],
-        cost_estimate=COST,
         name="project_out",
     )(at, mine, other)
 
@@ -874,26 +887,15 @@
 class Chips:
     def __init__(self, count):
         self.count = count
-        chips = count // 2
-        self.factors = []
-        if (chips.bit_length() - 1) % 2:
-            self.factors.append(2)
-            chips //= 2
-        while chips > 1:
-            self.factors.append(4)
-            chips //= 4
+        self.factors = [2] * ((count // 2).bit_length() - 1)
         self.index = lax.axis_index("dp")
         self.core = self.index % 2
-        self.near = (self.index // 2) % 2
 
     def flip(self, value, bit):
         return lax.ppermute(value, "dp", [(i, i ^ bit) for i in range(self.count)])
 
     def swap_core(self, value):
         return self.flip(value, 1)
-
-    def swap_near(self, value):
-        return self.flip(value, 2)
 
     def shift(self, value, stride, factor, by):
         perm = []
@@ -995,16 +997,15 @@
     cotangent,
 ):
     chips = Chips(dp_count)
-    core, near = chips.core, chips.near
+    core = chips.core
     side = lax.axis_index("tensor")
-    at = jnp.stack([core, side, 2 * core + near]).astype(jnp.int32)
+    at = jnp.stack([core, side]).astype(jnp.int32)
     rows, length, width = block_input.shape
     tokens = rows * length
     local = query_weight.shape[1]
     local_half = local // 2
     hidden_local = up_weight.shape[1]
     piece = hidden_local // 2
-    quarter = 2 * core + near
     stages = list(chips.stages())
     where = Rows(width, local, hidden_local)
 
@@ -1012,14 +1013,12 @@
         at, query_weight, key_weight, value_weight.T, block_input, jnp.swapaxes(skip_values, 1, 2)
     )
     halo = lax.ppermute(halo_send, "tensor", [(0, 1)])
-    qkv_tensor = swap_tensor(qkv_send)
     row_vectors = jnp.concatenate(
         [
             up_bias, query_bias, value_bias, jnp.zeros((where.pad,), F32),
             first_gain, first_shift, second_gain, second_shift, out_bias, down_bias,
         ]
     ).reshape(1, -1)
-    rows_other = swap_tensor(after(row_vectors, qkv_send))
     normed = norm_rows(
         after(block_input, halo_send).astype(F32), first_gain, first_shift
     ).astype(BF).reshape(tokens, width)
@@ -1037,46 +1036,52 @@
     query_seg = query_seg.reshape(rows, 1, length)
     key_seg = key_seg.reshape(rows, SPAN + length, 1)
 
-    key_seg, query_seg, normed, row_vectors, qkv_tensor = together(
-        key_seg, query_seg, normed, row_vectors, qkv_tensor
-    )
-    qkv_near = chips.swap_near(qkv_tensor)
-    skip_got = swap_tensor(after(skip_send, qkv_tensor))
+    out_piece = block_of(out_weight, core, 2, 0)
+    down_piece = block_of(down_weight, core, 2, 0)
+    up_piece = block_of(up_weight, core, 2, 1)
+    key_seg, query_seg, normed, row_vectors, qkv_send, out_piece, down_piece, up_piece = together(
+        key_seg, query_seg, normed, row_vectors, qkv_send, out_piece, down_piece, up_piece
+    )
+    qkv_mine = swap_tensor(qkv_send)
+    rows_other = swap_tensor(after(row_vectors, qkv_send))
 
     normed_ext, qkv_l = project_own(where, normed, halo, row_vectors, qkv_own, rows)
-    qkv_l, qkv_near, skip_got = together(qkv_l, qkv_near, skip_got)
-    qkv_mine = in_order(near, qkv_tensor, qkv_near, 0)
+    qkv_l, skip_send, qkv_mine, rows_other = together(qkv_l, skip_send, qkv_mine, rows_other)
     qkv_theirs = chips.swap_core(qkv_mine)
-    down_tensor = swap_tensor(after(block_of(down_weight, quarter, 4, 0), qkv_near))
-    out_mine = swap_tensor(after(block_of(out_weight, core, 2, 0), qkv_near))
-    mixed_l, sums_l = attend_forward(after(qkv_l, qkv_mine), skip_own, key_seg, query_seg)
-    mixed_l, qkv_theirs, out_mine, down_tensor, rows_other = together(
-        mixed_l, qkv_theirs, out_mine, down_tensor, rows_other
-    )
-    up_mine = swap_tensor(after(block_of(up_weight, core, 2, 1), down_tensor))
-    down_near = chips.swap_near(down_tensor)
+    skip_got = swap_tensor(skip_send)
+    mixed_l, sums_l = attend_forward(qkv_l, skip_own, key_seg, query_seg)
+    mixed_l, qkv_theirs, skip_got, out_piece, down_piece = together(
+        mixed_l, qkv_theirs, skip_got, out_piece, down_piece
+    )
+    out_mine = swap_tensor(out_piece)
+    qkv_r = project_other(
+        where, at, after(normed_ext, mixed_l), qkv_mine, qkv_theirs, rows_other, rows
+    )
+    qkv_r, out_mine, down_piece, up_piece = together(qkv_r, out_mine, down_piece, up_piece)
+    down_r1 = swap_tensor(down_piece)
     out_theirs = chips.swap_core(out_mine)
-    qkv_r = project_other(where, at, after(normed_ext, mixed_l), qkv_mine, qkv_theirs, rows_other)
+    up_r1 = swap_tensor(up_piece)
     mixed_r, sums_r = attend_forward(qkv_r, skip_got, key_seg, query_seg)
-    mixed_r, down_near, out_theirs = together(mixed_r, down_near, out_theirs)
-    down_r1 = in_order(near, down_tensor, down_near, 0)
-    down_r2 = chips.swap_core(down_r1)
+    mixed_r, out_theirs = together(mixed_r, out_theirs)
     hidden, normed_two, out_other = middle(
         where, at, mixed_l, mixed_r, out_weight, out_mine, out_theirs,
-        after(block_input, down_r1).reshape(tokens, width), row_vectors,
-    )
-    normed_two, up_mine = together(normed_two, up_mine)
-    up_r1 = up_mine
-    up_r2 = chips.swap_core(up_r1)
+        block_input.reshape(tokens, width), row_vectors,
+    )
 
     out_grad = cotangent.reshape(tokens, width)
     (up_g_l2, up_g_l1, down_g_l2, down_g_l1, bias_g_l2, bias_g_l1, f_l, b_l) = feed(
         at, normed_two, out_grad, up_weight, up_weight, row_vectors, down_weight, down_weight, True,
     )
-    up_r2, down_r2, b_l, up_g_l2, down_g_l2 = together(up_r2, down_r2, b_l, up_g_l2, down_g_l2)
+    b_l, up_g_l2, down_g_l2, down_r1, up_r1 = together(b_l, up_g_l2, down_g_l2, down_r1, up_r1)
+    down_r2 = chips.swap_core(down_r1)
+    up_r2 = chips.swap_core(up_r1)
+    block_half = hidden + (after(f_l, b_l) + down_bias)
+    block_half, up_r2, down_r2, up_g_l2, down_g_l2 = together(
+        block_half, up_r2, down_r2, up_g_l2, down_g_l2
+    )
     up_c_l, down_c_l = chips.swap_core(up_g_l2), chips.swap_core(down_g_l2)
     (up_g_r2, up_g_r1, down_g_r2, down_g_r1, bias_g_r2, bias_g_r1, f_r, b_r) = feed(
-        at, after(normed_two, b_l), out_grad, up_r2, up_r1, rows_other, down_r2, down_r1, False
+        at, after(normed_two, block_half), out_grad, up_r2, up_r1, rows_other, down_r2, down_r1, False
     )
     up_g_r2, up_g_r1, down_g_r2, down_g_r1, b_r, up_c_l, down_c_l = together(
         up_g_r2, up_g_r1, down_g_r2, down_g_r1, b_r, up_c_l, down_c_l
@@ -1085,111 +1090,124 @@
     up_c_r, down_c_r = chips.swap_core(up_g_r2), chips.swap_core(down_g_r2)
     up_l, down_l = add(up_g_l1, up_c_l), add(down_g_l1, down_c_l)
     down_lx = chips.scatter_start(down_l, stages[0])
-    (hidden_grad, mixed_g_l, mixed_g_r, out_keep_l, out_keep_r, out_send, middle_sums) = middle_back(
-        where, at, b_l, b_r, hidden, out_grad, mixed_l, mixed_r, out_weight, out_other, row_vectors
-    )
-    mixed_g_r, out_send, up_c_r, down_c_r, down_lx = together(
-        mixed_g_r, out_send, up_c_r, down_c_r, down_lx
-    )
+    hidden_grad, mixed_g_l, mixed_g_r, out_g_l, out_g_r, middle_sums = middle_back(
+        where, b_l, b_r, hidden, out_grad, mixed_l, mixed_r, out_weight, out_other, row_vectors
+    )
+    mixed_g_r, up_c_r, down_c_r, down_lx = together(mixed_g_r, up_c_r, down_c_r, down_lx)
 
     up_sum_r, down_sum_r = add(up_g_r1, up_c_r), add(down_g_r1, down_c_r)
+    down_rx = chips.scatter_start(down_sum_r, stages[0])
     up_t = swap_tensor(up_sum_r)
-    down_rx = chips.scatter_start(down_sum_r, stages[0])
-    out_c = chips.swap_core(out_send)
     qkv_g_r, skip_g_r = attend_backward(
         qkv_r, skip_got, key_seg, query_seg, sums_r, after(mixed_g_r, up_sum_r, down_sum_r)
     )
-    qkv_g_r, skip_g_r, down_rx, out_c = together(qkv_g_r, skip_g_r, down_rx, out_c)
-
-    out_rows = local // 2
+    qkv_g_r, skip_g_r, down_rx = together(qkv_g_r, skip_g_r, down_rx)
+
     down_y = add(*down_rx)
     down_t = swap_tensor(down_y)
-    out_y = add(out_keep_r, out_c[out_rows:])
-    out_t = swap_tensor(out_y)
     qkv_keep_r, qkv_send_r, qkv_sums_r = project_grad(
-        at, after(normed_ext, down_y, out_y), qkv_g_r
+        at, after(normed_ext, down_y), qkv_g_r, out_g_r
     )
     qkv_keep_r, qkv_send_r, up_t = together(qkv_keep_r, qkv_send_r, up_t)
     qkv_c_r = chips.swap_core(qkv_send_r)
     up_1 = add(up_l, up_t)
     up_x = chips.scatter_start(up_1, stages[0])
     qkv_y = add(qkv_keep_r, qkv_c_r)
-    qkv_t = swap_tensor(qkv_y)
+    qkv_t_1 = swap_tensor(qkv_y[: width // 6])
     qkv_g_l, skip_g_l = attend_backward(
         qkv_l, skip_own, key_seg, query_seg, sums_l, after(mixed_g_l, up_1, qkv_y)
     )
-    qkv_g_l, skip_g_l, up_x, down_t, out_t = together(qkv_g_l, skip_g_l, up_x, down_t, out_t)
-    skip_back = swap_tensor(skip_g_r)
-    out_x = chips.scatter_start(add(out_keep_l, out_c[:out_rows], out_t), stages[0])
-    qkv_keep_l, qkv_send_l, qkv_sums_l = project_grad(at, normed_ext, qkv_g_l)
+    qkv_g_l, skip_g_l, up_x, down_t, qkv_t_1 = together(qkv_g_l, skip_g_l, up_x, down_t, qkv_t_1)
+    qkv_t_2 = swap_tensor(qkv_y[width // 6 :])
+
+    def rest(value):
+        for stage in stages[3:]:
+            value = chips.scatter(value, stage)
+        for stage in reversed(stages[3:]):
+            value = chips.gather(value, stage)
+        return value
+
+    factor = stages[0][1]
+    up_rows = up_1.shape[0] // factor
+    feed_2 = jnp.concatenate([add(*up_x), add(*down_lx, down_t)], axis=0)
+    feed_x = chips.scatter_start(feed_2, stages[1])
+    qkv_keep_l, qkv_send_l, qkv_sums_l = project_grad(
+        at, after(normed_ext, feed_2), qkv_g_l, out_g_l
+    )
+    qkv_keep_l, qkv_send_l, qkv_sums_l, feed_x, qkv_t_2 = together(
+        qkv_keep_l, qkv_send_l, qkv_sums_l, feed_x, qkv_t_2
+    )
     qkv_c_l = chips.swap_core(qkv_send_l)
-    up_2, down_2 = add(*up_x), add(*down_lx, down_t)
-    qkv_keep_l, qkv_sums_l, out_x, up_2, down_2 = together(
-        qkv_keep_l, qkv_sums_l, out_x, up_2, down_2
-    )
-
-    out_2 = add(*out_x)
-    feed_2 = jnp.concatenate([up_2, down_2, out_2], axis=0)
-    feed_x = chips.scatter_start(feed_2, stages[1])
+    feed_3 = add(*feed_x)
+    feed_x = chips.scatter_start(feed_3, stages[2])
+    qkv_t = jnp.concatenate([qkv_t_1, qkv_t_2], axis=0)
+
+    qkv_1 = add(qkv_keep_l, qkv_c_l, qkv_t)
+    qkv_x = chips.scatter_start(qkv_1, stages[0])
+    skip_back = swap_tensor(after(skip_g_r, qkv_1))
     input_grad, halo_grad, first_sums = first_back(
-        where, at, after(qkv_g_l, feed_2), qkv_g_r, qkv_own, qkv_mine, qkv_theirs,
+        where, at, after(qkv_g_l, qkv_1, feed_3), qkv_g_r, qkv_own, qkv_mine, qkv_theirs,
         block_input.reshape(tokens, width), halo, hidden_grad, row_vectors, rows,
     )
-    input_grad, halo_grad, first_sums, qkv_c_l, qkv_t = together(
-        input_grad, halo_grad, first_sums, qkv_c_l, qkv_t
-    )
-    halo_got = lax.ppermute(halo_grad, "tensor", [(1, 0)])
-    qkv_x = chips.scatter_start(add(qkv_keep_l, qkv_c_l, qkv_t), stages[0])
-
-    own_small, other_small = small_step(
-        where, at, middle_sums, first_sums, qkv_sums_l, qkv_sums_r,
-        bias_g_l1, bias_g_l2, bias_g_r1, bias_g_r2,
-    )
-    small_t = swap_tensor(other_small)
-    block_output = hidden + (f_l + after(f_r, input_grad) + down_bias)
-    block_output, qkv_x, feed_x, small_t = together(block_output, qkv_x, feed_x, small_t)
-
-    feed_3 = add(*feed_x)
-    for stage in stages[2:]:
-        feed_3 = chips.scatter(feed_3, stage)
-    for stage in reversed(stages[2:]):
-        feed_3 = chips.gather(feed_3, stage)
+    input_grad, halo_grad, first_sums, qkv_x, feed_x = together(
+        input_grad, halo_grad, first_sums, qkv_x, feed_x
+    )
+
     qkv_2 = add(*qkv_x)
     qkv_x = chips.scatter_start(qkv_2, stages[1])
-    feed_x = chips.gather_start(feed_3, stages[1])
+    feed_4 = rest(add(*feed_x))
+    feed_x = chips.gather_start(after(feed_4, qkv_2), stages[2])
+    own_small, other_small = small_step(
+        where, at, middle_sums, after(first_sums, qkv_2, feed_4), qkv_sums_l, qkv_sums_r,
+        bias_g_l1, bias_g_l2, bias_g_r1, bias_g_r2,
+    )
+    small_t = swap_tensor(other_small)
+    halo_got = lax.ppermute(after(halo_grad, other_small), "tensor", [(1, 0)])
+    skip_grad = skip_grad_of(at, after(skip_g_l, own_small), skip_back, rows)
+    skip_grad, qkv_x, small_t = together(skip_grad, qkv_x, small_t)
+    qkv_3 = add(*qkv_x)
+    qkv_x = chips.scatter_start(qkv_3, stages[2])
     small = own_small + small_t
-    small = small + chips.swap_core(small)
-    skip_grad = skip_grad_of(at, after(skip_g_l, block_output), skip_back, rows)
-    skip_grad, qkv_x, feed_x, small = together(skip_grad, qkv_x, feed_x, small)
-    qkv_3 = add(*qkv_x)
-    for stage in stages[2:]:
-        qkv_3 = chips.scatter(qkv_3, stage)
-    for stage in reversed(stages[2:]):
-        qkv_3 = chips.gather(qkv_3, stage)
-    qkv_x = chips.gather_start(qkv_3, stages[1])
-    feed_4 = chips.gather_finish(feed_x, stages[1])
-    feed_x = chips.gather_start(feed_4, stages[0])
-    small_x = chips.gather_start(small, stages[0])
-    input_grad = add_halo(after(input_grad, skip_grad), halo_got, rows)
-    input_grad, qkv_x, small_x = together(input_grad, qkv_x, small_x)
-    qkv_4 = chips.gather_finish(qkv_x, stages[1])
+    small_c = chips.swap_core(small)
+    block_output = block_half + after(f_r, small, qkv_3)
+    block_output, small_c, feed_x = together(block_output, small_c, feed_x)
+    feed_5 = chips.gather_finish(feed_x, stages[2])
+    feed_x = chips.gather_start(feed_5, stages[1])
+    small = small + small_c
+    for stage in stages[3:]:
+        small = sum(chips.gather_start(small, stage))
+    columns = qkv_2.shape[1]
+    small_rows = -(-where.size // (8 * columns)) * 8
+    small = jnp.pad(small[0], (0, small_rows * columns - where.size)).reshape(small_rows, columns)
+    small, qkv_x = together(after(small, feed_5), qkv_x)
+
+    qkv_4 = jnp.concatenate([rest(add(*qkv_x)), small.astype(BF)], axis=0)
     qkv_x = chips.gather_start(qkv_4, stages[0])
-    small = sum(small_x)
-    for stage in stages[1:]:
-        small = sum(chips.gather_start(small, stage))
-    feed_x, qkv_x, small = together(feed_x, qkv_x, small)
-    feed_4 = chips.gather_finish(feed_x, stages[0])
-    feed_other = chips.swap_core(feed_4)
-    qkv_4 = chips.gather_finish(qkv_x, stages[0])
-    qkv_other = chips.swap_core(qkv_4)
-    parts = up_2.shape[0], down_2.shape[0], out_2.shape[0]
-    up_weight_grad, down_weight_grad, out_weight_grad = feed_out(
-        at, feed_4, feed_other, parts, stages[0][1]
-    )
-    query_weight_grad, key_weight_grad, value_weight_grad = project_out(
-        at, qkv_4, qkv_other, local
-    )
-    small = small[0]
+    qkv_x, feed_x = together(qkv_x, feed_x)
+    feed_6 = chips.gather_finish(feed_x, stages[1])
+    up_6, down_6 = feed_6[:up_rows], feed_6[up_rows:]
+    up_x = chips.gather_start(up_6, stages[0])
+    qkv_5 = chips.gather_finish(qkv_x, stages[0])
+    qkv_x = chips.gather_start(after(qkv_5, up_6), stages[2])
+    qkv_x, up_x, down_6 = together(qkv_x, up_x, down_6)
+    down_x = chips.gather_start(down_6, stages[0])
+    up_7 = chips.gather_finish(up_x, stages[0])
+    up_c = chips.swap_core(up_7)
+    qkv_6 = chips.gather_finish(qkv_x, stages[2])
+    qkv_x = chips.gather_start(after(qkv_6, up_7), stages[1])
+    input_grad = add_halo(after(input_grad, qkv_6, up_7), halo_got, rows)
+    up_weight_grad = up_out(at, after(up_7, input_grad), up_c)
+    up_weight_grad, qkv_x, down_x = together(up_weight_grad, qkv_x, down_x)
+    qkv_7 = chips.gather_finish(qkv_x, stages[1])
+    qkv_other = chips.swap_core(qkv_7)
+    down_7 = chips.gather_finish(down_x, stages[0])
+    down_c = chips.swap_core(down_7)
+    query_weight_grad, key_weight_grad, value_weight_grad, out_weight_grad, small = project_out(
+        at, after(qkv_7, down_7), qkv_other, local, width // 2, factor**3
+    )
+    query_weight_grad, down_c = together(query_weight_grad, down_c)
+    down_weight_grad = down_out(at, down_7, down_c)
+    small = small.reshape(-1)
 
     return (
         block_output.reshape(rows, length, width),

time: 395 us -> 376 us (0.952)
  starting transfers between devices: 55.7 us -> 40.6 us
  waiting for transfers between devices: 88 us -> 74.8 us
  other arithmetic: 28.2 us -> 36.7 us
  local copies, waits for them, and re-layouts: 17.3 us -> 23.7 us
  Pallas kernels: 200 us -> 194 us
    ppermute x23 -> x15, waiting for transfers between devices: 58.5 us -> 43 us  [shift(): return lax.ppermute(value, 'dp', perm)]
    ppermute x23 -> x15, starting transfers between devices: 29.6 us -> 17.8 us  [shift(): return lax.ppermute(value, 'dp', perm)]
    pallas_call x2, Pallas kernels: 58 us -> 52.1 us  [feed(): pl.pallas_call(feed_kernel, grid_spec=pltpu.PrefetchScalarGridSpec(num_sc...]
    convert_element_type x15 -> x14, other arithmetic: 15.6 us -> 21.4 us  [add(): return total.astype(BF)]
    dynamic_slice x7, local copies, waits for them, and re-layouts: 2.22 us -> 6.87 us  [scatter_start(): lax.dynamic_slice_in_dim(value, (digit + by) % factor * rows, rows, 0)]
    ppermute x16 -> x14, waiting for transfers between devices: 2.38 us -> 6.48 us  [flip(): return lax.ppermute(value, 'dp', [(i, i ^ bit) for i in range(self.count)])]
    pallas_call x4 -> x5, Pallas kernels: 32.1 us -> 33.4 us  [the longest x1 11.6 us: middle_back(): pl.pallas_call(functools.partial(middle_back_kernel, where), grid=(tokens...]
  transfers between devices with their start and end apart: 53 -> 43, of which waited for: 15 -> 18; matrix products, arithmetic and copies ran while one was open for 9% -> 12% of each run, Pallas kernels for 48% -> 49%
where the time goes in v3:
time: 376 us; the launch traced here: 372 us
  Pallas kernels  194 us (52%)
  waiting for transfers between devices  74.8 us (20%)
  starting transfers between devices  40.6 us (11%)
  other arithmetic  36.7 us (10%)
  local copies, waits for them, and re-layouts  23.7 us (6%)
    pallas_call x2, Pallas kernels, feed(): pl.pallas_call(feed_kernel, grid_spec=pltpu.PrefetchScalarGridSpec(num_sc...  52.1 us
    ppermute x15, waiting for transfers between devices, shift(): return lax.ppermute(value, 'dp', perm)  43 us
    pallas_call x2, Pallas kernels, attend_backward(): pl.pallas_call(functools.partial(attend_backward_kernel, pairs), grid=(ro...  26.4 us
    pallas_call x2, Pallas kernels, attend_forward(): pl.pallas_call(functools.partial(attend_forward_kernel, pairs), grid=(row...  25.9 us
    convert_element_type x14, other arithmetic, add(): return total.astype(BF)  21.4 us
    ppermute x15, starting transfers between devices, shift(): return lax.ppermute(value, 'dp', perm)  17.8 us
    pallas_call x2, Pallas kernels, project_grad(): pl.pallas_call(project_grad_kernel, grid_spec=pltpu.PrefetchScalarGridSpe...  16.1 us
    ppermute x12, starting transfers between devices, swap_tensor(): return lax.ppermute(value, 'tensor', [(0, 1), (1, 0)])  14.6 us
  transfers between devices with their start and end apart: 43, of which 18 were waited for; matrix products, arithmetic and copies ran while one was open for 12% of the time, Pallas kernels for 49%

profile of v3, /device:TPU:0, one launch (start us, length us, event | category | flops | bytes accessed | tf_op | source)
XLA Modules:
  0.0 371.8 jit_solution(7574896714162197643)
XLA Ops:
  1.3 5.1 %open.1 = (bf16[768,1024]{1,0:T(8,128)(2,1)}, bf16[384,1024]{1,0:T(8,128)(2,1)}, bf16[512,768]{1,0:T(8,128)(2,1)}, bf16[384,768]{1,0:T(8,128)(2,1)}, bf16[384,768]{1,0:T(8,128)(2,1)}) custom-call(s32[2]{0:T(128)} %pad_add_fusion.at_ref.core_ref, bf16[768,384]{1,0:T(8,128)(2,1)} %qw_ref.1, bf16[768,384]{1,0:T(8,128)(2,1)} %kw_ref.1, ...), custom_call_target="tpu_custom_call" | custom-call | flops 1048576 | bytes 1048576 | tf_op jit(solution)/shard_map/open/pallas_call | solution.py:381
  6.4 4.9 %collective-permute-start = (bf16[512,768]{1,0:T(8,128)(2,1)}, bf16[512,768]{1,0:T(8,128)(2,1)S(1)}, u32[]{:S(2)}, u32[]{:S(2)}) collective-permute-start(bf16[512,768]{1,0:T(8,128)(2,1)} %get-tuple-element.194), channel_id=1, source_target_pairs={{0,1},{2,3},{4,5},{6,7},{8,9},{10,11},{12,13},{14,15},{16,17},{18,... | collective-permute-start | bytes 2359304 | tf_op jit(solution)/shard_map/ppermute | solution.py:1015
  15.1 3.3 constant_dynamic-slice_fusion.14
  20.5 9.0 %collective-permute-done.h_ref = bf16[512,768]{1,0:T(8,128)(2,1)S(1)} collective-permute-done((bf16[512,768]{1,0:T(8,128)(2,1)}, bf16[512,768]{1,0:T(8,128)(2,1)S(1)}, u32[]{:S(2)}, u32[]{:S(2)}) %collective-permute-start) | collective-permute-done | bytes 786464 | tf_op jit(solution)/shard_map/ppermute | solution.py:1015
  30.5 6.4 %project_own.1 = (bf16[1536,768]{1,0:T(8,128)(2,1)}, bf16[1536,1024]{1,0:T(8,128)(2,1)}) custom-call(bf16[1024,768]{1,0:T(8,128)(2,1)} %bitcast.18, bf16[512,768]{1,0:T(8,128)(2,1)} %copy-done.9, f32[1,6784]{1,0:T(1,128)} %copy-done.15, bf16[768,1024]{1,0:T(8,128)(2,1)} %get-tuple-element.199.w_ref.wl_ref), custom_call_target="tpu_custom_call" | custom-call | flops 1048576 | bytes 1048576 | tf_op jit(solution)/shard_map/project_own/pallas_call | solution.py:433
  36.8 8.9 %collective-permute-done.2.rows_ref.ba_ref.bb_ref = f32[1,6784]{1,0:T(1,128)S(1)} collective-permute-done((f32[1,6784]{1,0:T(1,128)S(1)}, f32[1,6784]{1,0:T(1,128)S(1)}, u32[]{:S(2)}, u32[]{:S(2)}) %collective-permute-start.2) | collective-permute-done | bytes 27168 | tf_op jit(solution)/shard_map/ppermute | solution.py:955
  49.5 12.9 %attend_forward.2 = (bf16[1024,384]{1,0:T(8,128)(2,1)}, f32[2,4,3,256]{3,2,1,0:T(4,128)}) custom-call(bf16[1536,1024]{1,0:T(8,128)(2,1)} %get-tuple-element.204.x_ref, bf16[384,768]{1,0:T(8,128)(2,1)} %get-tuple-element.205.s_ref, s32[2,768,1]{2,1,0:T(8,128)} %copy.39.kseg_ref, s32[2,1,512]{2,1,0:T(1,128)} %reshape.84.qseg_ref), custom_call_target="tpu_custom_call" | custom-call | flops 1048576 | bytes 1048576 | tf_op jit(solution)/shard_map/attend_forward/pallas_call | solution.py:153
  64.3 6.5 %project_other.1.x_ref = bf16[1536,1024]{1,0:T(8,128)(2,1)} custom-call(s32[2]{0:T(128)} %pad_add_fusion.at_ref.core_ref, bf16[1536,768]{1,0:T(8,128)(2,1)} %get-tuple-element.293.ne_ref.n_ref, bf16[384,1024]{1,0:T(8,128)(2,1)} %copy-done.7, bf16[384,1024]{1,0:T(8,128)(2,1)} %copy-done.8, f32[1,6784]{1,0:T(1,128)} %copy-done.26), custom_call_target="tpu_custom_call" | custom-call | flops 1048576 | bytes 1048576 | tf_op jit(solution)/shard_map/project_other/pallas_call | solution.py:468
  73.7 12.9 %attend_forward.3 = (bf16[1024,384]{1,0:T(8,128)(2,1)}, f32[2,4,3,256]{3,2,1,0:T(4,128)}) custom-call(bf16[1536,1024]{1,0:T(8,128)(2,1)} %project_other.1.x_ref, bf16[384,768]{1,0:T(8,128)(2,1)} %copy-done.10, s32[2,768,1]{2,1,0:T(8,128)} %copy.39.kseg_ref, s32[2,1,512]{2,1,0:T(1,128)} %reshape.84.qseg_ref), custom_call_target="tpu_custom_call" | custom-call | flops 1048576 | bytes 1048576 | tf_op jit(solution)/shard_map/attend_forward/pallas_call | solution.py:153
  87.3 7.1 %middle.1 = (f32[1024,768]{1,0:T(8,128)}, bf16[1024,768]{1,0:T(8,128)(2,1)}, bf16[384,768]{1,0:T(8,128)(2,1)}) custom-call(s32[2]{0:T(128)} %pad_add_fusion.at_ref.core_ref, bf16[1024,384]{1,0:T(8,128)(2,1)} %get-tuple-element.213.ml_ref, bf16[1024,384]{1,0:T(8,128)(2,1)} %get-tuple-element.225.mr_ref, bf16[384,768]{1,0:T(8,128)(2,1)} %wl_ref.3, ...), custom_call_target="tpu_custom_call" | custom-call | flops 1048576 | bytes 1048576 | tf_op jit(solution)/shard_map/middle/pallas_call | solution.py:503
  94.5 26.0 %feed.2 = (bf16[768,768]{1,0:T(8,128)(2,1)}, bf16[768,768]{1,0:T(8,128)(2,1)}, bf16[768,768]{1,0:T(8,128)(2,1)}, bf16[768,768]{1,0:T(8,128)(2,1)}, f32[1,768]{1,...) custom-call(s32[2]{0:T(128)} %pad_add_fusion.at_ref.core_ref, ...), custom_call_target="tpu_custom_call" | custom-call | flops 1048576 | bytes 1048576 | tf_op jit(solution)/shard_map/feed/pallas_call | solution.py:314
  120.5 4.0 %collective-permute-done.8.ub_ref = bf16[768,768]{1,0:T(8,128)(2,1)} collective-permute-done((bf16[768,768]{1,0:T(8,128)(2,1)}, bf16[768,768]{1,0:T(8,128)(2,1)}, u32[]{:S(2)}, u32[]{:S(2)}) %collective-permute-start.8) | collective-permute-done | bytes 1179680 | tf_op jit(solution)/shard_map/ppermute | solution.py:955
  130.2 26.1 %feed.3 = (bf16[768,768]{1,0:T(8,128)(2,1)}, bf16[768,768]{1,0:T(8,128)(2,1)}, bf16[768,768]{1,0:T(8,128)(2,1)}, bf16[768,768]{1,0:T(8,128)(2,1)}, f32[1,768]{1,...) custom-call(s32[2]{0:T(128)} %pad_add_fusion.at_ref.core_ref, ...), custom_call_target="tpu_custom_call" | custom-call | flops 1048576 | bytes 1048576 | tf_op jit(solution)/shard_map/feed/pallas_call | solution.py:314
  161.4 11.6 %middle_back.1 = (f32[1024,768]{1,0:T(8,128)}, bf16[1024,384]{1,0:T(8,128)(2,1)}, bf16[1024,384]{1,0:T(8,128)(2,1)}, bf16[768,384]{1,0:T(8,128)(2,1)}, bf16[768,384]{1,0:T(8,128)(2,1)}, /*index=5*/f32[8,768]{1,0:T(8,128)}) custom-call(f32[1024,768]{1,0:T(8,128)} %get-tuple-element.235.bl_ref, f32[1024,768]{1,0:T(8,128)} %get-tuple-element.253.br_ref, ...), custom_call_target="tpu_custom_call" | custom-call | flops 1048576 | bytes 1048576 | tf_op jit(solution)/shard_map/middle_back/pallas_call | solution.py:579
  175.6 3.0 add_convert_fusion.2
  183.5 13.2 %attend_backward.2 = (bf16[1536,1024]{1,0:T(8,128)(2,1)}, bf16[384,768]{1,0:T(8,128)(2,1)}) custom-call(bf16[1536,1024]{1,0:T(8,128)(2,1)} %project_other.1.x_ref, bf16[384,768]{1,0:T(8,128)(2,1)} %copy-done.10, s32[2,768,1]{2,1,0:T(8,128)} %copy.39.kseg_ref, s32[2,1,512]{2,1,0:T(1,128)} %reshape.84.qseg_ref, f32[2,4,3,256]{3,2,1,0:T(4,128)} %get-tuple-element.260.lse_ref, ...), custom_call_target="tpu_custom_call" | custom-call | flops 1048576 | bytes 1048576 | tf_op jit(solution)/shard_map/attend_backward/pallas_call | solution.py:176
  198.9 8.0 %project_grad.2 = (bf16[384,1408]{1,0:T(8,128)(2,1)}, bf16[384,1408]{1,0:T(8,128)(2,1)}, f32[1,1024]{1,0:T(1,128)}) custom-call(s32[2]{0:T(128)} %pad_add_fusion.at_ref.core_ref, bf16[1536,768]{1,0:T(8,128)(2,1)} %get-tuple-element.293.ne_ref.n_ref, bf16[1536,1024]{1,0:T(8,128)(2,1)} %get-tuple-element.277.d_ref.dr_ref, ...), custom_call_target="tpu_custom_call" | custom-call | flops 1048576 | bytes 1048576 | tf_op jit(solution)/shard_map/project_grad/pallas_call | solution.py:625
  218.8 13.2 %attend_backward.3 = (bf16[1536,1024]{1,0:T(8,128)(2,1)}, bf16[384,768]{1,0:T(8,128)(2,1)}) custom-call(bf16[1536,1024]{1,0:T(8,128)(2,1)} %get-tuple-element.204.x_ref, bf16[384,768]{1,0:T(8,128)(2,1)} %get-tuple-element.205.s_ref, s32[2,768,1]{2,1,0:T(8,128)} %copy.39.kseg_ref, s32[2,1,512]{2,1,0:T(1,128)} %reshape.84.qseg_ref, ...), custom_call_target="tpu_custom_call" | custom-call | flops 1048576 | bytes 1048576 | tf_op jit(solution)/shard_map/attend_backward/pallas_call | solution.py:176
  239.3 8.0 %project_grad.3 = (bf16[384,1408]{1,0:T(8,128)(2,1)}, bf16[384,1408]{1,0:T(8,128)(2,1)}, f32[1,1024]{1,0:T(1,128)}) custom-call(s32[2]{0:T(128)} %pad_add_fusion.at_ref.core_ref, bf16[1536,768]{1,0:T(8,128)(2,1)} %get-tuple-element.293.ne_ref.n_ref, bf16[1536,1024]{1,0:T(8,128)(2,1)} %get-tuple-element.304.d_ref.dl_ref, ...), custom_call_target="tpu_custom_call" | custom-call | flops 1048576 | bytes 1048576 | tf_op jit(solution)/shard_map/project_grad/pallas_call | solution.py:625
  247.3 5.3 %collective-permute-done.22 = bf16[384,768]{1,0:T(8,128)(2,1)} collective-permute-done((bf16[384,768]{1,0:T(8,128)(2,1)}, bf16[384,768]{1,0:T(8,128)(2,1)}, u32[]{:S(2)}, u32[]{:S(2)}) %collective-permute-start.22) | collective-permute-done | bytes 589856 | tf_op jit(solution)/shard_map/ppermute | solution.py:905
  252.6 3.0 collective-permute-done.24
  265.4 13.9 %first_back.1 = (f32[1024,768]{1,0:T(8,128)}, bf16[512,768]{1,0:T(8,128)(2,1)}, f32[8,768]{1,0:T(8,128)}) custom-call(s32[2]{0:T(128)} %pad_add_fusion.at_ref.core_ref, bf16[1536,1024]{1,0:T(8,128)(2,1)} %get-tuple-element.304.d_ref.dl_ref, bf16[1536,1024]{1,0:T(8,128)(2,1)} %get-tuple-element.277.d_ref.dr_ref, ...), custom_call_target="tpu_custom_call" | custom-call | flops 1048576 | bytes 1048576 | tf_op jit(solution)/shard_map/first_back/pallas_call | solution.py:680
  288.5 3.2 skip_grad.1
  293.7 3.9 %add.234 = f32[1024,768]{1,0:T(8,128)} add(f32[1024,768]{1,0:T(8,128)S(1)} %add_add_fusion, f32[1024,768]{1,0:T(8,128)} %get-tuple-element.330) | non-fusion elementwise | flops 786432 | bytes 9437184 | tf_op jit(solution)/shard_map/add | solution.py:1172
  299.5 6.2 %collective-permute-done.31 = bf16[192,768]{1,0:T(8,128)(2,1)} collective-permute-done((bf16[192,768]{1,0:T(8,128)(2,1)S(1)}, bf16[192,768]{1,0:T(8,128)(2,1)}, u32[]{:S(2)}, u32[]{:S(2)}) %collective-permute-start.31) | collective-permute-done | bytes 294944 | tf_op jit(solution)/shard_map/ppermute | solution.py:905
  309.6 4.4 %collective-permute-done.33 = bf16[56,1408]{1,0:T(8,128)(2,1)S(1)} collective-permute-done((bf16[56,1408]{1,0:T(8,128)(2,1)S(1)}, bf16[56,1408]{1,0:T(8,128)(2,1)S(1)}, u32[]{:S(2)}, u32[]{:S(2)}) %collective-permute-start.33) | collective-permute-done | bytes 157728 | tf_op jit(solution)/shard_map/ppermute | solution.py:905
  314.0 6.8 %collective-permute-done.34 = bf16[384,768]{1,0:T(8,128)(2,1)S(1)} collective-permute-done((bf16[384,768]{1,0:T(8,128)(2,1)S(1)}, bf16[384,768]{1,0:T(8,128)(2,1)S(1)}, u32[]{:S(2)}, u32[]{:S(2)}) %collective-permute-start.34) | collective-permute-done | bytes 589856 | tf_op jit(solution)/shard_map/ppermute | solution.py:905
  323.6 12.5 %collective-permute-done.35 = bf16[112,1408]{1,0:T(8,128)(2,1)S(1)} collective-permute-done((bf16[112,1408]{1,0:T(8,128)(2,1)S(1)}, bf16[112,1408]{1,0:T(8,128)(2,1)S(1)}, u32[]{:S(2)}, u32[]{:S(2)}) %collective-permute-start.35) | collective-permute-done | bytes 315424 | tf_op jit(solution)/shard_map/ppermute | solution.py:905
  343.7 5.0 %up_out.1 = f32[768,1536]{1,0:T(8,128)} custom-call(s32[2]{0:T(128)} %pad_add_fusion.at_ref.core_ref, bf16[768,768]{1,0:T(8,128)(2,1)} %copy-done.3, bf16[768,768]{1,0:T(8,128)(2,1)} %collective-permute-done.38.other_ref), custom_call_target="tpu_custom_call" | custom-call | flops 1048576 | bytes 1048576 | tf_op jit(solution)/shard_map/up_out/pallas_call | solution.py:822
  348.7 3.9 %collective-permute-done.40 = bf16[384,768]{1,0:T(8,128)(2,1)S(1)} collective-permute-done((bf16[384,768]{1,0:T(8,128)(2,1)S(1)}, bf16[384,768]{1,0:T(8,128)(2,1)S(1)}, u32[]{:S(2)}, u32[]{:S(2)}) %collective-permute-start.40) | collective-permute-done | bytes 589856 | tf_op jit(solution)/shard_map/ppermute | solution.py:905
  358.0 4.7 %project_out.1 = (f32[768,384]{1,0:T(8,128)}, f32[768,384]{1,0:T(8,128)}, f32[192,768]{1,0:T(8,128)}, f32[384,768]{1,0:T(8,128)}, f32[8,1408]{1,0:T(8,128)}) custom-call(s32[2]{0:T(128)} %pad_add_fusion.at_ref.core_ref, bf16[448,1408]{1,0:T(8,128)(2,1)} %copy-done.2, bf16[448,1408]{1,0:T(8,128)(2,1)} %collective-permute-done.41.other_ref), custom_call_target="tpu_custom_call" | custom-call | flops 1048576 | bytes 1048576 | tf_op jit(solution)/shard_map/project_out/pallas_call | solution.py:865
  365.9 5.7 %down_out.1 = f32[1536,768]{1,0:T(8,128)} custom-call(s32[2]{0:T(128)} %pad_add_fusion.at_ref.core_ref, bf16[768,768]{1,0:T(8,128)(2,1)} %copy-done.4, bf16[768,768]{1,0:T(8,128)(2,1)} %collective-permute-done.42.other_ref), custom_call_target="tpu_custom_call" | custom-call | flops 1048576 | bytes 1048576 | tf_op jit(solution)/shard_map/down_out/pallas_call | solution.py:798
  (222 shorter events, 101.3 us)
Async XLA Ops:
  6.4 23.1 %collective-permute-start = (bf16[512,768]{1,0:T(8,128)(2,1)}, bf16[512,768]{1,0:T(8,128)(2,1)S(1)}, u32[]{:S(2)}, u32[]{:S(2)}) collective-permute-start(bf16[512,768]{1,0:T(8,128)(2,1)} %get-tuple-element.194), channel_id=1, source_target_pairs={{0,1},{2,3},{4,5},{6,7},{8,9},{10,11},{12,13},{14,15},{16,17},{18,... | collective-permute-start | bytes 2359304 | tf_op jit(solution)/shard_map/ppermute | solution.py:1015
  18.4 27.3 %collective-permute-start.1 = (bf16[384,1024]{1,0:T(8,128)(2,1)S(1)}, bf16[384,1024]{1,0:T(8,128)(2,1)S(1)}, u32[]{:S(2)}, u32[]{:S(2)}) collective-permute-start(bf16[384,1024]{1,0:T(8,128)(2,1)S(1)} %copy-done.40), channel_id=1, source_target_pairs={{0,1},{1,0},{2,3},{3,2},{4,5},{5,4},{6,7},{7,6},{8,9},{9,8},{10,11... | collective-permute-start | bytes 2359304 | tf_op jit(solution)/shard_map/ppermute | solution.py:955
  18.5 27.2 %collective-permute-start.2 = (f32[1,6784]{1,0:T(1,128)S(1)}, f32[1,6784]{1,0:T(1,128)S(1)}, u32[]{:S(2)}, u32[]{:S(2)}) collective-permute-start(f32[1,6784]{1,0:T(1,128)S(1)} %reshape.86.rows_ref.ba_ref.bb_ref), channel_id=1, source_target_pairs={{0,1},{1,0},{2,3},{3,2},{4,5},{5,4},{6,7},{7,6},{8,9},{9,8},{10,11... | collective-permute-start | bytes 81416 | tf_op jit(solution)/shard_map/ppermute | solution.py:955
  45.7 16.8 %collective-permute-start.3 = (bf16[384,1024]{1,0:T(8,128)(2,1)S(1)}, bf16[384,1024]{1,0:T(8,128)(2,1)S(1)}, u32[]{:S(2)}, u32[]{:S(2)}) collective-permute-start(bf16[384,1024]{1,0:T(8,128)(2,1)S(1)} %collective-permute-done.1.mine_ref), channel_id=1, source_target_pairs={{0,2},{2,0},{4,6},{6,4},{8,10},{10,8},{12,14},{14,12},{16,18},{18,... | collective-permute-start | bytes 2359304 | tf_op jit(solution)/shard_map/ppermute | solution.py:895
  45.7 16.7 %collective-permute-start.4 = (bf16[384,768]{1,0:T(8,128)(2,1)}, bf16[384,768]{1,0:T(8,128)(2,1)S(1)}, u32[]{:S(2)}, u32[]{:S(2)}) collective-permute-start(bf16[384,768]{1,0:T(8,128)(2,1)} %get-tuple-element.210), channel_id=1, source_target_pairs={{0,1},{1,0},{2,3},{3,2},{4,5},{5,4},{6,7},{7,6},{8,9},{9,8},{10,11... | collective-permute-start | bytes 1769480 | tf_op jit(solution)/shard_map/ppermute | solution.py:955
  71.6 48.8 %collective-permute-start.7 = (bf16[768,768]{1,0:T(8,128)(2,1)}, bf16[768,768]{1,0:T(8,128)(2,1)}, u32[]{:S(2)}, u32[]{:S(2)}) collective-permute-start(bf16[768,768]{1,0:T(8,128)(2,1)} %get-tuple-element.233), channel_id=1, source_target_pairs={{0,1},{1,0},{2,3},{3,2},{4,5},{5,4},{6,7},{7,6},{8,9},{9,8},{10,11... | collective-permute-start | bytes 3538952 | tf_op jit(solution)/shard_map/ppermute | solution.py:955
  72.9 51.6 %collective-permute-start.8 = (bf16[768,768]{1,0:T(8,128)(2,1)}, bf16[768,768]{1,0:T(8,128)(2,1)}, u32[]{:S(2)}, u32[]{:S(2)}) collective-permute-start(bf16[768,768]{1,0:T(8,128)(2,1)} %get-tuple-element.234), channel_id=1, source_target_pairs={{0,1},{1,0},{2,3},{3,2},{4,5},{5,4},{6,7},{7,6},{8,9},{9,8},{10,11... | collective-permute-start | bytes 3538952 | tf_op jit(solution)/shard_map/ppermute | solution.py:955
  73.7 12.9 %collective-permute-start.6 = (bf16[192,768]{1,0:T(8,128)(2,1)S(1)}, bf16[192,768]{1,0:T(8,128)(2,1)S(1)}, u32[]{:S(2)}, u32[]{:S(2)}) collective-permute-start(bf16[192,768]{1,0:T(8,128)(2,1)S(1)} %collective-permute-done.5.w1_ref), channel_id=1, source_target_pairs={{0,2},{2,0},{4,6},{6,4},{8,10},{10,8},{12,14},{14,12},{16,18},{18,... | collective-permute-start | bytes 884744 | tf_op jit(solution)/shard_map/ppermute | solution.py:895
  129.3 27.0 %collective-permute-start.11 = (bf16[768,768]{1,0:T(8,128)(2,1)}, bf16[768,768]{1,0:T(8,128)(2,1)}, u32[]{:S(2)}, u32[]{:S(2)}) collective-permute-start(bf16[768,768]{1,0:T(8,128)(2,1)} %get-tuple-element.251), channel_id=1, source_target_pairs={{0,2},{2,0},{4,6},{6,4},{8,10},{10,8},{12,14},{14,12},{16,18},{18,... | collective-permute-start | bytes 3538952 | tf_op jit(solution)/shard_map/ppermute | solution.py:895
  129.5 26.9 %collective-permute-start.12 = (bf16[768,768]{1,0:T(8,128)(2,1)}, bf16[768,768]{1,0:T(8,128)(2,1)}, u32[]{:S(2)}, u32[]{:S(2)}) collective-permute-start(bf16[768,768]{1,0:T(8,128)(2,1)} %get-tuple-element.252), channel_id=1, source_target_pairs={{0,2},{2,0},{4,6},{6,4},{8,10},{10,8},{12,14},{14,12},{16,18},{18,... | collective-permute-start | bytes 3538952 | tf_op jit(solution)/shard_map/ppermute | solution.py:895
  156.3 19.3 %collective-permute-start.13 = (bf16[768,768]{1,0:T(8,128)(2,1)}, bf16[768,768]{1,0:T(8,128)(2,1)}, u32[]{:S(2)}, u32[]{:S(2)}) collective-permute-start(bf16[768,768]{1,0:T(8,128)(2,1)} %get-tuple-element.262), channel_id=1, source_target_pairs={{0,2},{2,0},{4,6},{6,4},{8,10},{10,8},{12,14},{14,12},{16,18},{18,... | collective-permute-start | bytes 3538952 | tf_op jit(solution)/shard_map/ppermute | solution.py:895
  156.5 19.1 %collective-permute-start.14 = (bf16[768,768]{1,0:T(8,128)(2,1)}, bf16[768,768]{1,0:T(8,128)(2,1)}, u32[]{:S(2)}, u32[]{:S(2)}) collective-permute-start(bf16[768,768]{1,0:T(8,128)(2,1)} %get-tuple-element.263), channel_id=1, source_target_pairs={{0,2},{2,0},{4,6},{6,4},{8,10},{10,8},{12,14},{14,12},{16,18},{18,... | collective-permute-start | bytes 3538952 | tf_op jit(solution)/shard_map/ppermute | solution.py:895
  159.9 15.7 %collective-permute-start.15 = (bf16[384,768]{1,0:T(8,128)(2,1)}, bf16[384,768]{1,0:T(8,128)(2,1)}, u32[]{:S(2)}, u32[]{:S(2)}) collective-permute-start(bf16[384,768]{1,0:T(8,128)(2,1)} %get-tuple-element.384), channel_id=1, source_target_pairs={{0,4},{2,6},{4,0},{6,2},{8,12},{10,14},{12,8},{14,10},{16,20},{18,... | collective-permute-start | bytes 1769480 | tf_op jit(solution)/shard_map/ppermute | solution.py:905
  178.6 28.3 %collective-permute-start.17 = (bf16[768,768]{1,0:T(8,128)(2,1)}, bf16[768,768]{1,0:T(8,128)(2,1)}, u32[]{:S(2)}, u32[]{:S(2)}) collective-permute-start(bf16[768,768]{1,0:T(8,128)(2,1)} %add_convert_fusion.2), channel_id=1, source_target_pairs={{0,1},{1,0},{2,3},{3,2},{4,5},{5,4},{6,7},{7,6},{8,9},{9,8},{10,11... | collective-permute-start | bytes 3538952 | tf_op jit(solution)/shard_map/ppermute | solution.py:955
  182.0 14.7 %collective-permute-start.16 = (bf16[384,768]{1,0:T(8,128)(2,1)}, bf16[384,768]{1,0:T(8,128)(2,1)}, u32[]{:S(2)}, u32[]{:S(2)}) collective-permute-start(bf16[384,768]{1,0:T(8,128)(2,1)} %get-tuple-element.382), channel_id=1, source_target_pairs={{0,4},{2,6},{4,0},{6,2},{8,12},{10,14},{12,8},{14,10},{16,20},{18,... | collective-permute-start | bytes 1769480 | tf_op jit(solution)/shard_map/ppermute | solution.py:905
  207.0 25.0 %collective-permute-start.20 = (bf16[384,768]{1,0:T(8,128)(2,1)}, bf16[384,768]{1,0:T(8,128)(2,1)}, u32[]{:S(2)}, u32[]{:S(2)}) collective-permute-start(bf16[384,768]{1,0:T(8,128)(2,1)} %add_convert_fusion.10), channel_id=1, source_target_pairs={{0,1},{1,0},{2,3},{3,2},{4,5},{5,4},{6,7},{7,6},{8,9},{9,8},{10,11... | collective-permute-start | bytes 1769480 | tf_op jit(solution)/shard_map/ppermute | solution.py:955
  212.0 20.1 %collective-permute-start.19 = (bf16[384,768]{1,0:T(8,128)(2,1)}, bf16[384,768]{1,0:T(8,128)(2,1)}, u32[]{:S(2)}, u32[]{:S(2)}) collective-permute-start(bf16[384,768]{1,0:T(8,128)(2,1)} %get-tuple-element.380), channel_id=1, source_target_pairs={{0,4},{2,6},{4,0},{6,2},{8,12},{10,14},{12,8},{14,10},{16,20},{18,... | collective-permute-start | bytes 1769480 | tf_op jit(solution)/shard_map/ppermute | solution.py:905
  214.7 17.4 %collective-permute-start.21 = (bf16[128,1408]{1,0:T(8,128)(2,1)S(1)}, bf16[128,1408]{1,0:T(8,128)(2,1)}, u32[]{:S(2)}, u32[]{:S(2)}) collective-permute-start(bf16[128,1408]{1,0:T(8,128)(2,1)S(1)} %slice.49), channel_id=1, source_target_pairs={{0,1},{1,0},{2,3},{3,2},{4,5},{5,4},{6,7},{7,6},{8,9},{9,8},{10,11... | collective-permute-start | bytes 1081352 | tf_op jit(solution)/shard_map/ppermute | solution.py:955
  217.4 29.9 %collective-permute-start.23 = (bf16[256,1408]{1,0:T(8,128)(2,1)}, bf16[256,1408]{1,0:T(8,128)(2,1)}, u32[]{:S(2)}, u32[]{:S(2)}) collective-permute-start(bf16[256,1408]{1,0:T(8,128)(2,1)} %slice.50), channel_id=1, source_target_pairs={{0,1},{1,0},{2,3},{3,2},{4,5},{5,4},{6,7},{7,6},{8,9},{9,8},{10,11... | collective-permute-start | bytes 2162696 | tf_op jit(solution)/shard_map/ppermute | solution.py:955
  237.7 14.9 %collective-permute-start.22 = (bf16[384,768]{1,0:T(8,128)(2,1)}, bf16[384,768]{1,0:T(8,128)(2,1)}, u32[]{:S(2)}, u32[]{:S(2)}) collective-permute-start(bf16[384,768]{1,0:T(8,128)(2,1)} %get-tuple-element.378), channel_id=1, source_target_pairs={{0,8},{2,10},{4,12},{6,14},{8,0},{10,2},{12,4},{14,6},{16,24},{18,... | collective-permute-start | bytes 1769480 | tf_op jit(solution)/shard_map/ppermute | solution.py:905
  258.9 20.4 %collective-permute-start.25 = (bf16[192,1408]{1,0:T(8,128)(2,1)}, bf16[192,1408]{1,0:T(8,128)(2,1)}, u32[]{:S(2)}, u32[]{:S(2)}) collective-permute-start(bf16[192,1408]{1,0:T(8,128)(2,1)} %get-tuple-element.386), channel_id=1, source_target_pairs={{0,4},{2,6},{4,0},{6,2},{8,12},{10,14},{12,8},{14,10},{16,20},{18,... | collective-permute-start | bytes 1622024 | tf_op jit(solution)/shard_map/ppermute | solution.py:905
  261.8 17.5 %collective-permute-start.26 = (bf16[192,768]{1,0:T(8,128)(2,1)}, bf16[192,768]{1,0:T(8,128)(2,1)S(1)}, u32[]{:S(2)}, u32[]{:S(2)}) collective-permute-start(bf16[192,768]{1,0:T(8,128)(2,1)} %get-tuple-element.392), channel_id=1, source_target_pairs={{0,16},{2,18},{4,20},{6,22},{8,24},{10,26},{12,28},{14,30},{16,0},... | collective-permute-start | bytes 884744 | tf_op jit(solution)/shard_map/ppermute | solution.py:905
  264.4 24.1 %collective-permute-start.27 = (bf16[384,768]{1,0:T(8,128)(2,1)}, bf16[384,768]{1,0:T(8,128)(2,1)}, u32[]{:S(2)}, u32[]{:S(2)}) collective-permute-start(bf16[384,768]{1,0:T(8,128)(2,1)} %get-tuple-element.325), channel_id=1, source_target_pairs={{0,1},{1,0},{2,3},{3,2},{4,5},{5,4},{6,7},{7,6},{8,9},{9,8},{10,11... | collective-permute-start | bytes 1769480 | tf_op jit(solution)/shard_map/ppermute | solution.py:955
  287.4 18.3 %collective-permute-start.31 = (bf16[192,768]{1,0:T(8,128)(2,1)S(1)}, bf16[192,768]{1,0:T(8,128)(2,1)}, u32[]{:S(2)}, u32[]{:S(2)}) collective-permute-start(bf16[192,768]{1,0:T(8,128)(2,1)S(1)} %add_convert_fusion.12), channel_id=1, source_target_pairs={{0,16},{2,18},{4,20},{6,22},{8,24},{10,26},{12,28},{14,30},{16,0},... | collective-permute-start | bytes 884744 | tf_op jit(solution)/shard_map/ppermute | solution.py:905
  291.8 14.0 %collective-permute-start.30 = (f32[1,6784]{1,0:T(1,128)S(1)}, f32[1,6784]{1,0:T(1,128)S(1)}, u32[]{:S(2)}, u32[]{:S(2)}) collective-permute-start(f32[1,6784]{1,0:T(1,128)S(1)} %add.232), channel_id=1, source_target_pairs={{0,2},{2,0},{4,6},{6,4},{8,10},{10,8},{12,14},{14,12},{16,18},{18,... | collective-permute-start | bytes 81416 | tf_op jit(solution)/shard_map/ppermute | solution.py:895
  297.6 10.6 %collective-permute-start.32 = (bf16[48,1408]{1,0:T(8,128)(2,1)}, bf16[48,1408]{1,0:T(8,128)(2,1)S(1)}, u32[]{:S(2)}, u32[]{:S(2)}) collective-permute-start(bf16[48,1408]{1,0:T(8,128)(2,1)} %get-tuple-element.398), channel_id=1, source_target_pairs={{0,16},{2,18},{4,20},{6,22},{8,24},{10,26},{12,28},{14,30},{16,0},... | collective-permute-start | bytes 405512 | tf_op jit(solution)/shard_map/ppermute | solution.py:905
  307.0 13.8 %collective-permute-start.34 = (bf16[384,768]{1,0:T(8,128)(2,1)S(1)}, bf16[384,768]{1,0:T(8,128)(2,1)S(1)}, u32[]{:S(2)}, u32[]{:S(2)}) collective-permute-start(bf16[384,768]{1,0:T(8,128)(2,1)S(1)} %pad_maximum_fusion.5), channel_id=1, source_target_pairs={{0,8},{2,10},{4,12},{6,14},{8,0},{10,2},{12,4},{14,6},{16,24},{18,... | collective-permute-start | bytes 1769480 | tf_op jit(solution)/shard_map/ppermute | solution.py:905
  320.9 15.3 %collective-permute-start.36 = (bf16[384,768]{1,0:T(8,128)(2,1)S(1)}, bf16[384,768]{1,0:T(8,128)(2,1)S(1)}, u32[]{:S(2)}, u32[]{:S(2)}) collective-permute-start(bf16[384,768]{1,0:T(8,128)(2,1)S(1)} %get-tuple-element.348), channel_id=1, source_target_pairs={{0,4},{2,6},{4,0},{6,2},{8,12},{10,14},{12,8},{14,10},{16,20},{18,... | collective-permute-start | bytes 1769480 | tf_op jit(solution)/shard_map/ppermute | solution.py:905
  322.2 13.9 %collective-permute-start.35 = (bf16[112,1408]{1,0:T(8,128)(2,1)S(1)}, bf16[112,1408]{1,0:T(8,128)(2,1)S(1)}, u32[]{:S(2)}, u32[]{:S(2)}) collective-permute-start(bf16[112,1408]{1,0:T(8,128)(2,1)S(1)} %pad_maximum_fusion.6), channel_id=1, source_target_pairs={{0,16},{2,18},{4,20},{6,22},{8,24},{10,26},{12,28},{14,30},{16,0},... | collective-permute-start | bytes 946184 | tf_op jit(solution)/shard_map/ppermute | solution.py:905
  322.3 18.9 %collective-permute-start.37 = (bf16[512,768]{1,0:T(8,128)(2,1)S(1)}, bf16[512,768]{1,0:T(8,128)(2,1)}, u32[]{:S(2)}, u32[]{:S(2)}) collective-permute-start(bf16[512,768]{1,0:T(8,128)(2,1)S(1)} %copy-done.39), channel_id=1, source_target_pairs={{1,0},{3,2},{5,4},{7,6},{9,8},{11,10},{13,12},{15,14},{17,16},{19,... | collective-permute-start | bytes 2359304 | tf_op jit(solution)/shard_map/ppermute | solution.py:1165
  337.3 16.2 %collective-permute-start.39 = (bf16[224,1408]{1,0:T(8,128)(2,1)S(1)}, bf16[224,1408]{1,0:T(8,128)(2,1)}, u32[]{:S(2)}, u32[]{:S(2)}) collective-permute-start(bf16[224,1408]{1,0:T(8,128)(2,1)S(1)} %pad_maximum_fusion.4), channel_id=1, source_target_pairs={{0,8},{2,10},{4,12},{6,14},{8,0},{10,2},{12,4},{14,6},{16,24},{18,... | collective-permute-start | bytes 1892360 | tf_op jit(solution)/shard_map/ppermute | solution.py:905
  337.3 15.2 %collective-permute-start.40 = (bf16[384,768]{1,0:T(8,128)(2,1)S(1)}, bf16[384,768]{1,0:T(8,128)(2,1)S(1)}, u32[]{:S(2)}, u32[]{:S(2)}) collective-permute-start(bf16[384,768]{1,0:T(8,128)(2,1)S(1)} %get-tuple-element.359), channel_id=1, source_target_pairs={{0,4},{2,6},{4,0},{6,2},{8,12},{10,14},{12,8},{14,10},{16,20},{18,... | collective-permute-start | bytes 1769480 | tf_op jit(solution)/shard_map/ppermute | solution.py:905
  (52 other events, 276.9 us)

commit v4 on v3

--- a/solution.py
+++ b/solution.py
@@ -58,7 +58,7 @@
             t_s[pair, DH:, :] = s_ref[pair * DH : (pair + 1) * DH, :]
 
 
-def attend_forward_kernel(pairs, x_ref, s_ref, kseg_ref, qseg_ref, o_ref, lse_ref, t_s):
+def attend_forward_kernel(pairs, x_ref, s_ref, kseg_ref, qseg_ref, o_ref, lse_ref, turned_ref, t_s):
     o_blocks = o_ref.shape[0] // QB
     pair_values(x_ref, s_ref, t_s, pairs)
 
@@ -80,12 +80,14 @@
         probs = (expon * (1.0 / total)).astype(BF)
         out = dot_nn(t_s[pair, :, win], probs)
         out = jnp.concatenate([out[:DH, :QB], out[DH:, QB:]], axis=0)
+        turned_ref[cols, here] = out
         o_ref[here, cols] = out.T.astype(BF)
         lse_ref[0, block, pair : pair + 1, :] = largest + jnp.log(total)
 
 
 def attend_backward_kernel(
-    pairs, x_ref, s_ref, kseg_ref, qseg_ref, lse_ref, g_ref, dx_ref, ds_ref, v_s, t_s, dk_s, dv_s
+    pairs, x_ref, s_ref, kseg_ref, qseg_ref, lse_ref, turned_ref, g_ref, dx_ref, ds_ref,
+    v_s, t_s, dk_s, dv_s,
 ):
     o_blocks = g_ref.shape[0] // QB
     pair_values(x_ref, s_ref, t_s, pairs)
@@ -112,7 +114,8 @@
         scores = dot_nt(x_ref[win, key_cols], queries) + bias
         probs = jnp.exp(scores - lse_ref[0, block, pair : pair + 1, :])
         prob_grad = dot_nt(v_s[pair, win], grads)
-        row_total = jnp.sum(probs * prob_grad, axis=0, keepdims=True)
+        terms = g_ref[here, cols].T.astype(F32) * turned_ref[cols, here]
+        row_total = jnp.concatenate([down_rows(terms[:DH]), down_rows(terms[DH:])], axis=1)
         score_grad = (probs * (prob_grad - row_total)).astype(BF)
         dv_s[pair, win] += dot_nn(probs.astype(BF), grads)
         dk_s[pair, win] += dot_nn(score_grad, queries)
@@ -141,23 +144,25 @@
     qseg_spec = pl.BlockSpec((1, 1, blocks * QB), lambda r: (r, 0, 0))
     o_spec = pl.BlockSpec((blocks * QB, pairs * 128), lambda r: (r, 0))
     lse_spec = pl.BlockSpec((1, blocks, pairs, 2 * QB), lambda r: (r, 0, 0, 0))
-    return extended, x_spec, s_spec, kseg_spec, qseg_spec, o_spec, lse_spec
+    turned_spec = pl.BlockSpec((pairs * 128, blocks * QB), lambda r: (r, 0))
+    return extended, x_spec, s_spec, kseg_spec, qseg_spec, o_spec, lse_spec, turned_spec
 
 
 def attend_forward(extended_qkv, skip, kseg, qseg):
     rows, blocks, pairs = qseg.shape[0], qseg.shape[2] // QB, skip.shape[0] // DH // qseg.shape[0]
     columns = extended_qkv.shape[1]
-    extended, x_spec, s_spec, kseg_spec, qseg_spec, o_spec, lse_spec = attention_specs(
+    extended, x_spec, s_spec, kseg_spec, qseg_spec, o_spec, lse_spec, turned_spec = attention_specs(
         rows, blocks, columns, pairs
     )
     return pl.pallas_call(
         functools.partial(attend_forward_kernel, pairs),
         grid=(rows,),
         in_specs=[x_spec, s_spec, kseg_spec, qseg_spec],
-        out_specs=[o_spec, lse_spec],
+        out_specs=[o_spec, lse_spec, turned_spec],
         out_shape=[
             jax.ShapeDtypeStruct((rows * blocks * QB, pairs * 128), BF),
             jax.ShapeDtypeStruct((rows, blocks, pairs, 2 * QB), F32),
+            jax.ShapeDtypeStruct((rows * pairs * 128, blocks * QB), F32),
         ],
         scratch_shapes=[
             pltpu.VMEM((pairs, 128, extended), BF),
@@ -167,16 +172,16 @@
     )(extended_qkv, skip, kseg, qseg)
 
 
-def attend_backward(extended_qkv, skip, kseg, qseg, sums, grads):
+def attend_backward(extended_qkv, skip, kseg, qseg, sums, turned, grads):
     rows, blocks, pairs = qseg.shape[0], qseg.shape[2] // QB, skip.shape[0] // DH // qseg.shape[0]
     columns = extended_qkv.shape[1]
-    extended, x_spec, s_spec, kseg_spec, qseg_spec, o_spec, lse_spec = attention_specs(
+    extended, x_spec, s_spec, kseg_spec, qseg_spec, o_spec, lse_spec, turned_spec = attention_specs(
         rows, blocks, columns, pairs
     )
     return pl.pallas_call(
         functools.partial(attend_backward_kernel, pairs),
         grid=(rows,),
-        in_specs=[x_spec, s_spec, kseg_spec, qseg_spec, lse_spec, o_spec],
+        in_specs=[x_spec, s_spec, kseg_spec, qseg_spec, lse_spec, turned_spec, o_spec],
         out_specs=[x_spec, s_spec],
         out_shape=[
             jax.ShapeDtypeStruct((rows * extended, columns), BF),
@@ -190,7 +195,7 @@
         ],
         cost_estimate=COST,
         name="attend_backward",
-    )(extended_qkv, skip, kseg, qseg, sums, grads)
+    )(extended_qkv, skip, kseg, qseg, sums, turned, grads)
 
 
 def feed_kernel(
@@ -1009,6 +1014,7 @@
     stages = list(chips.stages())
     where = Rows(width, local, hidden_local)
 
+    out_mine = swap_tensor(block_of(out_weight, core, 2, 0))
     qkv_own, qkv_send, halo_send, skip_send, skip_own = open_step(
         at, query_weight, key_weight, value_weight.T, block_input, jnp.swapaxes(skip_values, 1, 2)
     )
@@ -1036,33 +1042,35 @@
     query_seg = query_seg.reshape(rows, 1, length)
     key_seg = key_seg.reshape(rows, SPAN + length, 1)
 
-    out_piece = block_of(out_weight, core, 2, 0)
     down_piece = block_of(down_weight, core, 2, 0)
     up_piece = block_of(up_weight, core, 2, 1)
-    key_seg, query_seg, normed, row_vectors, qkv_send, out_piece, down_piece, up_piece = together(
-        key_seg, query_seg, normed, row_vectors, qkv_send, out_piece, down_piece, up_piece
-    )
+    key_seg, query_seg, normed, row_vectors, qkv_send, out_mine, down_piece, up_piece = together(
+        key_seg, query_seg, normed, row_vectors, qkv_send, out_mine, down_piece, up_piece
+    )
+    out_theirs = chips.swap_core(out_mine)
     qkv_mine = swap_tensor(qkv_send)
     rows_other = swap_tensor(after(row_vectors, qkv_send))
 
     normed_ext, qkv_l = project_own(where, normed, halo, row_vectors, qkv_own, rows)
-    qkv_l, skip_send, qkv_mine, rows_other = together(qkv_l, skip_send, qkv_mine, rows_other)
+    lines = skip_send.shape[0] // 2
+    qkv_l, skip_send_1, skip_send_2, out_theirs = together(
+        qkv_l, skip_send[:lines], skip_send[lines:], out_theirs
+    )
+    skip_got_1 = swap_tensor(skip_send_1)
+    mixed_l, sums_l, turned_l = attend_forward(qkv_l, skip_own, key_seg, query_seg)
+    mixed_l, skip_got_1, qkv_mine, rows_other, skip_send_2 = together(
+        mixed_l, skip_got_1, qkv_mine, rows_other, skip_send_2
+    )
+    skip_got_2 = swap_tensor(skip_send_2)
     qkv_theirs = chips.swap_core(qkv_mine)
-    skip_got = swap_tensor(skip_send)
-    mixed_l, sums_l = attend_forward(qkv_l, skip_own, key_seg, query_seg)
-    mixed_l, qkv_theirs, skip_got, out_piece, down_piece = together(
-        mixed_l, qkv_theirs, skip_got, out_piece, down_piece
-    )
-    out_mine = swap_tensor(out_piece)
     qkv_r = project_other(
         where, at, after(normed_ext, mixed_l), qkv_mine, qkv_theirs, rows_other, rows
     )
-    qkv_r, out_mine, down_piece, up_piece = together(qkv_r, out_mine, down_piece, up_piece)
+    qkv_r, skip_got_2, down_piece, up_piece = together(qkv_r, skip_got_2, down_piece, up_piece)
     down_r1 = swap_tensor(down_piece)
-    out_theirs = chips.swap_core(out_mine)
-    up_r1 = swap_tensor(up_piece)
-    mixed_r, sums_r = attend_forward(qkv_r, skip_got, key_seg, query_seg)
-    mixed_r, out_theirs = together(mixed_r, out_theirs)
+    up_r1 = swap_tensor(after(up_piece, down_piece))
+    skip_got = jnp.concatenate([skip_got_1, skip_got_2], axis=0)
+    mixed_r, sums_r, turned_r = attend_forward(qkv_r, skip_got, key_seg, query_seg)
     hidden, normed_two, out_other = middle(
         where, at, mixed_l, mixed_r, out_weight, out_mine, out_theirs,
         block_input.reshape(tokens, width), row_vectors,
@@ -1090,16 +1098,17 @@
     up_c_r, down_c_r = chips.swap_core(up_g_r2), chips.swap_core(down_g_r2)
     up_l, down_l = add(up_g_l1, up_c_l), add(down_g_l1, down_c_l)
     down_lx = chips.scatter_start(down_l, stages[0])
+    up_c_r, down_c_r, up_l, down_l = together(up_c_r, down_c_r, up_l, down_l)
+    up_sum_r, down_sum_r = add(up_g_r1, up_c_r), add(down_g_r1, down_c_r)
+    up_t = swap_tensor(up_sum_r)
+    down_rx = chips.scatter_start(down_sum_r, stages[0])
     hidden_grad, mixed_g_l, mixed_g_r, out_g_l, out_g_r, middle_sums = middle_back(
-        where, b_l, b_r, hidden, out_grad, mixed_l, mixed_r, out_weight, out_other, row_vectors
-    )
-    mixed_g_r, up_c_r, down_c_r, down_lx = together(mixed_g_r, up_c_r, down_c_r, down_lx)
-
-    up_sum_r, down_sum_r = add(up_g_r1, up_c_r), add(down_g_r1, down_c_r)
-    down_rx = chips.scatter_start(down_sum_r, stages[0])
-    up_t = swap_tensor(up_sum_r)
+        where, b_l, after(b_r, up_sum_r, down_sum_r), hidden, out_grad, mixed_l, mixed_r,
+        out_weight, out_other, row_vectors,
+    )
+    mixed_g_r, down_lx = together(mixed_g_r, down_lx)
     qkv_g_r, skip_g_r = attend_backward(
-        qkv_r, skip_got, key_seg, query_seg, sums_r, after(mixed_g_r, up_sum_r, down_sum_r)
+        qkv_r, skip_got, key_seg, query_seg, sums_r, turned_r, mixed_g_r
     )
     qkv_g_r, skip_g_r, down_rx = together(qkv_g_r, skip_g_r, down_rx)
 
@@ -1112,13 +1121,15 @@
     qkv_c_r = chips.swap_core(qkv_send_r)
     up_1 = add(up_l, up_t)
     up_x = chips.scatter_start(up_1, stages[0])
-    qkv_y = add(qkv_keep_r, qkv_c_r)
-    qkv_t_1 = swap_tensor(qkv_y[: width // 6])
+    lead = width // 6
+    qkv_y_1 = add(qkv_keep_r[:lead], qkv_c_r[:lead])
+    qkv_y_2 = add(qkv_keep_r[lead:], qkv_c_r[lead:])
+    qkv_t_1 = swap_tensor(qkv_y_1)
     qkv_g_l, skip_g_l = attend_backward(
-        qkv_l, skip_own, key_seg, query_seg, sums_l, after(mixed_g_l, up_1, qkv_y)
+        qkv_l, skip_own, key_seg, query_seg, sums_l, turned_l, after(mixed_g_l, up_1, qkv_y_1, qkv_y_2)
     )
     qkv_g_l, skip_g_l, up_x, down_t, qkv_t_1 = together(qkv_g_l, skip_g_l, up_x, down_t, qkv_t_1)
-    qkv_t_2 = swap_tensor(qkv_y[width // 6 :])
+    qkv_t_2 = swap_tensor(qkv_y_2)
 
     def rest(value):
         for stage in stages[3:]:
@@ -1140,9 +1151,14 @@
     qkv_c_l = chips.swap_core(qkv_send_l)
     feed_3 = add(*feed_x)
     feed_x = chips.scatter_start(feed_3, stages[2])
-    qkv_t = jnp.concatenate([qkv_t_1, qkv_t_2], axis=0)
-
-    qkv_1 = add(qkv_keep_l, qkv_c_l, qkv_t)
+
+    qkv_1 = jnp.concatenate(
+        [
+            add(qkv_keep_l[:lead], qkv_c_l[:lead], qkv_t_1),
+            add(qkv_keep_l[lead:], qkv_c_l[lead:], qkv_t_2),
+        ],
+        axis=0,
+    )
     qkv_x = chips.scatter_start(qkv_1, stages[0])
     skip_back = swap_tensor(after(skip_g_r, qkv_1))
     input_grad, halo_grad, first_sums = first_back(

time: 376 us -> 368 us (0.979)
  waiting for transfers between devices: 74.8 us -> 65.7 us
  other arithmetic: 36.7 us -> 45 us
  Pallas kernels: 194 us -> 190 us
    ppermute x12 -> x13, waiting for transfers between devices: 13.7 us -> 7.72 us  [swap_tensor(): return lax.ppermute(value, 'tensor', [(0, 1), (1, 0)])]
    convert_element_type x14 -> x17, other arithmetic: 21.4 us -> 26.9 us  [add(): return total.astype(BF)]
    pallas_call x2, Pallas kernels: 26.4 us -> 21.7 us  [attend_backward(): pl.pallas_call(functools.partial(attend_backward_kernel, pairs), grid=(ro...]
    ppermute x15, waiting for transfers between devices: 43 us -> 38.7 us  [shift(): return lax.ppermute(value, 'dp', perm)]
    ppermute x12 -> x13, starting transfers between devices: 14.6 us -> 15.7 us  [swap_tensor(): return lax.ppermute(value, 'tensor', [(0, 1), (1, 0)])]
  transfers between devices with their start and end apart: 43 -> 44, of which waited for: 18 -> 18; matrix products, arithmetic and copies ran while one was open for 12% -> 15% of each run, Pallas kernels for 49% -> 51%
where the time goes in v4:
time: 368 us; the launch traced here: 364 us
  Pallas kernels  190 us (52%)
  waiting for transfers between devices  65.7 us (18%)
  other arithmetic  45 us (12%)
  starting transfers between devices  38.2 us (10%)
  local copies, waits for them, and re-layouts  22.7 us (6%)
    pallas_call x2, Pallas kernels, feed(): pl.pallas_call(feed_kernel, grid_spec=pltpu.PrefetchScalarGridSpec(num_sc...  52.1 us
    ppermute x15, waiting for transfers between devices, shift(): return lax.ppermute(value, 'dp', perm)  38.7 us
    convert_element_type x17, other arithmetic, add(): return total.astype(BF)  26.9 us
    pallas_call x2, Pallas kernels, attend_forward(): pl.pallas_call(functools.partial(attend_forward_kernel, pairs), grid=(row...  26.3 us
    pallas_call x2, Pallas kernels, attend_backward(): pl.pallas_call(functools.partial(attend_backward_kernel, pairs), grid=(ro...  21.7 us
    ppermute x15, starting transfers between devices, shift(): return lax.ppermute(value, 'dp', perm)  17.1 us
    pallas_call x2, Pallas kernels, project_grad(): pl.pallas_call(project_grad_kernel, grid_spec=pltpu.PrefetchScalarGridSpe...  16.1 us
    ppermute x13, starting transfers between devices, swap_tensor(): return lax.ppermute(value, 'tensor', [(0, 1), (1, 0)])  15.7 us
  transfers between devices with their start and end apart: 44, of which 18 were waited for; matrix products, arithmetic and copies ran while one was open for 15% of the time, Pallas kernels for 51%

profile of v4, /device:TPU:0, one launch (start us, length us, event | category | flops | bytes accessed | tf_op | source)
XLA Modules:
  0.0 363.7 jit_solution(10026607297693195943)
XLA Ops:
  2.4 3.0 collective-permute-start
  6.0 5.1 %open.1 = (bf16[768,1024]{1,0:T(8,128)(2,1)}, bf16[384,1024]{1,0:T(8,128)(2,1)}, bf16[512,768]{1,0:T(8,128)(2,1)}, bf16[384,768]{1,0:T(8,128)(2,1)}, bf16[384,768]{1,0:T(8,128)(2,1)}) custom-call(s32[2]{0:T(128)} %pad_add_fusion.at_ref.core_ref, bf16[768,384]{1,0:T(8,128)(2,1)} %qw_ref.1, bf16[768,384]{1,0:T(8,128)(2,1)} %kw_ref.1, ...), custom_call_target="tpu_custom_call" | custom-call | flops 1048576 | bytes 1048576 | tf_op jit(solution)/shard_map/open/pallas_call | solution.py:386
  15.6 3.2 constant_dynamic-slice_fusion.12
  21.4 9.8 %collective-permute-done.1.h_ref = bf16[512,768]{1,0:T(8,128)(2,1)S(1)} collective-permute-done((bf16[512,768]{1,0:T(8,128)(2,1)}, bf16[512,768]{1,0:T(8,128)(2,1)S(1)}, u32[]{:S(2)}, u32[]{:S(2)}) %collective-permute-start.1) | collective-permute-done | bytes 786464 | tf_op jit(solution)/shard_map/ppermute | solution.py:1021
  32.2 6.5 %project_own.1 = (bf16[1536,768]{1,0:T(8,128)(2,1)}, bf16[1536,1024]{1,0:T(8,128)(2,1)}) custom-call(bf16[1024,768]{1,0:T(8,128)(2,1)} %bitcast.18, bf16[512,768]{1,0:T(8,128)(2,1)} %copy-done.8, f32[1,6784]{1,0:T(1,128)} %reshape.86.rows_ref.ba_ref.bb_ref, bf16[768,1024]{1,0:T(8,128)(2,1)} %get-tuple-element.201.w_ref.wl_ref), custom_call_target="tpu_custom_call" | custom-call | flops 1048576 | bytes 1048576 | tf_op jit(solution)/shard_map/project_own/pallas_call | solution.py:438
  42.3 13.1 %attend_forward.2 = (bf16[1024,384]{1,0:T(8,128)(2,1)}, f32[2,4,3,256]{3,2,1,0:T(4,128)}, f32[768,512]{1,0:T(8,128)}) custom-call(bf16[1536,1024]{1,0:T(8,128)(2,1)} %get-tuple-element.205.x_ref, bf16[384,768]{1,0:T(8,128)(2,1)} %get-tuple-element.206.s_ref, s32[2,768,1]{2,1,0:T(8,128)} %copy.39.kseg_ref, s32[2,1,512]{2,1,0:T(1,128)} %reshape.84.qseg_ref), custom_call_target="tpu_custom_call" | custom-call | flops 1048576 | bytes 1048576 | tf_op jit(solution)/shard_map/attend_forward/pallas_call | solution.py:157
  58.7 6.5 %project_other.1.x_ref = bf16[1536,1024]{1,0:T(8,128)(2,1)} custom-call(s32[2]{0:T(128)} %pad_add_fusion.at_ref.core_ref, bf16[1536,768]{1,0:T(8,128)(2,1)} %get-tuple-element.297.ne_ref.n_ref, bf16[384,1024]{1,0:T(8,128)(2,1)} %copy-done.6, bf16[384,1024]{1,0:T(8,128)(2,1)} %copy-done.7, f32[1,6784]{1,0:T(1,128)} %copy-done.29), custom_call_target="tpu_custom_call" | custom-call | flops 1048576 | bytes 1048576 | tf_op jit(solution)/shard_map/project_other/pallas_call | solution.py:473
  68.3 13.2 %attend_forward.3 = (bf16[1024,384]{1,0:T(8,128)(2,1)}, f32[2,4,3,256]{3,2,1,0:T(4,128)}, f32[768,512]{1,0:T(8,128)}) custom-call(bf16[1536,1024]{1,0:T(8,128)(2,1)} %project_other.1.x_ref, bf16[384,768]{1,0:T(8,128)(2,1)} %copy-done.5, s32[2,768,1]{2,1,0:T(8,128)} %copy.39.kseg_ref, s32[2,1,512]{2,1,0:T(1,128)} %reshape.84.qseg_ref), custom_call_target="tpu_custom_call" | custom-call | flops 1048576 | bytes 1048576 | tf_op jit(solution)/shard_map/attend_forward/pallas_call | solution.py:157
  81.5 7.2 %middle.1 = (f32[1024,768]{1,0:T(8,128)}, bf16[1024,768]{1,0:T(8,128)(2,1)}, bf16[384,768]{1,0:T(8,128)(2,1)}) custom-call(s32[2]{0:T(128)} %pad_add_fusion.at_ref.core_ref, bf16[1024,384]{1,0:T(8,128)(2,1)} %get-tuple-element.214.ml_ref, bf16[1024,384]{1,0:T(8,128)(2,1)} %get-tuple-element.225.mr_ref, bf16[384,768]{1,0:T(8,128)(2,1)} %wl_ref.3, ...), custom_call_target="tpu_custom_call" | custom-call | flops 1048576 | bytes 1048576 | tf_op jit(solution)/shard_map/middle/pallas_call | solution.py:508
  88.6 26.0 %feed.2 = (bf16[768,768]{1,0:T(8,128)(2,1)}, bf16[768,768]{1,0:T(8,128)(2,1)}, bf16[768,768]{1,0:T(8,128)(2,1)}, bf16[768,768]{1,0:T(8,128)(2,1)}, f32[1,768]{1,...) custom-call(s32[2]{0:T(128)} %pad_add_fusion.at_ref.core_ref, ...), custom_call_target="tpu_custom_call" | custom-call | flops 1048576 | bytes 1048576 | tf_op jit(solution)/shard_map/feed/pallas_call | solution.py:319
  114.6 4.4 %collective-permute-done.9.ub_ref = bf16[768,768]{1,0:T(8,128)(2,1)} collective-permute-done((bf16[768,768]{1,0:T(8,128)(2,1)S(1)}, bf16[768,768]{1,0:T(8,128)(2,1)}, u32[]{:S(2)}, u32[]{:S(2)}) %collective-permute-start.9) | collective-permute-done | bytes 1179680 | tf_op jit(solution)/shard_map/ppermute | solution.py:960
  124.7 26.1 %feed.3 = (bf16[768,768]{1,0:T(8,128)(2,1)}, bf16[768,768]{1,0:T(8,128)(2,1)}, bf16[768,768]{1,0:T(8,128)(2,1)}, bf16[768,768]{1,0:T(8,128)(2,1)}, f32[1,768]{1,...) custom-call(s32[2]{0:T(128)} %pad_add_fusion.at_ref.core_ref, ...), custom_call_target="tpu_custom_call" | custom-call | flops 1048576 | bytes 1048576 | tf_op jit(solution)/shard_map/feed/pallas_call | solution.py:319
  166.9 11.8 %middle_back.1 = (f32[1024,768]{1,0:T(8,128)}, bf16[1024,384]{1,0:T(8,128)(2,1)}, bf16[1024,384]{1,0:T(8,128)(2,1)}, bf16[768,384]{1,0:T(8,128)(2,1)}, bf16[768,384]{1,0:T(8,128)(2,1)}, /*index=5*/f32[8,768]{1,0:T(8,128)}) custom-call(f32[1024,768]{1,0:T(8,128)} %get-tuple-element.236.bl_ref, f32[1024,768]{1,0:T(8,128)} %get-tuple-element.265.br_ref, ...), custom_call_target="tpu_custom_call" | custom-call | flops 1048576 | bytes 1048576 | tf_op jit(solution)/shard_map/middle_back/pallas_call | solution.py:584
  178.7 10.7 %attend_backward.2 = (bf16[1536,1024]{1,0:T(8,128)(2,1)}, bf16[384,768]{1,0:T(8,128)(2,1)}) custom-call(bf16[1536,1024]{1,0:T(8,128)(2,1)} %project_other.1.x_ref, bf16[384,768]{1,0:T(8,128)(2,1)} %copy-done.5, s32[2,768,1]{2,1,0:T(8,128)} %copy.39.kseg_ref, s32[2,1,512]{2,1,0:T(1,128)} %reshape.84.qseg_ref, f32[2,4,3,256]{3,2,1,0:T(4,128)} %get-tuple-element.272.lse_ref, ...), custom_call_target="tpu_custom_call" | custom-call | flops 1048576 | bytes 1048576 | tf_op jit(solution)/shard_map/attend_backward/pallas_call | solution.py:181
  191.7 8.0 %project_grad.2 = (bf16[384,1408]{1,0:T(8,128)(2,1)}, bf16[384,1408]{1,0:T(8,128)(2,1)}, f32[1,1024]{1,0:T(1,128)}) custom-call(s32[2]{0:T(128)} %pad_add_fusion.at_ref.core_ref, bf16[1536,768]{1,0:T(8,128)(2,1)} %get-tuple-element.297.ne_ref.n_ref, bf16[1536,1024]{1,0:T(8,128)(2,1)} %get-tuple-element.281.d_ref.dr_ref, ...), custom_call_target="tpu_custom_call" | custom-call | flops 1048576 | bytes 1048576 | tf_op jit(solution)/shard_map/project_grad/pallas_call | solution.py:630
  210.1 10.9 %attend_backward.3 = (bf16[1536,1024]{1,0:T(8,128)(2,1)}, bf16[384,768]{1,0:T(8,128)(2,1)}) custom-call(bf16[1536,1024]{1,0:T(8,128)(2,1)} %get-tuple-element.205.x_ref, bf16[384,768]{1,0:T(8,128)(2,1)} %get-tuple-element.206.s_ref, s32[2,768,1]{2,1,0:T(8,128)} %copy.39.kseg_ref, s32[2,1,512]{2,1,0:T(1,128)} %reshape.84.qseg_ref, ...), custom_call_target="tpu_custom_call" | custom-call | flops 1048576 | bytes 1048576 | tf_op jit(solution)/shard_map/attend_backward/pallas_call | solution.py:181
  221.0 3.1 collective-permute-done.22
  231.3 8.0 %project_grad.3 = (bf16[384,1408]{1,0:T(8,128)(2,1)}, bf16[384,1408]{1,0:T(8,128)(2,1)}, f32[1,1024]{1,0:T(1,128)}) custom-call(s32[2]{0:T(128)} %pad_add_fusion.at_ref.core_ref, bf16[1536,768]{1,0:T(8,128)(2,1)} %get-tuple-element.297.ne_ref.n_ref, bf16[1536,1024]{1,0:T(8,128)(2,1)} %get-tuple-element.308.d_ref.dl_ref, ...), custom_call_target="tpu_custom_call" | custom-call | flops 1048576 | bytes 1048576 | tf_op jit(solution)/shard_map/project_grad/pallas_call | solution.py:630
  239.3 4.9 %collective-permute-done.23 = bf16[384,768]{1,0:T(8,128)(2,1)} collective-permute-done((bf16[384,768]{1,0:T(8,128)(2,1)}, bf16[384,768]{1,0:T(8,128)(2,1)}, u32[]{:S(2)}, u32[]{:S(2)}) %collective-permute-start.23) | collective-permute-done | bytes 589856 | tf_op jit(solution)/shard_map/ppermute | solution.py:910
  244.2 3.0 collective-permute-done.25
  258.4 13.9 %first_back.1 = (f32[1024,768]{1,0:T(8,128)}, bf16[512,768]{1,0:T(8,128)(2,1)}, f32[8,768]{1,0:T(8,128)}) custom-call(s32[2]{0:T(128)} %pad_add_fusion.at_ref.core_ref, bf16[1536,1024]{1,0:T(8,128)(2,1)} %get-tuple-element.308.d_ref.dl_ref, bf16[1536,1024]{1,0:T(8,128)(2,1)} %get-tuple-element.281.d_ref.dr_ref, ...), custom_call_target="tpu_custom_call" | custom-call | flops 1048576 | bytes 1048576 | tf_op jit(solution)/shard_map/first_back/pallas_call | solution.py:685
  281.6 3.2 skip_grad.1
  286.8 3.9 %add.246 = f32[1024,768]{1,0:T(8,128)} add(f32[1024,768]{1,0:T(8,128)S(1)} %add_add_fusion, f32[1024,768]{1,0:T(8,128)} %get-tuple-element.334) | non-fusion elementwise | flops 786432 | bytes 9437184 | tf_op jit(solution)/shard_map/add | solution.py:1188
  293.2 6.9 %collective-permute-done.32 = bf16[192,768]{1,0:T(8,128)(2,1)} collective-permute-done((bf16[192,768]{1,0:T(8,128)(2,1)S(1)}, bf16[192,768]{1,0:T(8,128)(2,1)}, u32[]{:S(2)}, u32[]{:S(2)}) %collective-permute-start.32) | collective-permute-done | bytes 294944 | tf_op jit(solution)/shard_map/ppermute | solution.py:910
  302.6 4.7 %collective-permute-done.34 = bf16[56,1408]{1,0:T(8,128)(2,1)S(1)} collective-permute-done((bf16[56,1408]{1,0:T(8,128)(2,1)S(1)}, bf16[56,1408]{1,0:T(8,128)(2,1)S(1)}, u32[]{:S(2)}, u32[]{:S(2)}) %collective-permute-start.34) | collective-permute-done | bytes 157728 | tf_op jit(solution)/shard_map/ppermute | solution.py:910
  307.3 7.2 %collective-permute-done.35 = bf16[384,768]{1,0:T(8,128)(2,1)S(1)} collective-permute-done((bf16[384,768]{1,0:T(8,128)(2,1)S(1)}, bf16[384,768]{1,0:T(8,128)(2,1)S(1)}, u32[]{:S(2)}, u32[]{:S(2)}) %collective-permute-start.35) | collective-permute-done | bytes 589856 | tf_op jit(solution)/shard_map/ppermute | solution.py:910
  317.2 11.0 %collective-permute-done.36 = bf16[112,1408]{1,0:T(8,128)(2,1)S(1)} collective-permute-done((bf16[112,1408]{1,0:T(8,128)(2,1)S(1)}, bf16[112,1408]{1,0:T(8,128)(2,1)S(1)}, u32[]{:S(2)}, u32[]{:S(2)}) %collective-permute-start.36) | collective-permute-done | bytes 315424 | tf_op jit(solution)/shard_map/ppermute | solution.py:910
  330.9 3.3 collective-permute-done.38.got_ref
  336.7 5.1 %up_out.1 = f32[768,1536]{1,0:T(8,128)} custom-call(s32[2]{0:T(128)} %pad_add_fusion.at_ref.core_ref, bf16[768,768]{1,0:T(8,128)(2,1)} %copy-done.3, bf16[768,768]{1,0:T(8,128)(2,1)} %collective-permute-done.39.other_ref), custom_call_target="tpu_custom_call" | custom-call | flops 1048576 | bytes 1048576 | tf_op jit(solution)/shard_map/up_out/pallas_call | solution.py:827
  341.9 2.7 collective-permute-done.41
  349.9 4.7 %project_out.1 = (f32[768,384]{1,0:T(8,128)}, f32[768,384]{1,0:T(8,128)}, f32[192,768]{1,0:T(8,128)}, f32[384,768]{1,0:T(8,128)}, f32[8,1408]{1,0:T(8,128)}) custom-call(s32[2]{0:T(128)} %pad_add_fusion.at_ref.core_ref, bf16[448,1408]{1,0:T(8,128)(2,1)} %copy-done.2, bf16[448,1408]{1,0:T(8,128)(2,1)} %collective-permute-done.42.other_ref), custom_call_target="tpu_custom_call" | custom-call | flops 1048576 | bytes 1048576 | tf_op jit(solution)/shard_map/project_out/pallas_call | solution.py:870
  357.7 5.7 %down_out.1 = f32[1536,768]{1,0:T(8,128)} custom-call(s32[2]{0:T(128)} %pad_add_fusion.at_ref.core_ref, bf16[768,768]{1,0:T(8,128)(2,1)} %copy-done.4, bf16[768,768]{1,0:T(8,128)(2,1)} %collective-permute-done.43.other_ref), custom_call_target="tpu_custom_call" | custom-call | flops 1048576 | bytes 1048576 | tf_op jit(solution)/shard_map/down_out/pallas_call | solution.py:803
  (232 shorter events, 105.0 us)
Async XLA Ops:
  2.4 18.2 %collective-permute-start = (bf16[192,768]{1,0:T(8,128)(2,1)}, bf16[192,768]{1,0:T(8,128)(2,1)S(1)}, u32[]{:S(2)}, u32[]{:S(2)}) collective-permute-start(bf16[192,768]{1,0:T(8,128)(2,1)} %constant_dynamic-slice_fusion.14), channel_id=1, source_target_pairs={{0,1},{1,0},{2,3},{3,2},{4,5},{5,4},{6,7},{7,6},{8,9},{9,8},{10,11... | collective-permute-start | bytes 884744 | tf_op jit(solution)/shard_map/ppermute | solution.py:960
  11.1 20.1 %collective-permute-start.1 = (bf16[512,768]{1,0:T(8,128)(2,1)}, bf16[512,768]{1,0:T(8,128)(2,1)S(1)}, u32[]{:S(2)}, u32[]{:S(2)}) collective-permute-start(bf16[512,768]{1,0:T(8,128)(2,1)} %get-tuple-element.196), channel_id=1, source_target_pairs={{0,1},{2,3},{4,5},{6,7},{8,9},{10,11},{12,13},{14,15},{16,17},{18,... | collective-permute-start | bytes 2359304 | tf_op jit(solution)/shard_map/ppermute | solution.py:1021
  20.6 34.9 %collective-permute-start.4 = (bf16[384,1024]{1,0:T(8,128)(2,1)}, bf16[384,1024]{1,0:T(8,128)(2,1)S(1)}, u32[]{:S(2)}, u32[]{:S(2)}) collective-permute-start(bf16[384,1024]{1,0:T(8,128)(2,1)} %get-tuple-element.211), channel_id=1, source_target_pairs={{0,1},{1,0},{2,3},{3,2},{4,5},{5,4},{6,7},{7,6},{8,9},{9,8},{10,11... | collective-permute-start | bytes 2359304 | tf_op jit(solution)/shard_map/ppermute | solution.py:960
  20.6 18.1 %collective-permute-start.2 = (bf16[192,768]{1,0:T(8,128)(2,1)S(1)}, bf16[192,768]{1,0:T(8,128)(2,1)S(1)}, u32[]{:S(2)}, u32[]{:S(2)}) collective-permute-start(bf16[192,768]{1,0:T(8,128)(2,1)S(1)} %collective-permute-done.w1_ref), channel_id=1, source_target_pairs={{0,2},{2,0},{4,6},{6,4},{8,10},{10,8},{12,14},{14,12},{16,18},{18,... | collective-permute-start | bytes 884744 | tf_op jit(solution)/shard_map/ppermute | solution.py:900
  38.6 16.8 %collective-permute-start.3 = (bf16[192,768]{1,0:T(8,128)(2,1)S(1)}, bf16[192,768]{1,0:T(8,128)(2,1)S(1)}, u32[]{:S(2)}, u32[]{:S(2)}) collective-permute-start(bf16[192,768]{1,0:T(8,128)(2,1)S(1)} %get-tuple-element.210), channel_id=1, source_target_pairs={{0,1},{1,0},{2,3},{3,2},{4,5},{5,4},{6,7},{7,6},{8,9},{9,8},{10,11... | collective-permute-start | bytes 884744 | tf_op jit(solution)/shard_map/ppermute | solution.py:960
  41.1 14.4 %collective-permute-start.5 = (f32[1,6784]{1,0:T(1,128)S(1)}, f32[1,6784]{1,0:T(1,128)S(1)}, u32[]{:S(2)}, u32[]{:S(2)}) collective-permute-start(f32[1,6784]{1,0:T(1,128)S(1)} %copy-done.15), channel_id=1, source_target_pairs={{0,1},{1,0},{2,3},{3,2},{4,5},{5,4},{6,7},{7,6},{8,9},{9,8},{10,11... | collective-permute-start | bytes 81416 | tf_op jit(solution)/shard_map/ppermute | solution.py:960
  55.6 9.8 %collective-permute-start.7 = (bf16[192,768]{1,0:T(8,128)(2,1)}, bf16[192,768]{1,0:T(8,128)(2,1)S(1)}, u32[]{:S(2)}, u32[]{:S(2)}) collective-permute-start(bf16[192,768]{1,0:T(8,128)(2,1)} %get-tuple-element.219), channel_id=1, source_target_pairs={{0,1},{1,0},{2,3},{3,2},{4,5},{5,4},{6,7},{7,6},{8,9},{9,8},{10,11... | collective-permute-start | bytes 884744 | tf_op jit(solution)/shard_map/ppermute | solution.py:960
  65.4 49.2 %collective-permute-start.8 = (bf16[768,768]{1,0:T(8,128)(2,1)}, bf16[768,768]{1,0:T(8,128)(2,1)}, u32[]{:S(2)}, u32[]{:S(2)}) collective-permute-start(bf16[768,768]{1,0:T(8,128)(2,1)} %get-tuple-element.233), channel_id=1, source_target_pairs={{0,1},{1,0},{2,3},{3,2},{4,5},{5,4},{6,7},{7,6},{8,9},{9,8},{10,11... | collective-permute-start | bytes 3538952 | tf_op jit(solution)/shard_map/ppermute | solution.py:960
  67.2 51.8 %collective-permute-start.9 = (bf16[768,768]{1,0:T(8,128)(2,1)S(1)}, bf16[768,768]{1,0:T(8,128)(2,1)}, u32[]{:S(2)}, u32[]{:S(2)}) collective-permute-start(bf16[768,768]{1,0:T(8,128)(2,1)S(1)} %copy-done.19), channel_id=1, source_target_pairs={{0,1},{1,0},{2,3},{3,2},{4,5},{5,4},{6,7},{7,6},{8,9},{9,8},{10,11... | collective-permute-start | bytes 3538952 | tf_op jit(solution)/shard_map/ppermute | solution.py:960
  123.9 26.9 %collective-permute-start.12 = (bf16[768,768]{1,0:T(8,128)(2,1)}, bf16[768,768]{1,0:T(8,128)(2,1)}, u32[]{:S(2)}, u32[]{:S(2)}) collective-permute-start(bf16[768,768]{1,0:T(8,128)(2,1)} %get-tuple-element.252), channel_id=1, source_target_pairs={{0,2},{2,0},{4,6},{6,4},{8,10},{10,8},{12,14},{14,12},{16,18},{18,... | collective-permute-start | bytes 3538952 | tf_op jit(solution)/shard_map/ppermute | solution.py:900
  124.0 26.8 %collective-permute-start.13 = (bf16[768,768]{1,0:T(8,128)(2,1)}, bf16[768,768]{1,0:T(8,128)(2,1)}, u32[]{:S(2)}, u32[]{:S(2)}) collective-permute-start(bf16[768,768]{1,0:T(8,128)(2,1)} %get-tuple-element.253), channel_id=1, source_target_pairs={{0,2},{2,0},{4,6},{6,4},{8,10},{10,8},{12,14},{14,12},{16,18},{18,... | collective-permute-start | bytes 3538952 | tf_op jit(solution)/shard_map/ppermute | solution.py:900
  154.5 24.2 %collective-permute-start.16 = (bf16[384,768]{1,0:T(8,128)(2,1)}, bf16[384,768]{1,0:T(8,128)(2,1)}, u32[]{:S(2)}, u32[]{:S(2)}) collective-permute-start(bf16[384,768]{1,0:T(8,128)(2,1)} %get-tuple-element.388), channel_id=1, source_target_pairs={{0,4},{2,6},{4,0},{6,2},{8,12},{10,14},{12,8},{14,10},{16,20},{18,... | collective-permute-start | bytes 1769480 | tf_op jit(solution)/shard_map/ppermute | solution.py:910
  161.9 37.8 %collective-permute-start.18 = (bf16[768,768]{1,0:T(8,128)(2,1)}, bf16[768,768]{1,0:T(8,128)(2,1)}, u32[]{:S(2)}, u32[]{:S(2)}) collective-permute-start(bf16[768,768]{1,0:T(8,128)(2,1)} %add_convert_fusion.2), channel_id=1, source_target_pairs={{0,1},{1,0},{2,3},{3,2},{4,5},{5,4},{6,7},{7,6},{8,9},{9,8},{10,11... | collective-permute-start | bytes 3538952 | tf_op jit(solution)/shard_map/ppermute | solution.py:960
  166.4 23.1 %collective-permute-start.17 = (bf16[384,768]{1,0:T(8,128)(2,1)}, bf16[384,768]{1,0:T(8,128)(2,1)}, u32[]{:S(2)}, u32[]{:S(2)}) collective-permute-start(bf16[384,768]{1,0:T(8,128)(2,1)} %get-tuple-element.386), channel_id=1, source_target_pairs={{0,4},{2,6},{4,0},{6,2},{8,12},{10,14},{12,8},{14,10},{16,20},{18,... | collective-permute-start | bytes 1769480 | tf_op jit(solution)/shard_map/ppermute | solution.py:910
  199.8 21.1 %collective-permute-start.21 = (bf16[384,768]{1,0:T(8,128)(2,1)}, bf16[384,768]{1,0:T(8,128)(2,1)}, u32[]{:S(2)}, u32[]{:S(2)}) collective-permute-start(bf16[384,768]{1,0:T(8,128)(2,1)} %add_convert_fusion.10), channel_id=1, source_target_pairs={{0,1},{1,0},{2,3},{3,2},{4,5},{5,4},{6,7},{7,6},{8,9},{9,8},{10,11... | collective-permute-start | bytes 1769480 | tf_op jit(solution)/shard_map/ppermute | solution.py:960
  203.2 17.8 %collective-permute-start.20 = (bf16[384,768]{1,0:T(8,128)(2,1)}, bf16[384,768]{1,0:T(8,128)(2,1)}, u32[]{:S(2)}, u32[]{:S(2)}) collective-permute-start(bf16[384,768]{1,0:T(8,128)(2,1)} %get-tuple-element.384), channel_id=1, source_target_pairs={{0,4},{2,6},{4,0},{6,2},{8,12},{10,14},{12,8},{14,10},{16,20},{18,... | collective-permute-start | bytes 1769480 | tf_op jit(solution)/shard_map/ppermute | solution.py:910
  205.8 18.3 %collective-permute-start.22 = (bf16[128,1408]{1,0:T(8,128)(2,1)S(1)}, bf16[128,1408]{1,0:T(8,128)(2,1)}, u32[]{:S(2)}, u32[]{:S(2)}) collective-permute-start(bf16[128,1408]{1,0:T(8,128)(2,1)S(1)} %add_convert_fusion.13), channel_id=1, source_target_pairs={{0,1},{1,0},{2,3},{3,2},{4,5},{5,4},{6,7},{7,6},{8,9},{9,8},{10,11... | collective-permute-start | bytes 1081352 | tf_op jit(solution)/shard_map/ppermute | solution.py:960
  209.8 29.5 %collective-permute-start.24 = (bf16[256,1408]{1,0:T(8,128)(2,1)}, bf16[256,1408]{1,0:T(8,128)(2,1)}, u32[]{:S(2)}, u32[]{:S(2)}) collective-permute-start(bf16[256,1408]{1,0:T(8,128)(2,1)} %add_convert_fusion.6), channel_id=1, source_target_pairs={{0,1},{1,0},{2,3},{3,2},{4,5},{5,4},{6,7},{7,6},{8,9},{9,8},{10,11... | collective-permute-start | bytes 2162696 | tf_op jit(solution)/shard_map/ppermute | solution.py:960
  229.7 14.6 %collective-permute-start.23 = (bf16[384,768]{1,0:T(8,128)(2,1)}, bf16[384,768]{1,0:T(8,128)(2,1)}, u32[]{:S(2)}, u32[]{:S(2)}) collective-permute-start(bf16[384,768]{1,0:T(8,128)(2,1)} %get-tuple-element.382), channel_id=1, source_target_pairs={{0,8},{2,10},{4,12},{6,14},{8,0},{10,2},{12,4},{14,6},{16,24},{18,... | collective-permute-start | bytes 1769480 | tf_op jit(solution)/shard_map/ppermute | solution.py:910
  251.9 20.4 %collective-permute-start.26 = (bf16[192,1408]{1,0:T(8,128)(2,1)}, bf16[192,1408]{1,0:T(8,128)(2,1)}, u32[]{:S(2)}, u32[]{:S(2)}) collective-permute-start(bf16[192,1408]{1,0:T(8,128)(2,1)} %get-tuple-element.390), channel_id=1, source_target_pairs={{0,4},{2,6},{4,0},{6,2},{8,12},{10,14},{12,8},{14,10},{16,20},{18,... | collective-permute-start | bytes 1622024 | tf_op jit(solution)/shard_map/ppermute | solution.py:910
  255.5 16.8 %collective-permute-start.27 = (bf16[192,768]{1,0:T(8,128)(2,1)}, bf16[192,768]{1,0:T(8,128)(2,1)S(1)}, u32[]{:S(2)}, u32[]{:S(2)}) collective-permute-start(bf16[192,768]{1,0:T(8,128)(2,1)} %get-tuple-element.396), channel_id=1, source_target_pairs={{0,16},{2,18},{4,20},{6,22},{8,24},{10,26},{12,28},{14,30},{16,0},... | collective-permute-start | bytes 884744 | tf_op jit(solution)/shard_map/ppermute | solution.py:910
  258.1 23.4 %collective-permute-start.28 = (bf16[384,768]{1,0:T(8,128)(2,1)}, bf16[384,768]{1,0:T(8,128)(2,1)}, u32[]{:S(2)}, u32[]{:S(2)}) collective-permute-start(bf16[384,768]{1,0:T(8,128)(2,1)} %get-tuple-element.329), channel_id=1, source_target_pairs={{0,1},{1,0},{2,3},{3,2},{4,5},{5,4},{6,7},{7,6},{8,9},{9,8},{10,11... | collective-permute-start | bytes 1769480 | tf_op jit(solution)/shard_map/ppermute | solution.py:960
  274.7 10.1 %collective-permute-start.29 = (bf16[96,1408]{1,0:T(8,128)(2,1)}, bf16[96,1408]{1,0:T(8,128)(2,1)}, u32[]{:S(2)}, u32[]{:S(2)}) collective-permute-start(bf16[96,1408]{1,0:T(8,128)(2,1)} %get-tuple-element.400), channel_id=1, source_target_pairs={{0,8},{2,10},{4,12},{6,14},{8,0},{10,2},{12,4},{14,6},{16,24},{18,... | collective-permute-start | bytes 811016 | tf_op jit(solution)/shard_map/ppermute | solution.py:910
  281.2 19.0 %collective-permute-start.32 = (bf16[192,768]{1,0:T(8,128)(2,1)S(1)}, bf16[192,768]{1,0:T(8,128)(2,1)}, u32[]{:S(2)}, u32[]{:S(2)}) collective-permute-start(bf16[192,768]{1,0:T(8,128)(2,1)S(1)} %add_convert_fusion.14), channel_id=1, source_target_pairs={{0,16},{2,18},{4,20},{6,22},{8,24},{10,26},{12,28},{14,30},{16,0},... | collective-permute-start | bytes 884744 | tf_op jit(solution)/shard_map/ppermute | solution.py:910
  284.9 15.3 %collective-permute-start.31 = (f32[1,6784]{1,0:T(1,128)S(1)}, f32[1,6784]{1,0:T(1,128)S(1)}, u32[]{:S(2)}, u32[]{:S(2)}) collective-permute-start(f32[1,6784]{1,0:T(1,128)S(1)} %add.244), channel_id=1, source_target_pairs={{0,2},{2,0},{4,6},{6,4},{8,10},{10,8},{12,14},{14,12},{16,18},{18,... | collective-permute-start | bytes 81416 | tf_op jit(solution)/shard_map/ppermute | solution.py:900
  290.7 11.2 %collective-permute-start.33 = (bf16[48,1408]{1,0:T(8,128)(2,1)}, bf16[48,1408]{1,0:T(8,128)(2,1)S(1)}, u32[]{:S(2)}, u32[]{:S(2)}) collective-permute-start(bf16[48,1408]{1,0:T(8,128)(2,1)} %get-tuple-element.404), channel_id=1, source_target_pairs={{0,16},{2,18},{4,20},{6,22},{8,24},{10,26},{12,28},{14,30},{16,0},... | collective-permute-start | bytes 405512 | tf_op jit(solution)/shard_map/ppermute | solution.py:910
  301.4 13.1 %collective-permute-start.35 = (bf16[384,768]{1,0:T(8,128)(2,1)S(1)}, bf16[384,768]{1,0:T(8,128)(2,1)S(1)}, u32[]{:S(2)}, u32[]{:S(2)}) collective-permute-start(bf16[384,768]{1,0:T(8,128)(2,1)S(1)} %pad_maximum_fusion.6), channel_id=1, source_target_pairs={{0,8},{2,10},{4,12},{6,14},{8,0},{10,2},{12,4},{14,6},{16,24},{18,... | collective-permute-start | bytes 1769480 | tf_op jit(solution)/shard_map/ppermute | solution.py:910
  314.6 13.6 %collective-permute-start.37 = (bf16[384,768]{1,0:T(8,128)(2,1)S(1)}, bf16[384,768]{1,0:T(8,128)(2,1)S(1)}, u32[]{:S(2)}, u32[]{:S(2)}) collective-permute-start(bf16[384,768]{1,0:T(8,128)(2,1)S(1)} %get-tuple-element.352), channel_id=1, source_target_pairs={{0,4},{2,6},{4,0},{6,2},{8,12},{10,14},{12,8},{14,10},{16,20},{18,... | collective-permute-start | bytes 1769480 | tf_op jit(solution)/shard_map/ppermute | solution.py:910
  315.2 12.9 %collective-permute-start.36 = (bf16[112,1408]{1,0:T(8,128)(2,1)S(1)}, bf16[112,1408]{1,0:T(8,128)(2,1)S(1)}, u32[]{:S(2)}, u32[]{:S(2)}) collective-permute-start(bf16[112,1408]{1,0:T(8,128)(2,1)S(1)} %pad_maximum_fusion.7), channel_id=1, source_target_pairs={{0,16},{2,18},{4,20},{6,22},{8,24},{10,26},{12,28},{14,30},{16,0},... | collective-permute-start | bytes 946184 | tf_op jit(solution)/shard_map/ppermute | solution.py:910
  315.9 18.3 %collective-permute-start.38 = (bf16[512,768]{1,0:T(8,128)(2,1)S(1)}, bf16[512,768]{1,0:T(8,128)(2,1)}, u32[]{:S(2)}, u32[]{:S(2)}) collective-permute-start(bf16[512,768]{1,0:T(8,128)(2,1)S(1)} %copy-done.42), channel_id=1, source_target_pairs={{1,0},{3,2},{5,4},{7,6},{9,8},{11,10},{13,12},{15,14},{17,16},{19,... | collective-permute-start | bytes 2359304 | tf_op jit(solution)/shard_map/ppermute | solution.py:1181
  329.4 16.0 %collective-permute-start.40 = (bf16[224,1408]{1,0:T(8,128)(2,1)S(1)}, bf16[224,1408]{1,0:T(8,128)(2,1)}, u32[]{:S(2)}, u32[]{:S(2)}) collective-permute-start(bf16[224,1408]{1,0:T(8,128)(2,1)S(1)} %pad_maximum_fusion.5), channel_id=1, source_target_pairs={{0,8},{2,10},{4,12},{6,14},{8,0},{10,2},{12,4},{14,6},{16,24},{18,... | collective-permute-start | bytes 1892360 | tf_op jit(solution)/shard_map/ppermute | solution.py:910
  329.4 15.2 %collective-permute-start.41 = (bf16[384,768]{1,0:T(8,128)(2,1)S(1)}, bf16[384,768]{1,0:T(8,128)(2,1)}, u32[]{:S(2)}, u32[]{:S(2)}) collective-permute-start(bf16[384,768]{1,0:T(8,128)(2,1)S(1)} %get-tuple-element.363), channel_id=1, source_target_pairs={{0,4},{2,6},{4,0},{6,2},{8,12},{10,14},{12,8},{14,10},{16,20},{18,... | collective-permute-start | bytes 1769480 | tf_op jit(solution)/shard_map/ppermute | solution.py:910
  (55 other events, 279.2 us)

commit v5 on v4

--- a/solution.py
+++ b/solution.py
@@ -348,11 +348,11 @@
 
 
 def open_kernel(
-    at_ref, qw_ref, kw_ref, vw_ref, x_ref, s_ref, w_ref, w_send_ref, halo_ref, s_send_ref, s_own_ref
+    at_ref, qw_ref, kw_ref, vw_ref, s_ref, w_ref, w_send_ref, s_send_ref, s_own_ref
 ):
     side = at_ref[1]
-    rows, length, width = x_ref.shape
-    local, half = qw_ref.shape[1], vw_ref.shape[0]
+    rows, half, total = s_ref.shape
+    width, local, length = qw_ref.shape[0], qw_ref.shape[1], total // 2
     depth = w_send_ref.shape[0]
     cut = pl.ds(pl.multiple_of(at_ref[0] * depth, depth), depth)
     w_ref[:, :local] = qw_ref[...]
@@ -363,7 +363,6 @@
     own = pl.ds(pl.multiple_of(side * length, length), length)
     other = pl.ds(pl.multiple_of((1 - side) * length, length), length)
     for row in range(rows):
-        halo_ref[row * SPAN : (row + 1) * SPAN, :] = x_ref[row, length - SPAN :, :]
         lines = slice(row * half, (row + 1) * half)
         middle = s_ref[row, :, length - SPAN : length]
         s_send_ref[lines, :SPAN] = middle
@@ -372,14 +371,13 @@
         s_own_ref[lines, SPAN:] = s_ref[row, :, own]
 
 
-def open_step(at, qw, kw, vw, x, skip):
-    rows, length, width = x.shape
-    local, half = qw.shape[1], vw.shape[0]
+def open_step(at, qw, kw, vw, skip):
+    rows, half, length = skip.shape[0], skip.shape[1], skip.shape[2] // 2
+    width, local = qw.shape
     columns = -(-(2 * local + half) // 256) * 256
     shapes = [
         (width, columns),
         (width // 2, columns),
-        (rows * SPAN, width),
         (rows * half, SPAN + length),
         (rows * half, SPAN + length),
     ]
@@ -388,13 +386,13 @@
         grid_spec=pltpu.PrefetchScalarGridSpec(
             num_scalar_prefetch=1,
             grid=(1,),
-            in_specs=[whole_spec(v) for v in (qw, kw, vw, x, skip)],
+            in_specs=[whole_spec(v) for v in (qw, kw, vw, skip)],
             out_specs=[pl.BlockSpec(shape, lambda *_: (0, 0)) for shape in shapes],
         ),
         out_shape=[jax.ShapeDtypeStruct(shape, BF) for shape in shapes],
         cost_estimate=COST,
         name="open",
-    )(at, qw, kw, vw, x, skip)
+    )(at, qw, kw, vw, skip)
 
 
 class Rows:
@@ -1015,10 +1013,12 @@
     where = Rows(width, local, hidden_local)
 
     out_mine = swap_tensor(block_of(out_weight, core, 2, 0))
-    qkv_own, qkv_send, halo_send, skip_send, skip_own = open_step(
-        at, query_weight, key_weight, value_weight.T, block_input, jnp.swapaxes(skip_values, 1, 2)
-    )
+    halo_send = block_input[:, length - SPAN :].reshape(rows * SPAN, width)
     halo = lax.ppermute(halo_send, "tensor", [(0, 1)])
+    qkv_own, qkv_send, skip_send, skip_own = open_step(
+        at, after(query_weight, halo_send), key_weight, value_weight.T,
+        jnp.swapaxes(skip_values, 1, 2),
+    )
     row_vectors = jnp.concatenate(
         [
             up_bias, query_bias, value_bias, jnp.zeros((where.pad,), F32),

time: 368 us -> 366 us (level)
  transfers between devices with their start and end apart: 44 -> 44, of which waited for: 18 -> 18; matrix products, arithmetic and copies ran while one was open for 15% -> 16% of each run, Pallas kernels for 51% -> 51%
where the time goes in v5:
time: 366 us; the launch traced here: 361 us
  Pallas kernels  189 us (52%)
  waiting for transfers between devices  62.9 us (17%)
  other arithmetic  45 us (12%)
  starting transfers between devices  37.7 us (10%)
  local copies, waits for them, and re-layouts  24.2 us (7%)
    pallas_call x2, Pallas kernels, feed(): pl.pallas_call(feed_kernel, grid_spec=pltpu.PrefetchScalarGridSpec(num_sc...  52.1 us
    ppermute x15, waiting for transfers between devices, shift(): return lax.ppermute(value, 'dp', perm)  38.7 us
    convert_element_type x17, other arithmetic, add(): return total.astype(BF)  26.9 us
    pallas_call x2, Pallas kernels, attend_forward(): pl.pallas_call(functools.partial(attend_forward_kernel, pairs), grid=(row...  26.3 us
    pallas_call x2, Pallas kernels, attend_backward(): pl.pallas_call(functools.partial(attend_backward_kernel, pairs), grid=(ro...  21.7 us
    ppermute x15, starting transfers between devices, shift(): return lax.ppermute(value, 'dp', perm)  16.6 us
    pallas_call x2, Pallas kernels, project_grad(): pl.pallas_call(project_grad_kernel, grid_spec=pltpu.PrefetchScalarGridSpe...  16.1 us
    ppermute x13, starting transfers between devices, swap_tensor(): return lax.ppermute(value, 'tensor', [(0, 1), (1, 0)])  15.8 us
  transfers between devices with their start and end apart: 44, of which 18 were waited for; matrix products, arithmetic and copies ran while one was open for 16% of the time, Pallas kernels for 51%

profile of v5, /device:TPU:0, one launch (start us, length us, event | category | flops | bytes accessed | tf_op | source)
XLA Modules:
  0.0 361.1 jit_solution(11858128146447642922)
XLA Ops:
  1.8 3.0 collective-permute-start
  12.0 3.2 constant_dynamic-slice_fusion.12
  15.2 4.3 %open.1 = (bf16[768,1024]{1,0:T(8,128)(2,1)}, bf16[384,1024]{1,0:T(8,128)(2,1)}, bf16[384,768]{1,0:T(8,128)(2,1)}, bf16[384,768]{1,0:T(8,128)(2,1)}) custom-call(s32[2]{0:T(128)} %pad_add_fusion.at_ref.core_ref, bf16[768,384]{1,0:T(8,128)(2,1)} %qw_ref, bf16[768,384]{1,0:T(8,128)(2,1)} %kw_ref.1, bf16[192,768]{1,0:T(8,128)(2,1)} %bitcast.24, ...), custom_call_target="tpu_custom_call" | custom-call | flops 1048576 | bytes 1048576 | tf_op jit(solution)/shard_map/open/pallas_call | solution.py:384
  22.1 7.1 %collective-permute-done.1.h_ref = bf16[512,768]{1,0:T(8,128)(2,1)S(1)} collective-permute-done((bf16[512,768]{1,0:T(8,128)(2,1)}, bf16[512,768]{1,0:T(8,128)(2,1)S(1)}, u32[]{:S(2)}, u32[]{:S(2)}) %collective-permute-start.1) | collective-permute-done | bytes 786464 | tf_op jit(solution)/shard_map/ppermute | solution.py:1017
  30.1 6.5 %project_own.1 = (bf16[1536,768]{1,0:T(8,128)(2,1)}, bf16[1536,1024]{1,0:T(8,128)(2,1)}) custom-call(bf16[1024,768]{1,0:T(8,128)(2,1)} %bitcast.19, bf16[512,768]{1,0:T(8,128)(2,1)} %copy-done.8, f32[1,6784]{1,0:T(1,128)} %reshape.90.rows_ref.ba_ref.bb_ref, bf16[768,1024]{1,0:T(8,128)(2,1)} %get-tuple-element.201.w_ref.wl_ref), custom_call_target="tpu_custom_call" | custom-call | flops 1048576 | bytes 1048576 | tf_op jit(solution)/shard_map/project_own/pallas_call | solution.py:436
  40.3 13.1 %attend_forward.2 = (bf16[1024,384]{1,0:T(8,128)(2,1)}, f32[2,4,3,256]{3,2,1,0:T(4,128)}, f32[768,512]{1,0:T(8,128)}) custom-call(bf16[1536,1024]{1,0:T(8,128)(2,1)} %get-tuple-element.205.x_ref, bf16[384,768]{1,0:T(8,128)(2,1)} %get-tuple-element.206.s_ref, s32[2,768,1]{2,1,0:T(8,128)} %copy.39.kseg_ref, s32[2,1,512]{2,1,0:T(1,128)} %reshape.87.qseg_ref), custom_call_target="tpu_custom_call" | custom-call | flops 1048576 | bytes 1048576 | tf_op jit(solution)/shard_map/attend_forward/pallas_call | solution.py:157
  56.7 6.5 %project_other.1.x_ref = bf16[1536,1024]{1,0:T(8,128)(2,1)} custom-call(s32[2]{0:T(128)} %pad_add_fusion.at_ref.core_ref, bf16[1536,768]{1,0:T(8,128)(2,1)} %get-tuple-element.297.ne_ref.n_ref, bf16[384,1024]{1,0:T(8,128)(2,1)} %copy-done.6, bf16[384,1024]{1,0:T(8,128)(2,1)} %copy-done.7, f32[1,6784]{1,0:T(1,128)} %copy-done.29), custom_call_target="tpu_custom_call" | custom-call | flops 1048576 | bytes 1048576 | tf_op jit(solution)/shard_map/project_other/pallas_call | solution.py:471
  66.3 13.2 %attend_forward.3 = (bf16[1024,384]{1,0:T(8,128)(2,1)}, f32[2,4,3,256]{3,2,1,0:T(4,128)}, f32[768,512]{1,0:T(8,128)}) custom-call(bf16[1536,1024]{1,0:T(8,128)(2,1)} %project_other.1.x_ref, bf16[384,768]{1,0:T(8,128)(2,1)} %copy-done.5, s32[2,768,1]{2,1,0:T(8,128)} %copy.39.kseg_ref, s32[2,1,512]{2,1,0:T(1,128)} %reshape.87.qseg_ref), custom_call_target="tpu_custom_call" | custom-call | flops 1048576 | bytes 1048576 | tf_op jit(solution)/shard_map/attend_forward/pallas_call | solution.py:157
  79.4 7.2 %middle.1 = (f32[1024,768]{1,0:T(8,128)}, bf16[1024,768]{1,0:T(8,128)(2,1)}, bf16[384,768]{1,0:T(8,128)(2,1)}) custom-call(s32[2]{0:T(128)} %pad_add_fusion.at_ref.core_ref, bf16[1024,384]{1,0:T(8,128)(2,1)} %get-tuple-element.214.ml_ref, bf16[1024,384]{1,0:T(8,128)(2,1)} %get-tuple-element.225.mr_ref, bf16[384,768]{1,0:T(8,128)(2,1)} %wl_ref.3, ...), custom_call_target="tpu_custom_call" | custom-call | flops 1048576 | bytes 1048576 | tf_op jit(solution)/shard_map/middle/pallas_call | solution.py:506
  86.6 26.0 %feed.2 = (bf16[768,768]{1,0:T(8,128)(2,1)}, bf16[768,768]{1,0:T(8,128)(2,1)}, bf16[768,768]{1,0:T(8,128)(2,1)}, bf16[768,768]{1,0:T(8,128)(2,1)}, f32[1,768]{1,...) custom-call(s32[2]{0:T(128)} %pad_add_fusion.at_ref.core_ref, ...), custom_call_target="tpu_custom_call" | custom-call | flops 1048576 | bytes 1048576 | tf_op jit(solution)/shard_map/feed/pallas_call | solution.py:319
  112.6 4.4 %collective-permute-done.9.ub_ref = bf16[768,768]{1,0:T(8,128)(2,1)} collective-permute-done((bf16[768,768]{1,0:T(8,128)(2,1)S(1)}, bf16[768,768]{1,0:T(8,128)(2,1)}, u32[]{:S(2)}, u32[]{:S(2)}) %collective-permute-start.9) | collective-permute-done | bytes 1179680 | tf_op jit(solution)/shard_map/ppermute | solution.py:958
  122.7 26.1 %feed.3 = (bf16[768,768]{1,0:T(8,128)(2,1)}, bf16[768,768]{1,0:T(8,128)(2,1)}, bf16[768,768]{1,0:T(8,128)(2,1)}, bf16[768,768]{1,0:T(8,128)(2,1)}, f32[1,768]{1,...) custom-call(s32[2]{0:T(128)} %pad_add_fusion.at_ref.core_ref, ...), custom_call_target="tpu_custom_call" | custom-call | flops 1048576 | bytes 1048576 | tf_op jit(solution)/shard_map/feed/pallas_call | solution.py:319
  164.4 11.8 %middle_back.1 = (f32[1024,768]{1,0:T(8,128)}, bf16[1024,384]{1,0:T(8,128)(2,1)}, bf16[1024,384]{1,0:T(8,128)(2,1)}, bf16[768,384]{1,0:T(8,128)(2,1)}, bf16[768,384]{1,0:T(8,128)(2,1)}, /*index=5*/f32[8,768]{1,0:T(8,128)}) custom-call(f32[1024,768]{1,0:T(8,128)} %get-tuple-element.236.bl_ref, f32[1024,768]{1,0:T(8,128)} %get-tuple-element.265.br_ref, ...), custom_call_target="tpu_custom_call" | custom-call | flops 1048576 | bytes 1048576 | tf_op jit(solution)/shard_map/middle_back/pallas_call | solution.py:582
  176.2 10.7 %attend_backward.2 = (bf16[1536,1024]{1,0:T(8,128)(2,1)}, bf16[384,768]{1,0:T(8,128)(2,1)}) custom-call(bf16[1536,1024]{1,0:T(8,128)(2,1)} %project_other.1.x_ref, bf16[384,768]{1,0:T(8,128)(2,1)} %copy-done.5, s32[2,768,1]{2,1,0:T(8,128)} %copy.39.kseg_ref, s32[2,1,512]{2,1,0:T(1,128)} %reshape.87.qseg_ref, f32[2,4,3,256]{3,2,1,0:T(4,128)} %get-tuple-element.272.lse_ref, ...), custom_call_target="tpu_custom_call" | custom-call | flops 1048576 | bytes 1048576 | tf_op jit(solution)/shard_map/attend_backward/pallas_call | solution.py:181
  189.1 8.0 %project_grad.2 = (bf16[384,1408]{1,0:T(8,128)(2,1)}, bf16[384,1408]{1,0:T(8,128)(2,1)}, f32[1,1024]{1,0:T(1,128)}) custom-call(s32[2]{0:T(128)} %pad_add_fusion.at_ref.core_ref, bf16[1536,768]{1,0:T(8,128)(2,1)} %get-tuple-element.297.ne_ref.n_ref, bf16[1536,1024]{1,0:T(8,128)(2,1)} %get-tuple-element.281.d_ref.dr_ref, ...), custom_call_target="tpu_custom_call" | custom-call | flops 1048576 | bytes 1048576 | tf_op jit(solution)/shard_map/project_grad/pallas_call | solution.py:628
  207.5 10.9 %attend_backward.3 = (bf16[1536,1024]{1,0:T(8,128)(2,1)}, bf16[384,768]{1,0:T(8,128)(2,1)}) custom-call(bf16[1536,1024]{1,0:T(8,128)(2,1)} %get-tuple-element.205.x_ref, bf16[384,768]{1,0:T(8,128)(2,1)} %get-tuple-element.206.s_ref, s32[2,768,1]{2,1,0:T(8,128)} %copy.39.kseg_ref, s32[2,1,512]{2,1,0:T(1,128)} %reshape.87.qseg_ref, ...), custom_call_target="tpu_custom_call" | custom-call | flops 1048576 | bytes 1048576 | tf_op jit(solution)/shard_map/attend_backward/pallas_call | solution.py:181
  218.4 3.1 collective-permute-done.22
  228.7 8.0 %project_grad.3 = (bf16[384,1408]{1,0:T(8,128)(2,1)}, bf16[384,1408]{1,0:T(8,128)(2,1)}, f32[1,1024]{1,0:T(1,128)}) custom-call(s32[2]{0:T(128)} %pad_add_fusion.at_ref.core_ref, bf16[1536,768]{1,0:T(8,128)(2,1)} %get-tuple-element.297.ne_ref.n_ref, bf16[1536,1024]{1,0:T(8,128)(2,1)} %get-tuple-element.308.d_ref.dl_ref, ...), custom_call_target="tpu_custom_call" | custom-call | flops 1048576 | bytes 1048576 | tf_op jit(solution)/shard_map/project_grad/pallas_call | solution.py:628
  236.7 4.9 %collective-permute-done.23 = bf16[384,768]{1,0:T(8,128)(2,1)} collective-permute-done((bf16[384,768]{1,0:T(8,128)(2,1)}, bf16[384,768]{1,0:T(8,128)(2,1)}, u32[]{:S(2)}, u32[]{:S(2)}) %collective-permute-start.23) | collective-permute-done | bytes 589856 | tf_op jit(solution)/shard_map/ppermute | solution.py:908
  241.7 3.0 collective-permute-done.25
  255.8 13.9 %first_back.1 = (f32[1024,768]{1,0:T(8,128)}, bf16[512,768]{1,0:T(8,128)(2,1)}, f32[8,768]{1,0:T(8,128)}) custom-call(s32[2]{0:T(128)} %pad_add_fusion.at_ref.core_ref, bf16[1536,1024]{1,0:T(8,128)(2,1)} %get-tuple-element.308.d_ref.dl_ref, bf16[1536,1024]{1,0:T(8,128)(2,1)} %get-tuple-element.281.d_ref.dr_ref, ...), custom_call_target="tpu_custom_call" | custom-call | flops 1048576 | bytes 1048576 | tf_op jit(solution)/shard_map/first_back/pallas_call | solution.py:683
  279.0 3.2 skip_grad.1
  284.2 3.9 %add.246 = f32[1024,768]{1,0:T(8,128)} add(f32[1024,768]{1,0:T(8,128)S(1)} %add_add_fusion, f32[1024,768]{1,0:T(8,128)} %get-tuple-element.334) | non-fusion elementwise | flops 786432 | bytes 9437184 | tf_op jit(solution)/shard_map/add | solution.py:1188
  290.7 6.9 %collective-permute-done.32 = bf16[192,768]{1,0:T(8,128)(2,1)} collective-permute-done((bf16[192,768]{1,0:T(8,128)(2,1)S(1)}, bf16[192,768]{1,0:T(8,128)(2,1)}, u32[]{:S(2)}, u32[]{:S(2)}) %collective-permute-start.32) | collective-permute-done | bytes 294944 | tf_op jit(solution)/shard_map/ppermute | solution.py:908
  300.0 4.7 %collective-permute-done.34 = bf16[56,1408]{1,0:T(8,128)(2,1)S(1)} collective-permute-done((bf16[56,1408]{1,0:T(8,128)(2,1)S(1)}, bf16[56,1408]{1,0:T(8,128)(2,1)S(1)}, u32[]{:S(2)}, u32[]{:S(2)}) %collective-permute-start.34) | collective-permute-done | bytes 157728 | tf_op jit(solution)/shard_map/ppermute | solution.py:908
  304.7 7.2 %collective-permute-done.35 = bf16[384,768]{1,0:T(8,128)(2,1)S(1)} collective-permute-done((bf16[384,768]{1,0:T(8,128)(2,1)S(1)}, bf16[384,768]{1,0:T(8,128)(2,1)S(1)}, u32[]{:S(2)}, u32[]{:S(2)}) %collective-permute-start.35) | collective-permute-done | bytes 589856 | tf_op jit(solution)/shard_map/ppermute | solution.py:908
  314.6 11.0 %collective-permute-done.36 = bf16[112,1408]{1,0:T(8,128)(2,1)S(1)} collective-permute-done((bf16[112,1408]{1,0:T(8,128)(2,1)S(1)}, bf16[112,1408]{1,0:T(8,128)(2,1)S(1)}, u32[]{:S(2)}, u32[]{:S(2)}) %collective-permute-start.36) | collective-permute-done | bytes 315424 | tf_op jit(solution)/shard_map/ppermute | solution.py:908
  328.3 3.3 collective-permute-done.38.got_ref
  334.2 5.1 %up_out.1 = f32[768,1536]{1,0:T(8,128)} custom-call(s32[2]{0:T(128)} %pad_add_fusion.at_ref.core_ref, bf16[768,768]{1,0:T(8,128)(2,1)} %copy-done.3, bf16[768,768]{1,0:T(8,128)(2,1)} %collective-permute-done.39.other_ref), custom_call_target="tpu_custom_call" | custom-call | flops 1048576 | bytes 1048576 | tf_op jit(solution)/shard_map/up_out/pallas_call | solution.py:825
  339.3 2.7 collective-permute-done.41
  347.3 4.7 %project_out.1 = (f32[768,384]{1,0:T(8,128)}, f32[768,384]{1,0:T(8,128)}, f32[192,768]{1,0:T(8,128)}, f32[384,768]{1,0:T(8,128)}, f32[8,1408]{1,0:T(8,128)}) custom-call(s32[2]{0:T(128)} %pad_add_fusion.at_ref.core_ref, bf16[448,1408]{1,0:T(8,128)(2,1)} %copy-done.2, bf16[448,1408]{1,0:T(8,128)(2,1)} %collective-permute-done.42.other_ref), custom_call_target="tpu_custom_call" | custom-call | flops 1048576 | bytes 1048576 | tf_op jit(solution)/shard_map/project_out/pallas_call | solution.py:868
  355.2 5.7 %down_out.1 = f32[1536,768]{1,0:T(8,128)} custom-call(s32[2]{0:T(128)} %pad_add_fusion.at_ref.core_ref, bf16[768,768]{1,0:T(8,128)(2,1)} %copy-done.4, bf16[768,768]{1,0:T(8,128)(2,1)} %collective-permute-done.43.other_ref), custom_call_target="tpu_custom_call" | custom-call | flops 1048576 | bytes 1048576 | tf_op jit(solution)/shard_map/down_out/pallas_call | solution.py:801
  (233 shorter events, 105.9 us)
Async XLA Ops:
  1.8 19.5 %collective-permute-start = (bf16[192,768]{1,0:T(8,128)(2,1)S(1)}, bf16[192,768]{1,0:T(8,128)(2,1)S(1)}, u32[]{:S(2)}, u32[]{:S(2)}) collective-permute-start(bf16[192,768]{1,0:T(8,128)(2,1)S(1)} %constant_dynamic-slice_fusion.14), channel_id=1, source_target_pairs={{0,1},{1,0},{2,3},{3,2},{4,5},{5,4},{6,7},{7,6},{8,9},{9,8},{10,11... | collective-permute-start | bytes 884744 | tf_op jit(solution)/shard_map/ppermute | solution.py:958
  6.9 22.3 %collective-permute-start.1 = (bf16[512,768]{1,0:T(8,128)(2,1)}, bf16[512,768]{1,0:T(8,128)(2,1)S(1)}, u32[]{:S(2)}, u32[]{:S(2)}) collective-permute-start(bf16[512,768]{1,0:T(8,128)(2,1)} %bitcast.3), channel_id=1, source_target_pairs={{0,1},{2,3},{4,5},{6,7},{8,9},{10,11},{12,13},{14,15},{16,17},{18,... | collective-permute-start | bytes 2359304 | tf_op jit(solution)/shard_map/ppermute | solution.py:1017
  21.3 32.2 %collective-permute-start.4 = (bf16[384,1024]{1,0:T(8,128)(2,1)}, bf16[384,1024]{1,0:T(8,128)(2,1)S(1)}, u32[]{:S(2)}, u32[]{:S(2)}) collective-permute-start(bf16[384,1024]{1,0:T(8,128)(2,1)} %get-tuple-element.211), channel_id=1, source_target_pairs={{0,1},{1,0},{2,3},{3,2},{4,5},{5,4},{6,7},{7,6},{8,9},{9,8},{10,11... | collective-permute-start | bytes 2359304 | tf_op jit(solution)/shard_map/ppermute | solution.py:958
  21.3 15.3 %collective-permute-start.2 = (bf16[192,768]{1,0:T(8,128)(2,1)S(1)}, bf16[192,768]{1,0:T(8,128)(2,1)S(1)}, u32[]{:S(2)}, u32[]{:S(2)}) collective-permute-start(bf16[192,768]{1,0:T(8,128)(2,1)S(1)} %collective-permute-done.w1_ref), channel_id=1, source_target_pairs={{0,2},{2,0},{4,6},{6,4},{8,10},{10,8},{12,14},{14,12},{16,18},{18,... | collective-permute-start | bytes 884744 | tf_op jit(solution)/shard_map/ppermute | solution.py:898
  36.6 16.8 %collective-permute-start.3 = (bf16[192,768]{1,0:T(8,128)(2,1)S(1)}, bf16[192,768]{1,0:T(8,128)(2,1)S(1)}, u32[]{:S(2)}, u32[]{:S(2)}) collective-permute-start(bf16[192,768]{1,0:T(8,128)(2,1)S(1)} %get-tuple-element.210), channel_id=1, source_target_pairs={{0,1},{1,0},{2,3},{3,2},{4,5},{5,4},{6,7},{7,6},{8,9},{9,8},{10,11... | collective-permute-start | bytes 884744 | tf_op jit(solution)/shard_map/ppermute | solution.py:958
  39.0 14.4 %collective-permute-start.5 = (f32[1,6784]{1,0:T(1,128)S(1)}, f32[1,6784]{1,0:T(1,128)S(1)}, u32[]{:S(2)}, u32[]{:S(2)}) collective-permute-start(f32[1,6784]{1,0:T(1,128)S(1)} %copy-done.15), channel_id=1, source_target_pairs={{0,1},{1,0},{2,3},{3,2},{4,5},{5,4},{6,7},{7,6},{8,9},{9,8},{10,11... | collective-permute-start | bytes 81416 | tf_op jit(solution)/shard_map/ppermute | solution.py:958
  53.5 9.8 %collective-permute-start.7 = (bf16[192,768]{1,0:T(8,128)(2,1)}, bf16[192,768]{1,0:T(8,128)(2,1)S(1)}, u32[]{:S(2)}, u32[]{:S(2)}) collective-permute-start(bf16[192,768]{1,0:T(8,128)(2,1)} %get-tuple-element.219), channel_id=1, source_target_pairs={{0,1},{1,0},{2,3},{3,2},{4,5},{5,4},{6,7},{7,6},{8,9},{9,8},{10,11... | collective-permute-start | bytes 884744 | tf_op jit(solution)/shard_map/ppermute | solution.py:958
  63.4 49.2 %collective-permute-start.8 = (bf16[768,768]{1,0:T(8,128)(2,1)}, bf16[768,768]{1,0:T(8,128)(2,1)}, u32[]{:S(2)}, u32[]{:S(2)}) collective-permute-start(bf16[768,768]{1,0:T(8,128)(2,1)} %get-tuple-element.233), channel_id=1, source_target_pairs={{0,1},{1,0},{2,3},{3,2},{4,5},{5,4},{6,7},{7,6},{8,9},{9,8},{10,11... | collective-permute-start | bytes 3538952 | tf_op jit(solution)/shard_map/ppermute | solution.py:958
  65.1 51.8 %collective-permute-start.9 = (bf16[768,768]{1,0:T(8,128)(2,1)S(1)}, bf16[768,768]{1,0:T(8,128)(2,1)}, u32[]{:S(2)}, u32[]{:S(2)}) collective-permute-start(bf16[768,768]{1,0:T(8,128)(2,1)S(1)} %copy-done.19), channel_id=1, source_target_pairs={{0,1},{1,0},{2,3},{3,2},{4,5},{5,4},{6,7},{7,6},{8,9},{9,8},{10,11... | collective-permute-start | bytes 3538952 | tf_op jit(solution)/shard_map/ppermute | solution.py:958
  121.8 26.9 %collective-permute-start.12 = (bf16[768,768]{1,0:T(8,128)(2,1)}, bf16[768,768]{1,0:T(8,128)(2,1)}, u32[]{:S(2)}, u32[]{:S(2)}) collective-permute-start(bf16[768,768]{1,0:T(8,128)(2,1)} %get-tuple-element.252), channel_id=1, source_target_pairs={{0,2},{2,0},{4,6},{6,4},{8,10},{10,8},{12,14},{14,12},{16,18},{18,... | collective-permute-start | bytes 3538952 | tf_op jit(solution)/shard_map/ppermute | solution.py:898
  122.0 26.8 %collective-permute-start.13 = (bf16[768,768]{1,0:T(8,128)(2,1)}, bf16[768,768]{1,0:T(8,128)(2,1)}, u32[]{:S(2)}, u32[]{:S(2)}) collective-permute-start(bf16[768,768]{1,0:T(8,128)(2,1)} %get-tuple-element.253), channel_id=1, source_target_pairs={{0,2},{2,0},{4,6},{6,4},{8,10},{10,8},{12,14},{14,12},{16,18},{18,... | collective-permute-start | bytes 3538952 | tf_op jit(solution)/shard_map/ppermute | solution.py:898
  152.4 23.7 %collective-permute-start.16 = (bf16[384,768]{1,0:T(8,128)(2,1)}, bf16[384,768]{1,0:T(8,128)(2,1)}, u32[]{:S(2)}, u32[]{:S(2)}) collective-permute-start(bf16[384,768]{1,0:T(8,128)(2,1)} %get-tuple-element.388), channel_id=1, source_target_pairs={{0,4},{2,6},{4,0},{6,2},{8,12},{10,14},{12,8},{14,10},{16,20},{18,... | collective-permute-start | bytes 1769480 | tf_op jit(solution)/shard_map/ppermute | solution.py:908
  159.4 37.8 %collective-permute-start.18 = (bf16[768,768]{1,0:T(8,128)(2,1)}, bf16[768,768]{1,0:T(8,128)(2,1)}, u32[]{:S(2)}, u32[]{:S(2)}) collective-permute-start(bf16[768,768]{1,0:T(8,128)(2,1)} %add_convert_fusion.2), channel_id=1, source_target_pairs={{0,1},{1,0},{2,3},{3,2},{4,5},{5,4},{6,7},{7,6},{8,9},{9,8},{10,11... | collective-permute-start | bytes 3538952 | tf_op jit(solution)/shard_map/ppermute | solution.py:958
  163.8 23.1 %collective-permute-start.17 = (bf16[384,768]{1,0:T(8,128)(2,1)}, bf16[384,768]{1,0:T(8,128)(2,1)}, u32[]{:S(2)}, u32[]{:S(2)}) collective-permute-start(bf16[384,768]{1,0:T(8,128)(2,1)} %get-tuple-element.386), channel_id=1, source_target_pairs={{0,4},{2,6},{4,0},{6,2},{8,12},{10,14},{12,8},{14,10},{16,20},{18,... | collective-permute-start | bytes 1769480 | tf_op jit(solution)/shard_map/ppermute | solution.py:908
  197.3 21.1 %collective-permute-start.21 = (bf16[384,768]{1,0:T(8,128)(2,1)}, bf16[384,768]{1,0:T(8,128)(2,1)}, u32[]{:S(2)}, u32[]{:S(2)}) collective-permute-start(bf16[384,768]{1,0:T(8,128)(2,1)} %add_convert_fusion.10), channel_id=1, source_target_pairs={{0,1},{1,0},{2,3},{3,2},{4,5},{5,4},{6,7},{7,6},{8,9},{9,8},{10,11... | collective-permute-start | bytes 1769480 | tf_op jit(solution)/shard_map/ppermute | solution.py:958
  200.7 17.7 %collective-permute-start.20 = (bf16[384,768]{1,0:T(8,128)(2,1)}, bf16[384,768]{1,0:T(8,128)(2,1)}, u32[]{:S(2)}, u32[]{:S(2)}) collective-permute-start(bf16[384,768]{1,0:T(8,128)(2,1)} %get-tuple-element.384), channel_id=1, source_target_pairs={{0,4},{2,6},{4,0},{6,2},{8,12},{10,14},{12,8},{14,10},{16,20},{18,... | collective-permute-start | bytes 1769480 | tf_op jit(solution)/shard_map/ppermute | solution.py:908
  203.2 18.3 %collective-permute-start.22 = (bf16[128,1408]{1,0:T(8,128)(2,1)S(1)}, bf16[128,1408]{1,0:T(8,128)(2,1)}, u32[]{:S(2)}, u32[]{:S(2)}) collective-permute-start(bf16[128,1408]{1,0:T(8,128)(2,1)S(1)} %add_convert_fusion.13), channel_id=1, source_target_pairs={{0,1},{1,0},{2,3},{3,2},{4,5},{5,4},{6,7},{7,6},{8,9},{9,8},{10,11... | collective-permute-start | bytes 1081352 | tf_op jit(solution)/shard_map/ppermute | solution.py:958
  207.2 29.5 %collective-permute-start.24 = (bf16[256,1408]{1,0:T(8,128)(2,1)}, bf16[256,1408]{1,0:T(8,128)(2,1)}, u32[]{:S(2)}, u32[]{:S(2)}) collective-permute-start(bf16[256,1408]{1,0:T(8,128)(2,1)} %add_convert_fusion.6), channel_id=1, source_target_pairs={{0,1},{1,0},{2,3},{3,2},{4,5},{5,4},{6,7},{7,6},{8,9},{9,8},{10,11... | collective-permute-start | bytes 2162696 | tf_op jit(solution)/shard_map/ppermute | solution.py:958
  227.1 14.6 %collective-permute-start.23 = (bf16[384,768]{1,0:T(8,128)(2,1)}, bf16[384,768]{1,0:T(8,128)(2,1)}, u32[]{:S(2)}, u32[]{:S(2)}) collective-permute-start(bf16[384,768]{1,0:T(8,128)(2,1)} %get-tuple-element.382), channel_id=1, source_target_pairs={{0,8},{2,10},{4,12},{6,14},{8,0},{10,2},{12,4},{14,6},{16,24},{18,... | collective-permute-start | bytes 1769480 | tf_op jit(solution)/shard_map/ppermute | solution.py:908
  249.4 20.4 %collective-permute-start.26 = (bf16[192,1408]{1,0:T(8,128)(2,1)}, bf16[192,1408]{1,0:T(8,128)(2,1)}, u32[]{:S(2)}, u32[]{:S(2)}) collective-permute-start(bf16[192,1408]{1,0:T(8,128)(2,1)} %get-tuple-element.390), channel_id=1, source_target_pairs={{0,4},{2,6},{4,0},{6,2},{8,12},{10,14},{12,8},{14,10},{16,20},{18,... | collective-permute-start | bytes 1622024 | tf_op jit(solution)/shard_map/ppermute | solution.py:908
  253.0 16.8 %collective-permute-start.27 = (bf16[192,768]{1,0:T(8,128)(2,1)}, bf16[192,768]{1,0:T(8,128)(2,1)S(1)}, u32[]{:S(2)}, u32[]{:S(2)}) collective-permute-start(bf16[192,768]{1,0:T(8,128)(2,1)} %get-tuple-element.396), channel_id=1, source_target_pairs={{0,16},{2,18},{4,20},{6,22},{8,24},{10,26},{12,28},{14,30},{16,0},... | collective-permute-start | bytes 884744 | tf_op jit(solution)/shard_map/ppermute | solution.py:908
  255.6 23.4 %collective-permute-start.28 = (bf16[384,768]{1,0:T(8,128)(2,1)}, bf16[384,768]{1,0:T(8,128)(2,1)}, u32[]{:S(2)}, u32[]{:S(2)}) collective-permute-start(bf16[384,768]{1,0:T(8,128)(2,1)} %get-tuple-element.329), channel_id=1, source_target_pairs={{0,1},{1,0},{2,3},{3,2},{4,5},{5,4},{6,7},{7,6},{8,9},{9,8},{10,11... | collective-permute-start | bytes 1769480 | tf_op jit(solution)/shard_map/ppermute | solution.py:958
  272.1 10.1 %collective-permute-start.29 = (bf16[96,1408]{1,0:T(8,128)(2,1)}, bf16[96,1408]{1,0:T(8,128)(2,1)}, u32[]{:S(2)}, u32[]{:S(2)}) collective-permute-start(bf16[96,1408]{1,0:T(8,128)(2,1)} %get-tuple-element.400), channel_id=1, source_target_pairs={{0,8},{2,10},{4,12},{6,14},{8,0},{10,2},{12,4},{14,6},{16,24},{18,... | collective-permute-start | bytes 811016 | tf_op jit(solution)/shard_map/ppermute | solution.py:908
  278.6 19.0 %collective-permute-start.32 = (bf16[192,768]{1,0:T(8,128)(2,1)S(1)}, bf16[192,768]{1,0:T(8,128)(2,1)}, u32[]{:S(2)}, u32[]{:S(2)}) collective-permute-start(bf16[192,768]{1,0:T(8,128)(2,1)S(1)} %add_convert_fusion.14), channel_id=1, source_target_pairs={{0,16},{2,18},{4,20},{6,22},{8,24},{10,26},{12,28},{14,30},{16,0},... | collective-permute-start | bytes 884744 | tf_op jit(solution)/shard_map/ppermute | solution.py:908
  282.3 15.3 %collective-permute-start.31 = (f32[1,6784]{1,0:T(1,128)S(1)}, f32[1,6784]{1,0:T(1,128)S(1)}, u32[]{:S(2)}, u32[]{:S(2)}) collective-permute-start(f32[1,6784]{1,0:T(1,128)S(1)} %add.244), channel_id=1, source_target_pairs={{0,2},{2,0},{4,6},{6,4},{8,10},{10,8},{12,14},{14,12},{16,18},{18,... | collective-permute-start | bytes 81416 | tf_op jit(solution)/shard_map/ppermute | solution.py:898
  288.1 11.2 %collective-permute-start.33 = (bf16[48,1408]{1,0:T(8,128)(2,1)}, bf16[48,1408]{1,0:T(8,128)(2,1)S(1)}, u32[]{:S(2)}, u32[]{:S(2)}) collective-permute-start(bf16[48,1408]{1,0:T(8,128)(2,1)} %get-tuple-element.404), channel_id=1, source_target_pairs={{0,16},{2,18},{4,20},{6,22},{8,24},{10,26},{12,28},{14,30},{16,0},... | collective-permute-start | bytes 405512 | tf_op jit(solution)/shard_map/ppermute | solution.py:908
  298.8 13.1 %collective-permute-start.35 = (bf16[384,768]{1,0:T(8,128)(2,1)S(1)}, bf16[384,768]{1,0:T(8,128)(2,1)S(1)}, u32[]{:S(2)}, u32[]{:S(2)}) collective-permute-start(bf16[384,768]{1,0:T(8,128)(2,1)S(1)} %pad_maximum_fusion.6), channel_id=1, source_target_pairs={{0,8},{2,10},{4,12},{6,14},{8,0},{10,2},{12,4},{14,6},{16,24},{18,... | collective-permute-start | bytes 1769480 | tf_op jit(solution)/shard_map/ppermute | solution.py:908
  312.0 13.6 %collective-permute-start.37 = (bf16[384,768]{1,0:T(8,128)(2,1)S(1)}, bf16[384,768]{1,0:T(8,128)(2,1)S(1)}, u32[]{:S(2)}, u32[]{:S(2)}) collective-permute-start(bf16[384,768]{1,0:T(8,128)(2,1)S(1)} %get-tuple-element.352), channel_id=1, source_target_pairs={{0,4},{2,6},{4,0},{6,2},{8,12},{10,14},{12,8},{14,10},{16,20},{18,... | collective-permute-start | bytes 1769480 | tf_op jit(solution)/shard_map/ppermute | solution.py:908
  312.7 13.0 %collective-permute-start.36 = (bf16[112,1408]{1,0:T(8,128)(2,1)S(1)}, bf16[112,1408]{1,0:T(8,128)(2,1)S(1)}, u32[]{:S(2)}, u32[]{:S(2)}) collective-permute-start(bf16[112,1408]{1,0:T(8,128)(2,1)S(1)} %pad_maximum_fusion.7), channel_id=1, source_target_pairs={{0,16},{2,18},{4,20},{6,22},{8,24},{10,26},{12,28},{14,30},{16,0},... | collective-permute-start | bytes 946184 | tf_op jit(solution)/shard_map/ppermute | solution.py:908
  313.3 18.3 %collective-permute-start.38 = (bf16[512,768]{1,0:T(8,128)(2,1)S(1)}, bf16[512,768]{1,0:T(8,128)(2,1)}, u32[]{:S(2)}, u32[]{:S(2)}) collective-permute-start(bf16[512,768]{1,0:T(8,128)(2,1)S(1)} %copy-done.42), channel_id=1, source_target_pairs={{1,0},{3,2},{5,4},{7,6},{9,8},{11,10},{13,12},{15,14},{17,16},{19,... | collective-permute-start | bytes 2359304 | tf_op jit(solution)/shard_map/ppermute | solution.py:1181
  326.8 16.0 %collective-permute-start.40 = (bf16[224,1408]{1,0:T(8,128)(2,1)S(1)}, bf16[224,1408]{1,0:T(8,128)(2,1)}, u32[]{:S(2)}, u32[]{:S(2)}) collective-permute-start(bf16[224,1408]{1,0:T(8,128)(2,1)S(1)} %pad_maximum_fusion.5), channel_id=1, source_target_pairs={{0,8},{2,10},{4,12},{6,14},{8,0},{10,2},{12,4},{14,6},{16,24},{18,... | collective-permute-start | bytes 1892360 | tf_op jit(solution)/shard_map/ppermute | solution.py:908
  326.8 15.2 %collective-permute-start.41 = (bf16[384,768]{1,0:T(8,128)(2,1)S(1)}, bf16[384,768]{1,0:T(8,128)(2,1)}, u32[]{:S(2)}, u32[]{:S(2)}) collective-permute-start(bf16[384,768]{1,0:T(8,128)(2,1)S(1)} %get-tuple-element.363), channel_id=1, source_target_pairs={{0,4},{2,6},{4,0},{6,2},{8,12},{10,14},{12,8},{14,10},{16,20},{18,... | collective-permute-start | bytes 1769480 | tf_op jit(solution)/shard_map/ppermute | solution.py:908
  (55 other events, 278.1 us)
